TPU v7x, 128 devices: a whole 4x4x4 slice. The times are simulated.
128 devices in a mesh: row: 8 (over x, core), col: 16 (over z, y).
Axes of the slice: x: 4, y: 4, z: 4, core: 2. Of those that a mesh axis runs over, the one named last changes fastest.
Arguments:
- features: bfloat16 [32768, 256], P('row'), may hold values from -6 to 6
- join_weight: bfloat16 [256, 256], replicated, may hold values from -0.375 to 0.375
- partner: int32 [32768], replicated, may hold values from 0 to 32767, as said below
- tile_index: int32 [13312], P(('row', 'col')), may hold values from 0 to 127, as said below
- tile_values: bfloat16 [13312, 256, 256], P(('row', 'col')), may hold values from 0 to 10
- pert_slot: int32 [512], P(('row', 'col')), may hold values from 0 to 103
- pert_values: bfloat16 [512, 256, 256], P(('row', 'col')), may hold values from 0 to 0.5
- routes: int32 [13312, 2], P(('row', 'col')), may hold values from 0 to 127, as said below
Outputs:
- coarse_features: bfloat16 [16384, 256], P('row')
- coarse_quarters: bfloat16 [32768, 128, 128], P(('row', 'col'))
Inputs may be any that keep to these rules, and one draw needn't show every extreme that they name: `partner`: fine nodes 16384 + k * 256 + j and k * 256 + s are partners of each other, where s runs over a permutation of the 256 slots for each coarse tile k. `tile_index`: each entry is a local tile position i * 8 + j with i below 16; the entries of one device are distinct; the four devices whose row indices agree modulo 8 // 2 and whose col indices agree modulo 16 // 2 hold the same list in the same order. `routes`: every column of a row equals column 0. Among the 104 rows of one device no device number appears more than 2 times, and in every draw some device number appears exactly 2 times among one device's rows.
All inputs are finite; a program needn't handle non-finite values.
Results may differ from a plain program's by a relative error of at most 0.0052.
Values may be sent and summed in bfloat16 or wider, within the bound.
No kernel may reach another device: no remote copies, remote signals or barrier semaphores. Data moves between devices by JAX's collectives and lax.ppermute only.
A program may use at most 192 MiB of HBM per device.

v0:
```python
import jax
import jax.numpy as jnp
from jax import lax
from jax.sharding import PartitionSpec as P


def swapped(value, axis, stride):
    mask = 2**stride
    pairs = [(source, source ^ mask) for source in range(lax.axis_size(axis))]
    return lax.ppermute(value, axis, pairs)


def pairing_table(slot_table, table_width):
    levels = lax.broadcasted_iota(jnp.int32, slot_table.shape + (table_width,), slot_table.ndim)
    return (slot_table[..., None] == levels).astype(jnp.bfloat16)


def keep_block(tile_block):
    return tile_block


def local(features, join_weight, partner, tile_index, tile_values, pert_slot, pert_values, routes):
    row_count = lax.axis_size("row")
    col_count = lax.axis_size("col")
    row_half = row_count // 2
    col_half = col_count // 2
    row_bit = row_count.bit_length() - 2
    col_bit = col_count.bit_length() - 2
    row_index = lax.axis_index("row")
    col_index = lax.axis_index("col")
    row_side = row_index // row_half
    col_side = col_index // col_half
    tile_size = tile_values.shape[1]
    half_tile = tile_size // 2
    slot_count = tile_values.shape[0]
    feat_width = features.shape[1]
    tiles_row = features.shape[0] // tile_size
    node_count = partner.shape[0]
    tiles_col = node_count // tile_size // col_count
    coarse_count = node_count // tile_size // 2
    coarse_nodes = coarse_count * tile_size
    capacity = routes.shape[1]
    receive_slots = row_count * col_count * capacity
    row_start = row_index % row_half * tiles_row
    col_start = col_index % col_half * tiles_col
    local_row = tile_index // tiles_col
    local_col = tile_index % tiles_col
    odd_slots = (
        partner[coarse_nodes:].reshape(coarse_count, tile_size)
        - (jnp.arange(coarse_count, dtype=jnp.int32) * tile_size)[:, None]
    )
    row_table = lax.dynamic_slice_in_dim(odd_slots, row_start, tiles_row, 0)
    col_table = lax.dynamic_slice_in_dim(odd_slots, col_start, tiles_col, 0)
    feature_tiles = features.reshape(tiles_row, tile_size, feat_width)

    def permute_features(tile_block):
        pair_table = pairing_table(row_table, tile_size)
        return jnp.einsum(
            "ijs,ijf->isf", pair_table, tile_block, preferred_element_type=jnp.float32
        ).astype(jnp.bfloat16)

    own_features = lax.cond(row_side == 1, permute_features, keep_block, feature_tiles)
    given_rows = lax.dynamic_slice_in_dim(own_features, (1 - row_side) * half_tile, half_tile, 1)
    kept_rows = lax.dynamic_slice_in_dim(own_features, row_side * half_tile, half_tile, 1)
    partner_features = swapped(given_rows, "row", row_bit)
    merged = (kept_rows.astype(jnp.float32) + partner_features.astype(jnp.float32)).astype(
        jnp.bfloat16
    )
    joined_rows = jnp.dot(
        merged.reshape(tiles_row * half_tile, feat_width),
        join_weight,
        preferred_element_type=jnp.float32,
    )
    extra_table = (pert_slot[:, None] == jnp.arange(slot_count, dtype=jnp.int32)[None, :]).astype(
        jnp.bfloat16
    )
    added_tiles = jnp.einsum(
        "pn,pxy->nxy", extra_table, pert_values, preferred_element_type=jnp.float32
    )
    perturbed = (tile_values.astype(jnp.float32) + added_tiles).astype(jnp.bfloat16)

    def permute_rows(tile_block):
        pair_table = pairing_table(row_table[local_row], tile_size)
        return jnp.einsum(
            "njs,njc->nsc", pair_table, tile_block, preferred_element_type=jnp.float32
        ).astype(jnp.bfloat16)

    def permute_cols(tile_block):
        pair_table = pairing_table(col_table[local_col], tile_size)
        return jnp.einsum(
            "nrj,njs->nrs", tile_block, pair_table, preferred_element_type=jnp.float32
        ).astype(jnp.bfloat16)

    paired = lax.cond(row_side == 1, permute_rows, keep_block, perturbed)
    paired = lax.cond(col_side == 1, permute_cols, keep_block, paired)
    row_given = lax.dynamic_slice_in_dim(paired, (1 - row_side) * half_tile, half_tile, 1)
    row_kept = lax.dynamic_slice_in_dim(paired, row_side * half_tile, half_tile, 1)
    row_partner = swapped(row_given, "row", row_bit)
    row_summed = row_kept.astype(jnp.float32) + row_partner.astype(jnp.float32)
    col_given = lax.dynamic_slice_in_dim(row_summed, (1 - col_side) * half_tile, half_tile, 2)
    col_kept = lax.dynamic_slice_in_dim(row_summed, col_side * half_tile, half_tile, 2)
    col_partner = swapped(col_given, "col", col_bit)
    quarter = col_kept + col_partner
    row_select = (local_row[None, :] == jnp.arange(tiles_row, dtype=jnp.int32)[:, None]).astype(
        jnp.float32
    )
    owned_sums = jnp.dot(
        row_select,
        jnp.sum(quarter, axis=2),
        precision=lax.Precision.HIGHEST,
        preferred_element_type=jnp.float32,
    )
    spread = jnp.zeros((2, row_half, tiles_row, half_tile), jnp.float32)
    spread = lax.dynamic_update_slice(
        spread, owned_sums[None, None], (row_side, row_index % row_half, 0, 0)
    )
    layout = lax.psum(spread, ("row", "col"))
    degree = (
        1.0 + jnp.transpose(layout, (1, 2, 0, 3)).reshape(coarse_count, tile_size) / coarse_nodes
    )
    row_degree = lax.dynamic_slice(
        degree, (row_start, row_side * half_tile), (tiles_row, half_tile)
    )
    col_degree = lax.dynamic_slice(
        degree, (col_start, col_side * half_tile), (tiles_col, half_tile)
    )
    slot_row_degree = row_degree[local_row]
    slot_col_degree = col_degree[local_col]
    normalized = (
        quarter / jnp.sqrt(slot_row_degree[:, :, None] * slot_col_degree[:, None, :])
    ).astype(jnp.bfloat16)
    coarse_features = (
        joined_rows.reshape(tiles_row, half_tile, feat_width) / jnp.sqrt(row_degree)[:, :, None]
    ).astype(jnp.bfloat16)
    coarse_features = coarse_features.reshape(tiles_row * half_tile, feat_width)
    targets = routes[:, 0]
    slot_order = jnp.arange(slot_count, dtype=jnp.int32)
    earlier = jnp.sum(
        (
            (targets[:, None] == targets[None, :]) & (slot_order[None, :] < slot_order[:, None])
        ).astype(jnp.int32),
        axis=1,
    )
    position = targets * capacity + earlier
    place_table = (position[None, :] == jnp.arange(receive_slots, dtype=jnp.int32)[:, None]).astype(
        jnp.bfloat16
    )
    outgoing = jnp.dot(
        place_table,
        normalized.reshape(slot_count, half_tile * half_tile),
        preferred_element_type=jnp.float32,
    ).astype(jnp.bfloat16)
    arrived = lax.all_to_all(
        outgoing.reshape(receive_slots, half_tile, half_tile),
        ("row", "col"),
        split_axis=0,
        concat_axis=0,
        tiled=True,
    )
    return (coarse_features, arrived)


def solution(mesh):
    placed = (
        P("row", None),
        P(),
        P(),
        P(("row", "col")),
        P(("row", "col"), None, None),
        P(("row", "col")),
        P(("row", "col"), None, None),
        P(("row", "col"), None),
    )
    return jax.shard_map(
        local,
        mesh=mesh,
        in_specs=placed,
        out_specs=(P("row", None), P(("row", "col"), None, None)),
        check_vma=False,
    )
```

profile of v0, /device:TPU:32, one launch (start us, length us, event | category | flops | bytes accessed | tf_op | source)
XLA Modules:
  0.0 729.7 jit_solution(8674809250563732469)
XLA Ops:
  7.2 0.0 copy-start
  7.2 0.0 all-reduce.2.cloned.1.call-start
  7.3 0.9 slice.16
  8.2 0.7 compare_select_fusion.2
  8.9 0.0 copy-done
  8.9 17.9 %add_convert_fusion = bf16[104,256,256]{2,0,1:T(8,128)(2,1)} fusion(bf16[104,256,256]{2,1,0:T(8,128)(2,1)} %param.18, bf16[4,256,256]{2,1,0:T(8,128)(2,1)S(1)} %copy-done, s32[4]{0:T(128)} %param.19), kind=kOutput, calls=%fused_computation.22 | convolution fusion | flops 74973600 | bytes 27787280 | tf_op jit(solution)/shard_map/pn,pxy->nxy/dot_general | solution.py:77
  26.8 0.1 broadcast_subtract_fusion
  26.9 10.9 %conditional.4 = (bf16[104,256,256]{2,1,0:T(8,128)(2,1)}) conditional(s32[]{:T(128)} %convert_element_type.62, (bf16[104,256,256]{2,0,1:T(8,128)(2,1)}) %tuple.35, (s32[104]{0:T(128)S(1)}, s32[16,256]{1,0:T(8,128)S(1)}, bf16[104,256,256]{2,0,1:T(8,128)(2,1)}) %tuple.29), branch_computations={%region_2.3_spmd, %region_3.4_spmd} | conditional | flops 3503293696 | bytes 27588232 | solution.py:94
  26.9 10.9 %copy.30 = bf16[104,256,256]{2,1,0:T(8,128)(2,1)} copy(bf16[104,256,256]{2,0,1:T(8,128)(2,1)} %get-tuple-element.61) | data formatting | bytes 27262976 | tf_op jit(solution)/shard_map/convert_element_type | solution.py:80
  37.8 18.4 %conditional.5 = (bf16[104,256,256]{1,2,0:T(8,128)(2,1)}) conditional(s32[]{:T(128)} %convert_element_type.66, (bf16[104,256,256]{2,1,0:T(8,128)(2,1)}) %conditional.4, (s32[64,256]{1,0:T(8,128)S(1)}, s32[]{:T(128)}, s32[104]{0:T(128)S(1)}, bf16[104,256,256]{2,1,0:T(8,128)(2,1)}) %tuple.30), branch_computations={%region_4.5_spmd, %region_5.6_spmd} | conditional | flops 3503293696 | bytes 27604620 | solution.py:95
  37.8 18.4 %copy.31 = bf16[104,256,256]{1,2,0:T(8,128)(2,1)} copy(bf16[104,256,256]{2,1,0:T(8,128)(2,1)} %get-tuple-element.63) | data formatting | bytes 27262976 | tf_op jit(solution)/shard_map/cond | solution.py:94
  56.2 6.7 constant_dynamic-slice_fusion.2
  62.9 11.1 %collective-permute-start.1 = (bf16[104,128,256]{1,2,0:T(8,128)(2,1)}, bf16[104,128,256]{1,2,0:T(8,128)(2,1)}, u32[]{:S(2)}, u32[]{:S(2)}) collective-permute-start(bf16[104,128,256]{1,2,0:T(8,128)(2,1)} %constant_dynamic-slice_fusion.2), channel_id=1, source_target_pairs={{0,64},{16,80},{32,96},{48,112},{64,0},{80,16},{96,32},{112,48},{1... | collective-permute-start | bytes 20447240 | tf_op jit(solution)/shard_map/ppermute | solution.py:10
  73.9 147.1 %collective-permute-done.1 = bf16[104,128,256]{1,2,0:T(8,128)(2,1)} collective-permute-done((bf16[104,128,256]{1,2,0:T(8,128)(2,1)}, bf16[104,128,256]{1,2,0:T(8,128)(2,1)}, u32[]{:S(2)}, u32[]{:S(2)}) %collective-permute-start.1) | collective-permute-done | bytes 6815776 | tf_op jit(solution)/shard_map/ppermute | solution.py:10
  221.0 12.7 %convert_add_fusion = f32[104,128,256]{1,2,0:T(8,128)} fusion(bf16[104,128,256]{1,2,0:T(8,128)(2,1)} %collective-permute-done.1, bf16[104,256,256]{1,2,0:T(8,128)(2,1)} %get-tuple-element.80, s32[]{:T(128)S(6)} %select_n.77), kind=kLoop, calls=%fused_computation.24 | loop fusion | flops 10223616 | bytes 27262980 | tf_op jit(solution)/shard_map/add | solution.py:99
  233.7 0.0 copy-start.5
  233.7 6.7 constant_dynamic-slice_fusion.1
  240.4 8.8 %collective-permute-start.2 = (f32[104,128,128]{1,2,0:T(8,128)}, f32[104,128,128]{1,2,0:T(8,128)}, u32[]{:S(2)}, u32[]{:S(2)}) collective-permute-start(f32[104,128,128]{1,2,0:T(8,128)} %constant_dynamic-slice_fusion.1), channel_id=1, source_target_pairs={{0,8},{1,9},{2,10},{3,11},{4,12},{5,13},{6,14},{7,15},{8,0},{9,1},... | collective-permute-start | bytes 20447240 | tf_op jit(solution)/shard_map/ppermute | solution.py:10
  249.2 0.0 copy-done.5
  249.2 0.2 convert_reduce_fusion
  249.4 146.3 %collective-permute-done.2 = f32[104,128,128]{1,2,0:T(8,128)} collective-permute-done((f32[104,128,128]{1,2,0:T(8,128)}, f32[104,128,128]{1,2,0:T(8,128)}, u32[]{:S(2)}, u32[]{:S(2)}) %collective-permute-start.2) | collective-permute-done | bytes 6815776 | tf_op jit(solution)/shard_map/ppermute | solution.py:10
  395.7 6.7 fusion.14
  402.4 0.1 fusion.15
  402.5 0.0 copy-start.3
  402.5 0.6 copy-done.3
  403.2 0.0 all-reduce.2.cloned.1.call-update
  403.2 140.7 %all-reduce.2.cloned.1.call-done = f32[2,4,16,128]{3,2,1,0:T(8,128)} async-done(((f32[2,4,16,128]{3,2,1,0:T(8,128)}), f32[2,4,16,128]{3,2,1,0:T(8,128)}) %all-reduce.2.cloned.1.call-update) | async-done | bytes 65552 | tf_op jit(solution)/shard_map/psum | solution.py:117
  543.9 0.8 add_bitcast_fusion
  544.8 0.1 copy.28
  544.9 0.6 gather_fusion.3
  545.5 0.6 gather_fusion.2
  546.1 8.4 %multiply_convert_fusion = bf16[104,128,128]{1,2,0:T(8,128)(2,1)} fusion(f32[104,128]{1,0:T(8,128)S(1)} %gather_fusion.3, f32[104,128]{1,0:T(8,128)S(1)} %gather_fusion.2, f32[104,128,128]{1,2,0:T(8,128)} %collective-permute-done.2, f32[104,128,256]{1,2,0:T(8,128)} %convert_add_fusion, s32[]{:T(128)S(6)} %select_n.84), kind=kLoop, calls=%fused_computation.25 | loop fusion | flops 6815744 | bytes 17145860 | tf_op jit(solution)/shard_map/convert_element_type | solution.py:131
  554.5 5.8 copy.29
  560.3 8.3 %fusion.11 = bf16[32,8,128,128]{3,1,2,0:T(8,128)(2,1)} fusion(bf16[13,8,128,128]{3,2,1,0:T(8,128)(2,1)} %bitcast.36, s32[104]{0:T(128)S(1)} %multiply_add_fusion), kind=kOutput, calls=%fused_computation.27 | convolution fusion | flops 876636160 | bytes 11796896 | tf_op jit(solution)/shard_map/dot_general | solution.py:148
  568.7 9.2 %copy.34 = bf16[32,8,128,128]{3,2,1,0:T(8,128)(2,1)} copy(bf16[32,8,128,128]{3,1,2,0:T(8,128)(2,1)} %fusion.11) | data formatting | bytes 16777216
  577.9 0.0 copy-start.2
  577.9 6.9 all-to-all-start
  584.8 0.0 copy-start.4
  584.8 0.0 copy-done.2
  584.8 0.1 constant_dynamic-slice_fusion.3
  584.9 4.1 collective-permute-start
  589.0 121.7 %collective-permute-done = bf16[16,128,256]{2,1,0:T(8,128)(2,1)S(1)} collective-permute-done((bf16[16,128,256]{2,1,0:T(8,128)(2,1)S(1)}, bf16[16,128,256]{2,1,0:T(8,128)(2,1)S(1)}, u32[]{:S(2)}, u32[]{:S(2)}) %collective-permute-start) | collective-permute-done | bytes 1048608 | tf_op jit(solution)/shard_map/ppermute | solution.py:10
  710.7 0.0 copy-done.4
  710.7 1.5 divide_convert_fusion
  712.2 0.0 all-to-all-done
  712.2 0.0 copy-start.1
  712.2 10.6 %copy.61 = bf16[256,128,128]{2,1,0:T(8,128)(2,1)} copy(bf16[256,128,128]{2,1,0:T(8,128)(2,1)} %all-to-all-done) | data formatting | bytes 16777216
  722.8 0.0 copy-done.1
  (11 shorter events, 0.1 us)
Async XLA Ops:
  7.2 1.7 copy-start
  7.2 536.8 %all-reduce.2.cloned.1.call-start = ((), (), s32[]{:S(2)}) async-start(), calls=%async_computation.1 | async-start | bytes 131072 | tf_op jit(solution)/shard_map/psum | solution.py:117
  62.9 158.1 %collective-permute-start.1 = (bf16[104,128,256]{1,2,0:T(8,128)(2,1)}, bf16[104,128,256]{1,2,0:T(8,128)(2,1)}, u32[]{:S(2)}, u32[]{:S(2)}) collective-permute-start(bf16[104,128,256]{1,2,0:T(8,128)(2,1)} %constant_dynamic-slice_fusion.2), channel_id=1, source_target_pairs={{0,64},{16,80},{32,96},{48,112},{64,0},{80,16},{96,32},{112,48},{1... | collective-permute-start | bytes 20447240 | tf_op jit(solution)/shard_map/ppermute | solution.py:10
  233.7 15.5 %copy-start.5 = (s32[104,2]{0,1:T(2,128)S(1)}, s32[104,2]{0,1:T(2,128)}, u32[]{:S(2)}) copy-start(s32[104,2]{0,1:T(2,128)} %param.21) | copy-start | bytes 2500
  240.4 155.3 %collective-permute-start.2 = (f32[104,128,128]{1,2,0:T(8,128)}, f32[104,128,128]{1,2,0:T(8,128)}, u32[]{:S(2)}, u32[]{:S(2)}) collective-permute-start(f32[104,128,128]{1,2,0:T(8,128)} %constant_dynamic-slice_fusion.1), channel_id=1, source_target_pairs={{0,8},{1,9},{2,10},{3,11},{4,12},{5,13},{6,14},{7,15},{8,0},{9,1},... | collective-permute-start | bytes 20447240 | tf_op jit(solution)/shard_map/ppermute | solution.py:10
  402.5 0.6 copy-start.3
  577.9 6.9 copy-start.2
  577.9 134.3 %all-to-all-start = ((bf16[256,128,128]{2,1,0:T(8,128)(2,1)}), bf16[256,128,128]{2,1,0:T(8,128)(2,1)}, u32[]{:S(2)}, u32[]{:S(2)}) async-start(bf16[256,128,128]{2,1,0:T(8,128)(2,1)} %bitcast.35), calls=%async_computation | async-start | bytes 16777216 | tf_op jit(solution)/shard_map/all_to_all | solution.py:153
  584.8 125.9 %copy-start.4 = (bf16[256,256]{1,0:T(8,128)(2,1)S(1)}, bf16[256,256]{1,0:T(8,128)(2,1)}, u32[]{:S(2)}) copy-start(bf16[256,256]{1,0:T(8,128)(2,1)} %param.15) | copy-start | bytes 393220
  584.9 125.8 %collective-permute-start = (bf16[16,128,256]{2,1,0:T(8,128)(2,1)S(1)}, bf16[16,128,256]{2,1,0:T(8,128)(2,1)S(1)}, u32[]{:S(2)}, u32[]{:S(2)}) collective-permute-start(bf16[16,128,256]{2,1,0:T(8,128)(2,1)S(1)} %constant_dynamic-slice_fusion.3), channel_id=1, source_target_pairs={{0,64},{16,80},{32,96},{48,112},{64,0},{80,16},{96,32},{112,48},{1... | collective-permute-start | bytes 3145736 | tf_op jit(solution)/shard_map/ppermute | solution.py:10
  712.2 10.6 %copy-start.1 = (bf16[4,256,256]{2,1,0:T(8,128)(2,1)S(1)}, bf16[4,256,256]{2,1,0:T(8,128)(2,1)}, u32[]{:S(2)}) copy-start(bf16[4,256,256]{2,1,0:T(8,128)(2,1)} %param.20) | copy-start | bytes 1572868
Sparse Core Ops, SparseCore 0:
  403.3 140.5 all-reduce.1
where the time goes:
time: 731 us; the launch traced here: 730 us
  waiting for transfers between devices  556 us (76%)
  local copies, waits for them, and re-layouts  71.3 us (10%)
  starting transfers between devices  30.9 us (4%)
  other arithmetic  29.6 us (4%)
  matrix products  27.9 us (4%)
  between operations  14.2 us (2%)
    ppermute x3, waiting for transfers between devices, swapped(): return lax.ppermute(value, axis, pairs)  415 us
    psum x1, waiting for transfers between devices, local(): layout = lax.psum(spread, ('row', 'col'))  141 us
    ppermute x3, starting transfers between devices, swapped(): return lax.ppermute(value, axis, pairs)  23.9 us
    unnamed x15, local copies, waits for them, and re-layouts  20.5 us
    cond x1, local copies, waits for them, and re-layouts, local(): paired = lax.cond(row_side == 1, permute_rows, keep_block, perturbed)  18.4 us
    dot_general x1, matrix products, local(): jnp.einsum('pn,pxy->nxy', extra_table, pert_values, preferred_element_typ...  17.9 us
  transfers between devices with their start and end apart: 5, of which 4 were waited for; matrix products, arithmetic and copies ran while one was open for 0% of the time, Pallas kernels for 0%

commit v1 on v0

v1 whole, which is shorter than its diff:
```python
import functools

import jax
import jax.numpy as jnp
from jax import lax
from jax.experimental import pallas as pl
from jax.experimental.pallas import tpu as pltpu
from jax.sharding import PartitionSpec as P

TILE = 256
HALF = 128
STEP = 4
ROW_FIRST = 48
CHUNKS = (12, 36), (12, 44)
BF16 = jnp.bfloat16
F32 = jnp.float32


def flipped(value, axis, mask):
    pairs = [(source, source ^ mask) for source in range(lax.axis_size(axis))]
    return lax.ppermute(value, axis, pairs)


def full(shape):
    return pl.BlockSpec(shape, lambda *_: (0,) * len(shape))


def iota(shape, axis):
    return lax.broadcasted_iota(jnp.int32, shape, axis)


def sizes():
    row_half = lax.axis_size("row") // 2
    col_half = lax.axis_size("col") // 2
    return row_half, col_half


def position():
    row_half, col_half = sizes()
    row_index = lax.axis_index("row")
    col_index = lax.axis_index("col")
    return (
        lax.div(row_index, row_half),
        lax.rem(row_index, row_half),
        lax.div(col_index, col_half),
        lax.rem(col_index, col_half),
    )


def table_kernel(partner_ref, row_tables, col_tables):
    row_side, row_group, col_side, col_group = position()
    tiles_row = row_tables.shape[0]
    tiles_col = col_tables.shape[0]
    coarse_nodes = partner_ref.shape[0] * HALF // 2
    rotated = (iota((1, TILE), 1) + HALF) & (TILE - 1)
    level = iota((TILE, TILE), 0)

    def vector(start, shift):
        first = partner_ref[pl.ds(start, 1), :]
        second = partner_ref[pl.ds(start + 1, 1), :]
        return jnp.concatenate([first, second], axis=1) - shift

    def table(values):
        return (jnp.broadcast_to(values, (TILE, TILE)) == level).astype(F32).astype(BF16)

    for i in range(tiles_row):
        k = row_group * tiles_row + i
        slots = vector(coarse_nodes // HALF + 2 * k, k * TILE)
        row_tables[i] = table(jnp.where(row_side == 1, slots, rotated))
    for j in range(tiles_col):
        k = col_group * tiles_col + j
        nodes = vector(2 * k, coarse_nodes + k * TILE)
        col_tables[j] = table(jnp.where(col_side == 1, nodes, rotated))


def make_tables(partner, tiles_row, tiles_col):
    return pl.pallas_call(
        table_kernel,
        out_shape=(
            jax.ShapeDtypeStruct((tiles_row, TILE, TILE), BF16),
            jax.ShapeDtypeStruct((tiles_col, TILE, TILE), BF16),
        ),
        name="tables",
    )(partner.reshape(-1, HALF))


def pair_kernel(
    row_first, start, tiles_col,
    index_ref, pert_ref, tiles, perts, row_tables, col_tables,
    given, kept, sums, work,
):
    step = pl.program_id(0)
    count = pert_ref.shape[0]

    @pl.when(step == 0)
    def _():
        sums[...] = jnp.zeros_like(sums)

    for t in range(STEP):
        n = start + step * STEP + t
        work[t] = tiles[t]
        hits = sum((pert_ref[p] == n).astype(jnp.int32) for p in range(count))

        @pl.when(hits > 0)
        def _():
            total = tiles[t].astype(F32)
            for p in range(count):
                total = total + jnp.where(pert_ref[p] == n, perts[p].astype(F32), 0.0)
            work[t] = total.astype(BF16)

    ones = jnp.ones((8, TILE), BF16)
    for t in range(STEP):
        n = start + step * STEP + t
        place = index_ref[n]
        i = lax.div(place, tiles_col)
        j = lax.rem(place, tiles_col)
        rows = jnp.dot(row_tables[i], work[t], preferred_element_type=F32).astype(BF16)
        added = lax.dot_general(ones, rows, (((1,), (1,)), ((), ())), preferred_element_type=F32)
        sums[i] = sums[i] + added
        both = jnp.dot(rows, col_tables[j], preferred_element_type=F32).astype(BF16)
        if row_first:
            given[t] = both[:HALF]
            kept[t] = both[HALF:]
        else:
            given[t] = both[:, :HALF]
            kept[t] = both[:, HALF:]


def pair_tiles(row_first, start, count, tile_index, pert_slot, tile_values, pert_values, tables):
    row_tables, col_tables = tables
    tiles_row = row_tables.shape[0]
    tiles_col = col_tables.shape[0]
    shape = (HALF, TILE) if row_first else (TILE, HALF)
    block = pl.BlockSpec((STEP,) + shape, lambda s, *_: (s, 0, 0))
    half = jax.ShapeDtypeStruct((count,) + shape, BF16)
    return pl.pallas_call(
        functools.partial(pair_kernel, row_first, start, tiles_col),
        out_shape=(half, half, jax.ShapeDtypeStruct((tiles_row, 8, TILE), F32)),
        grid_spec=pltpu.PrefetchScalarGridSpec(
            num_scalar_prefetch=2,
            grid=(count // STEP,),
            in_specs=[
                pl.BlockSpec((STEP, TILE, TILE), lambda s, *_: (s + start // STEP, 0, 0)),
                full(pert_values.shape),
                full(row_tables.shape),
                full(col_tables.shape),
            ],
            out_specs=(block, block, full((tiles_row, 8, TILE))),
            scratch_shapes=[pltpu.VMEM((STEP, TILE, TILE), BF16)],
        ),
        name="pair_rows" if row_first else "pair_cols",
    )(tile_index, pert_slot, tile_values, pert_values, row_tables, col_tables)


def forward_kernel(kept, came, given):
    given[...] = (kept[...].astype(F32) + came[...].astype(F32)).astype(BF16)


def forward(kept, came):
    count = kept.shape[0]
    part = max(d for d in range(1, 13) if count % d == 0)
    block = pl.BlockSpec((part, HALF, HALF), lambda s: (s, 0, 0))
    return pl.pallas_call(
        forward_kernel,
        out_shape=jax.ShapeDtypeStruct((count, HALF, HALF), BF16),
        grid=(count // part,),
        in_specs=[block, block],
        out_specs=block,
        name="forward",
    )(kept, came)


def zero_kernel(_, out):
    out[...] = jnp.zeros_like(out)


def zero_buffer(anchor, count):
    return pl.pallas_call(
        zero_kernel,
        out_shape=jax.ShapeDtypeStruct((count, HALF, HALF), BF16),
        grid=(count // 32,),
        in_specs=[pl.BlockSpec(memory_space=pl.ANY)],
        out_specs=pl.BlockSpec((32, HALF, HALF), lambda s: (s, 0, 0)),
        name="zero_buffer",
    )(anchor)


def inverse_root(raw):
    half = raw.shape[0] // 2
    total = raw[:half] + raw[half:]
    degree = 1.0 + total / (total.shape[0] * total.shape[1])
    return 1.0 / jnp.sqrt(degree)


def picked(scale, k, side):
    return scale[side, pl.ds(k, 1), :]


def upright(line):
    return jnp.broadcast_to(line, (HALF, HALF)).T


def finish_kernel(
    start, tiles_row, tiles_col,
    index_ref, place_ref, kept, came, last, raw, _, out, scale, row_scale, col_scale, done, sem,
):
    step = pl.program_id(0)
    steps = pl.num_programs(0)

    @pl.when(step == 0)
    def _():
        row_side, row_group, col_side, col_group = position()
        roots = inverse_root(raw[...])
        scale[0] = roots[:, :HALF]
        scale[1] = roots[:, HALF:]
        for i in range(tiles_row):
            row_scale[i] = upright(picked(scale, row_group * tiles_row + i, row_side))
        for j in range(tiles_col):
            col_scale[j] = jnp.broadcast_to(
                picked(scale, col_group * tiles_col + j, col_side), (8, HALF)
            )

    for t in range(STEP):
        m = step * STEP + t
        place = index_ref[start + m]
        i = lax.div(place, tiles_col)
        j = lax.rem(place, tiles_col)
        total = kept[t].astype(F32) + came[t].astype(F32) + last[t].astype(F32)
        done[m] = (total * row_scale[i] * col_scale[j, 0:1]).astype(BF16)
        pltpu.make_async_copy(done.at[m], out.at[place_ref[start + m]], sem).start()

    @pl.when(step == steps - 1)
    def _():
        pltpu.make_async_copy(done, out.at[pl.ds(0, done.shape[0])], sem).wait()


def finish(row_first, start, tile_index, place, kept, came, last, raw, buffer, tiles_row, tiles_col):
    count = kept.shape[0]
    if row_first:
        second = pl.BlockSpec((STEP, HALF, HALF), lambda s, *_: (s, 0, 1))
    else:
        second = pl.BlockSpec((STEP, HALF, HALF), lambda s, *_: (s, 1, 0))
    anywhere = pl.BlockSpec(memory_space=pl.ANY)
    return pl.pallas_call(
        functools.partial(finish_kernel, start, tiles_row, tiles_col),
        out_shape=jax.ShapeDtypeStruct(buffer.shape, BF16),
        grid_spec=pltpu.PrefetchScalarGridSpec(
            num_scalar_prefetch=2,
            grid=(count // STEP,),
            in_specs=[
                second,
                second,
                pl.BlockSpec((STEP, HALF, HALF), lambda s, *_: (s, 0, 0)),
                full(raw.shape),
                anywhere,
            ],
            out_specs=anywhere,
            scratch_shapes=[
                pltpu.VMEM((2, raw.shape[0] // 2, HALF), F32),
                pltpu.VMEM((tiles_row, HALF, HALF), F32),
                pltpu.VMEM((tiles_col, 8, HALF), F32),
                pltpu.VMEM((count, HALF, HALF), BF16),
                pltpu.SemaphoreType.DMA,
            ],
        ),
        input_output_aliases={6: 0},
        name="finish_rows" if row_first else "finish_cols",
    )(tile_index, place, kept, came, last, raw, buffer)


def feature_kernel(lane_ref, tiles, tables, given, kept):
    for t in range(tiles.shape[0]):
        rows = jnp.dot(tables[t], tiles[t], preferred_element_type=F32).astype(BF16)
        given[t] = rows[:HALF]
        kept[t] = rows[HALF:]


def pair_features(lane, tiles, row_tables, part):
    width = tiles.shape[2]
    half = jax.ShapeDtypeStruct((part, HALF, width), BF16)
    return pl.pallas_call(
        feature_kernel,
        out_shape=(half, half),
        grid_spec=pltpu.PrefetchScalarGridSpec(
            num_scalar_prefetch=1,
            grid=(1,),
            in_specs=[
                pl.BlockSpec((part, TILE, width), lambda s, lane: (lane[0], 0, 0)),
                pl.BlockSpec((part, TILE, TILE), lambda s, lane: (lane[0], 0, 0)),
            ],
            out_specs=(full((part, HALF, width)), full((part, HALF, width))),
        ),
        name="pair_features",
    )(lane, tiles, row_tables)


def join_kernel(tiles_row, lane_ref, kept, came, weight, raw, out, scale):
    row_side, row_group, _, _ = position()
    part = kept.shape[0]
    roots = inverse_root(raw[...])
    scale[0] = roots[:, :HALF]
    scale[1] = roots[:, HALF:]
    for t in range(part):
        merged = (kept[t].astype(F32) + came[t].astype(F32)).astype(BF16)
        joined = jnp.dot(merged, weight[...], preferred_element_type=F32)
        k = row_group * tiles_row + lane_ref[0] * part + t
        column = upright(picked(scale, k, row_side))
        width = joined.shape[1] // HALF
        out[t] = (joined * jnp.concatenate([column] * width, axis=1)).astype(BF16)


def join_features(lane, kept, came, weight, raw, tiles_row):
    return pl.pallas_call(
        functools.partial(join_kernel, tiles_row),
        out_shape=jax.ShapeDtypeStruct(kept.shape, BF16),
        grid_spec=pltpu.PrefetchScalarGridSpec(
            num_scalar_prefetch=1,
            grid=(1,),
            in_specs=[full(kept.shape), full(kept.shape), full(weight.shape), full(raw.shape)],
            out_specs=full(kept.shape),
            scratch_shapes=[pltpu.VMEM((2, raw.shape[0] // 2, HALF), F32)],
        ),
        name="join_features",
    )(lane, kept, came, weight, raw)


def local(features, join_weight, partner, tile_index, tile_values, pert_slot, pert_values, routes):
    row_count = lax.axis_size("row")
    col_count = lax.axis_size("col")
    devices = row_count * col_count
    row_mask = row_count // 2
    col_mask = col_count // 2
    slot_count = tile_values.shape[0]
    width = features.shape[1]
    tiles_row = features.shape[0] // TILE
    tiles_col = partner.shape[0] // TILE // col_count
    capacity = routes.shape[1]
    lanes = 4
    part = tiles_row // lanes
    row_side = lax.axis_index("row") // row_mask
    lane = (lax.axis_index("col") % lanes).reshape(1)

    tables = make_tables(partner, tiles_row, tiles_col)

    pieces = []
    starts = [0, ROW_FIRST]
    for chunk in range(len(CHUNKS[0])):
        for kind in range(2):
            row_first = kind == 0
            count = CHUNKS[kind][chunk]
            given, kept, sums = pair_tiles(
                row_first, starts[kind], count, tile_index, pert_slot, tile_values, pert_values, tables
            )
            came = flipped(given, "row", row_mask) if row_first else flipped(given, "col", col_mask)
            pieces.append([row_first, starts[kind], kept, came, sums])
            starts[kind] += count

    feature_given, feature_kept = pair_features(
        lane, features.reshape(tiles_row, TILE, width), tables[0], part
    )
    feature_came = flipped(feature_given, "row", row_mask)

    own = sum(piece[4][:, 0, :] for piece in pieces)
    own = jnp.where(row_side == 1, own, jnp.roll(own, HALF, axis=1))
    spread = lax.all_to_all(own, "col", split_axis=0, concat_axis=0, tiled=True)
    line = jnp.sum(spread, axis=0)
    raw = lax.all_to_all(
        jnp.broadcast_to(line[None], (devices, TILE)),
        ("row", "col"),
        split_axis=0,
        concat_axis=0,
        tiled=True,
    )

    targets = routes[:, 0]
    order = jnp.arange(slot_count, dtype=jnp.int32)
    same = (targets[:, None] == targets[None, :]) & (order[None, :] < order[:, None])
    place = targets * capacity + jnp.sum(same.astype(jnp.int32), axis=1)

    for piece in pieces:
        row_first, start, kept, came, _ = piece
        given = forward(kept, came)
        last = flipped(given, "col", col_mask) if row_first else flipped(given, "row", row_mask)
        piece.append(last)

    joined = join_features(lane, feature_kept, feature_came, join_weight, raw, tiles_row)
    parts = jnp.zeros((lanes, part, HALF, width), BF16)
    for shift in range(lanes):
        shared = joined
        if shift > 0:
            pairs = [
                (source, source // lanes * lanes + (source + shift) % lanes)
                for source in range(col_count)
            ]
            shared = lax.ppermute(joined, "col", pairs)
        parts = lax.dynamic_update_slice(
            parts, shared[None], ((lane[0] - shift) % lanes, 0, 0, 0)
        )
    coarse_features = parts.reshape(tiles_row * HALF, width)

    buffer = zero_buffer(pieces[-1][3], devices * capacity)
    for row_first, start, kept, came, _, last in pieces:
        buffer = finish(
            row_first, start, tile_index, place, kept, came, last, raw, buffer, tiles_row, tiles_col
        )
    arrived = lax.all_to_all(buffer, ("row", "col"), split_axis=0, concat_axis=0, tiled=True)
    return (coarse_features, arrived)


def solution(mesh):
    both = P(("row", "col"))
    placed = (
        P("row", None),
        P(),
        P(),
        both,
        P(("row", "col"), None, None),
        both,
        P(("row", "col"), None, None),
        P(("row", "col"), None),
    )
    return jax.shard_map(
        local,
        mesh=mesh,
        in_specs=placed,
        out_specs=(P("row", None), P(("row", "col"), None, None)),
        check_vma=False,
    )
```

time: 731 us -> 355 us (0.49)
  waiting for transfers between devices: 556 us -> 190 us
  Pallas kernels: 0 us -> 90.5 us
  local copies, waits for them, and re-layouts: 71.3 us -> 20.1 us
  matrix products: 27.9 us -> 0 us
  other arithmetic: 29.6 us -> 2.54 us
  starting transfers between devices: 30.9 us -> 49.9 us
  between operations: 14.2 us -> 0.84 us
    ppermute x3 -> x12, waiting for transfers between devices: 415 us -> 178 us  [the longest x9 167 us: flipped(): return lax.ppermute(value, axis, pairs)]
    psum x1 -> x0, waiting for transfers between devices: 141 us -> none  [local(): layout = lax.psum(spread, ('row', 'col'))]
    pallas_call x0 -> x16, Pallas kernels: none -> 90.5 us  [the longest x4 42.6 us: pair_tiles(): pl.pallas_call(functools.partial(pair_kernel, row_first, start, tiles_col...]
    dot_general x4 -> x0, matrix products: 27.9 us -> none  [the longest x1 17.9 us: local(): jnp.einsum('pn,pxy->nxy', extra_table, pert_values, preferred_element_typ...]
    cond x1 -> x0, local copies, waits for them, and re-layouts: 18.4 us -> none  [local(): paired = lax.cond(row_side == 1, permute_rows, keep_block, perturbed)]
    all_to_all x1 -> x3, starting transfers between devices: 6.91 us -> 24.6 us  [the longest x1 10.2 us: local(): lax.all_to_all(jnp.broadcast_to(line[None], (devices, TILE)), ('row', 'co...]
    convert_element_type x2 -> x0, local copies, waits for them, and re-layouts: 16.7 us -> none  [the longest x1 10.9 us: local(): (tile_values.astype(jnp.float32) + added_tiles).astype(jnp.bfloat16)]
    dynamic_slice x5 -> x0, local copies, waits for them, and re-layouts: 13.5 us -> none  [the longest x1 6.7 us: local(): lax.dynamic_slice_in_dim(row_summed, (1 - col_side) * half_tile, half_til...]
  transfers between devices with their start and end apart: 5 -> 15, of which waited for: 4 -> 7; matrix products, arithmetic and copies ran while one was open for 0% -> 1% of each run, Pallas kernels for 0% -> 18%
where the time goes in v1:
time: 355 us; the launch traced here: 354 us
  waiting for transfers between devices  190 us (54%)
  Pallas kernels  90.5 us (25%)
  starting transfers between devices  49.9 us (14%)
  local copies, waits for them, and re-layouts  20.1 us (6%)
    ppermute x9, waiting for transfers between devices, flipped(): return lax.ppermute(value, axis, pairs)  167 us
    pallas_call x4, Pallas kernels, pair_tiles(): pl.pallas_call(functools.partial(pair_kernel, row_first, start, tiles_col...  42.6 us
    pallas_call x4, Pallas kernels, finish(): pl.pallas_call(functools.partial(finish_kernel, start, tiles_row, tiles_c...  24.4 us
    ppermute x9, starting transfers between devices, flipped(): return lax.ppermute(value, axis, pairs)  22 us
    unnamed x21, local copies, waits for them, and re-layouts  18.3 us
    pallas_call x4, Pallas kernels, forward(): pl.pallas_call(forward_kernel, out_shape=jax.ShapeDtypeStruct((count, HAL...  11.4 us
    ppermute x3, waiting for transfers between devices, local(): shared = lax.ppermute(joined, 'col', pairs)  10.9 us
    all_to_all x1, starting transfers between devices, local(): lax.all_to_all(jnp.broadcast_to(line[None], (devices, TILE)), ('row', 'co...  10.2 us
  transfers between devices with their start and end apart: 15, of which 7 were waited for; matrix products, arithmetic and copies ran while one was open for 1% of the time, Pallas kernels for 18%

profile of v1, /device:TPU:32, one launch (start us, length us, event | category | flops | bytes accessed | tf_op | source)
XLA Modules:
  0.0 353.6 jit_solution(1001525544189700409)
XLA Ops:
  0.6 2.9 tables.1
  3.6 15.6 %pair_cols.3 = (bf16[44,256,128]{2,1,0:T(8,128)(2,1)}, bf16[44,256,128]{2,1,0:T(8,128)(2,1)}, f32[16,8,256]{2,1,0:T(8,128)}) custom-call(s32[104]{0:T(128)} %index_ref.15, s32[4]{0:T(128)} %pert_ref.7, bf16[104,256,256]{2,1,0:T(8,128)(2,1)} %tiles.7, bf16[4,256,256]{2,1,0:T(8,128)(2,1)} %perts.7, bf16[16,256,256]{2,1,0:T(8,128)(2,1)} %get-tuple-element.18.tables.row_tables, ...), custom_call_target="tpu_custom_call" | custom-call | tf_op jit(solution)/shard_map/pair_cols/pallas_call | solution.py:136
  19.2 3.2 collective-permute-start.4
  22.4 13.4 %pair_rows.3 = (bf16[36,128,256]{2,1,0:T(8,128)(2,1)}, bf16[36,128,256]{2,1,0:T(8,128)(2,1)}, f32[16,8,256]{2,1,0:T(8,128)}) custom-call(s32[104]{0:T(128)} %index_ref.15, s32[4]{0:T(128)} %pert_ref.7, bf16[104,256,256]{2,1,0:T(8,128)(2,1)} %tiles.7, bf16[4,256,256]{2,1,0:T(8,128)(2,1)} %perts.7, bf16[16,256,256]{2,1,0:T(8,128)(2,1)} %get-tuple-element.18.tables.row_tables, ...), custom_call_target="tpu_custom_call" | custom-call | tf_op jit(solution)/shard_map/pair_rows/pallas_call | solution.py:136
  35.8 3.0 collective-permute-start.6
  38.8 46.5 %collective-permute-done.4.came._ = bf16[44,256,128]{2,1,0:T(8,128)(2,1)S(1)} collective-permute-done((bf16[44,256,128]{2,1,0:T(8,128)(2,1)}, bf16[44,256,128]{2,1,0:T(8,128)(2,1)S(1)}, u32[]{:S(2)}, u32[]{:S(2)}) %collective-permute-start.4) | collective-permute-done | bytes 2883616 | tf_op jit(solution)/shard_map/ppermute | solution.py:21
  85.3 1.6 copy-done
  86.9 3.9 %forward.4 = bf16[44,128,128]{2,1,0:T(8,128)(2,1)} custom-call(bf16[44,256,128]{2,1,0:T(8,128)(2,1)} %get-tuple-element.26.kept, bf16[44,256,128]{2,1,0:T(8,128)(2,1)} %copy-done), custom_call_target="tpu_custom_call" | custom-call | tf_op jit(solution)/shard_map/forward/pallas_call | solution.py:163
  90.8 2.9 collective-permute-start.5
  93.7 6.8 %pair_rows.2 = (bf16[12,128,256]{2,1,0:T(8,128)(2,1)}, bf16[12,128,256]{2,1,0:T(8,128)(2,1)}, f32[16,8,256]{2,1,0:T(8,128)}) custom-call(s32[104]{0:T(128)} %index_ref.15, s32[4]{0:T(128)} %pert_ref.7, bf16[104,256,256]{2,1,0:T(8,128)(2,1)} %tiles.7, bf16[4,256,256]{2,1,0:T(8,128)(2,1)} %perts.7, bf16[16,256,256]{2,1,0:T(8,128)(2,1)} %get-tuple-element.18.tables.row_tables, ...), custom_call_target="tpu_custom_call" | custom-call | tf_op jit(solution)/shard_map/pair_rows/pallas_call | solution.py:136
  100.5 0.7 collective-permute-start.10
  101.2 6.8 %pair_cols.2 = (bf16[12,256,128]{2,1,0:T(8,128)(2,1)}, bf16[12,256,128]{2,1,0:T(8,128)(2,1)}, f32[16,8,256]{2,1,0:T(8,128)}) custom-call(s32[104]{0:T(128)} %index_ref.15, s32[4]{0:T(128)} %pert_ref.7, bf16[104,256,256]{2,1,0:T(8,128)(2,1)} %tiles.7, bf16[4,256,256]{2,1,0:T(8,128)(2,1)} %perts.7, bf16[16,256,256]{2,1,0:T(8,128)(2,1)} %get-tuple-element.18.tables.row_tables, ...), custom_call_target="tpu_custom_call" | custom-call | tf_op jit(solution)/shard_map/pair_cols/pallas_call | solution.py:136
  108.0 2.9 collective-permute-start.8
  111.0 0.0 collective-permute-done.6.came
  111.0 3.5 forward.5
  114.5 0.7 collective-permute-start.7
  115.1 1.1 slice_add_fusion
  116.3 0.6 broadcast_select_fusion
  116.9 8.3 %all-to-all-start = ((f32[16,1,256]{2,1,0:T(1,128)}), f32[16,1,256]{2,1,0:T(1,128)S(1)}, u32[]{:S(2)}, u32[]{:S(2)}) async-start(f32[16,1,256]{2,1,0:T(1,128)} %broadcast_select_fusion), calls=%async_computation | async-start | bytes 32768 | tf_op jit(solution)/shard_map/all_to_all | solution.py:365
  125.2 16.8 %collective-permute-done.10.came = bf16[12,128,256]{2,1,0:T(8,128)(2,1)S(1)} collective-permute-done((bf16[12,128,256]{2,1,0:T(8,128)(2,1)}, bf16[12,128,256]{2,1,0:T(8,128)(2,1)S(1)}, u32[]{:S(2)}, u32[]{:S(2)}) %collective-permute-start.10) | collective-permute-done | bytes 786464 | tf_op jit(solution)/shard_map/ppermute | solution.py:21
  142.0 0.9 copy-done.1
  142.9 2.0 forward.7
  144.8 2.7 collective-permute-start.11
  147.5 0.0 collective-permute-done.8.came
  147.5 0.9 copy-done.2
  148.4 2.0 forward.6
  150.4 3.0 collective-permute-start.9
  153.3 0.0 copy-done.8
  153.3 0.2 convert_reduce_fusion
  153.5 2.5 all-to-all-done
  156.1 0.7 broadcast_in_dim.24
  156.8 10.2 %all-to-all-start.1 = ((f32[128,1,256]{2,1,0:T(1,128)}), f32[128,1,256]{2,1,0:T(1,128)S(1)}, u32[]{:S(2)}, u32[]{:S(2)}) async-start(f32[128,1,256]{2,1,0:T(1,128)} %broadcast_in_dim.24), calls=%async_computation.1 | async-start | bytes 262144 | tf_op jit(solution)/shard_map/all_to_all | solution.py:367
  167.0 0.6 multiply_add_fusion.place_ref
  167.5 8.8 %all-to-all-done.1 = f32[128,1,256]{2,1,0:T(1,128)S(1)} async-done(((f32[128,1,256]{2,1,0:T(1,128)}), f32[128,1,256]{2,1,0:T(1,128)S(1)}, u32[]{:S(2)}, u32[]{:S(2)}) %all-to-all-start.1) | async-done | bytes 131104 | tf_op jit(solution)/shard_map/all_to_all | solution.py:367
  176.3 0.7 copy.21
  177.0 4.8 %zero_buffer.1._ = bf16[256,128,128]{2,1,0:T(8,128)(2,1)} custom-call(bf16[44,256,128]{2,1,0:T(8,128)(2,1)} %copy-done), custom_call_target="tpu_custom_call" | custom-call | tf_op jit(solution)/shard_map/zero_buffer/pallas_call | solution.py:178
  181.7 0.0 collective-permute-done.11.last
  181.7 0.8 copy-done.5
  182.5 4.1 %finish_rows.2._ = bf16[256,128,128]{2,1,0:T(8,128)(2,1)} custom-call(s32[104]{0:T(128)} %index_ref.15, s32[104]{0:T(128)} %multiply_add_fusion.place_ref, bf16[12,128,256]{2,1,0:T(8,128)(2,1)} %get-tuple-element.32.kept, bf16[12,128,256]{2,1,0:T(8,128)(2,1)} %copy-done.1, bf16[12,128,128]{2,1,0:T(8,128)(2,1)} %copy-done.5, ...), custom_call_target="tpu_custom_call", output_to_operand_aliasing={{}: (6, {})} | custom-call | tf_op jit(solution)/shard_map/finish_rows/pallas_call | solution.py:244
  186.6 0.0 collective-permute-done.9.last
  186.6 0.7 copy-done.6
  187.4 4.0 %finish_cols.2._ = bf16[256,128,128]{2,1,0:T(8,128)(2,1)} custom-call(s32[104]{0:T(128)} %index_ref.15, s32[104]{0:T(128)} %multiply_add_fusion.place_ref, bf16[12,256,128]{2,1,0:T(8,128)(2,1)} %get-tuple-element.30.kept, bf16[12,256,128]{2,1,0:T(8,128)(2,1)} %copy-done.2, bf16[12,128,128]{2,1,0:T(8,128)(2,1)} %copy-done.6, ...), custom_call_target="tpu_custom_call", output_to_operand_aliasing={{}: (6, {})} | custom-call | tf_op jit(solution)/shard_map/finish_cols/pallas_call | solution.py:244
  191.4 0.0 collective-permute-done.7.last
  191.4 7.6 %finish_rows.3._ = bf16[256,128,128]{2,1,0:T(8,128)(2,1)} custom-call(s32[104]{0:T(128)} %index_ref.15, s32[104]{0:T(128)} %multiply_add_fusion.place_ref, bf16[36,128,256]{2,1,0:T(8,128)(2,1)} %get-tuple-element.28.kept, bf16[36,128,256]{2,1,0:T(8,128)(2,1)} %collective-permute-done.6.came, ...), custom_call_target="tpu_custom_call", output_to_operand_aliasing={{}: (6, {})} | custom-call | tf_op jit(solution)/shard_map/finish_rows/pallas_call | solution.py:244
  199.0 0.0 collective-permute-done.5.last
  199.0 1.1 copy-done.3
  200.1 8.7 %finish_cols.3 = bf16[256,128,128]{2,1,0:T(8,128)(2,1)} custom-call(s32[104]{0:T(128)} %index_ref.15, s32[104]{0:T(128)} %multiply_add_fusion.place_ref, bf16[44,256,128]{2,1,0:T(8,128)(2,1)} %get-tuple-element.26.kept, bf16[44,256,128]{2,1,0:T(8,128)(2,1)} %copy-done, bf16[44,128,128]{2,1,0:T(8,128)(2,1)} %copy-done.3, ...), custom_call_target="tpu_custom_call", output_to_operand_aliasing={{}: (6, {})} | custom-call | tf_op jit(solution)/shard_map/finish_cols/pallas_call | solution.py:244
  208.9 6.1 %all-to-all-start.2 = ((bf16[256,128,128]{2,1,0:T(8,128)(2,1)}), bf16[256,128,128]{2,1,0:T(8,128)(2,1)}, u32[]{:S(2)}, u32[]{:S(2)}) async-start(bf16[256,128,128]{2,1,0:T(8,128)(2,1)} %finish_cols.3), calls=%async_computation.2 | async-start | bytes 16777216 | tf_op jit(solution)/shard_map/all_to_all | solution.py:406
  215.0 2.3 pair_features.1
  217.3 3.0 collective-permute-start
  220.3 104.1 %collective-permute-done.came = bf16[4,128,256]{2,1,0:T(8,128)(2,1)S(1)} collective-permute-done((bf16[4,128,256]{2,1,0:T(8,128)(2,1)}, bf16[4,128,256]{2,1,0:T(8,128)(2,1)S(1)}, u32[]{:S(2)}, u32[]{:S(2)}) %collective-permute-start) | collective-permute-done | bytes 262176 | tf_op jit(solution)/shard_map/ppermute | solution.py:21
  324.4 0.7 copy-done.7
  325.1 2.1 join_features.1
  327.2 0.0 collective-permute-start.1
  327.2 0.7 collective-permute-start.2
  327.9 2.6 collective-permute-start.3
  330.5 0.1 broadcast_in_dim.23
  330.6 1.0 bitcast_dynamic-update-slice_fusion.3
  331.6 10.4 %collective-permute-done.1 = bf16[4,128,256]{2,1,0:T(8,128)(2,1)S(1)} collective-permute-done((bf16[4,128,256]{2,1,0:T(8,128)(2,1)}, bf16[4,128,256]{2,1,0:T(8,128)(2,1)S(1)}, u32[]{:S(2)}, u32[]{:S(2)}) %collective-permute-start.1) | collective-permute-done | bytes 262176 | tf_op jit(solution)/shard_map/ppermute | solution.py:395
  342.0 0.0 collective-permute-done.2
  342.1 0.6 collective-permute-done.3
  342.6 0.0 copy-start.4
  342.6 0.0 all-to-all-done.2
  342.7 10.9 %copy.32 = bf16[256,128,128]{2,1,0:T(8,128)(2,1)} copy(bf16[256,128,128]{2,1,0:T(8,128)(2,1)} %all-to-all-done.2) | data formatting | bytes 16777216
  (16 shorter events, 0.1 us)
Async XLA Ops:
  19.2 66.1 %collective-permute-start.4 = (bf16[44,256,128]{2,1,0:T(8,128)(2,1)}, bf16[44,256,128]{2,1,0:T(8,128)(2,1)S(1)}, u32[]{:S(2)}, u32[]{:S(2)}) collective-permute-start(bf16[44,256,128]{2,1,0:T(8,128)(2,1)} %get-tuple-element.27), channel_id=1, source_target_pairs={{0,8},{1,9},{2,10},{3,11},{4,12},{5,13},{6,14},{7,15},{8,0},{9,1},... | collective-permute-start | bytes 8650760 | tf_op jit(solution)/shard_map/ppermute | solution.py:21
  35.8 75.2 %collective-permute-start.6 = (bf16[36,128,256]{2,1,0:T(8,128)(2,1)}, bf16[36,128,256]{2,1,0:T(8,128)(2,1)}, u32[]{:S(2)}, u32[]{:S(2)}) collective-permute-start(bf16[36,128,256]{2,1,0:T(8,128)(2,1)} %get-tuple-element.29), channel_id=1, source_target_pairs={{0,64},{16,80},{32,96},{48,112},{64,0},{80,16},{96,32},{112,48},{1... | collective-permute-start | bytes 7077896 | tf_op jit(solution)/shard_map/ppermute | solution.py:21
  85.3 1.6 copy-start
  90.8 108.2 %collective-permute-start.5 = (bf16[44,128,128]{2,1,0:T(8,128)(2,1)}, bf16[44,128,128]{2,1,0:T(8,128)(2,1)S(1)}, u32[]{:S(2)}, u32[]{:S(2)}) collective-permute-start(bf16[44,128,128]{2,1,0:T(8,128)(2,1)} %forward.4), channel_id=1, source_target_pairs={{0,64},{16,80},{32,96},{48,112},{64,0},{80,16},{96,32},{112,48},{1... | collective-permute-start | bytes 4325384 | tf_op jit(solution)/shard_map/ppermute | solution.py:21
  100.5 41.5 %collective-permute-start.10 = (bf16[12,128,256]{2,1,0:T(8,128)(2,1)}, bf16[12,128,256]{2,1,0:T(8,128)(2,1)S(1)}, u32[]{:S(2)}, u32[]{:S(2)}) collective-permute-start(bf16[12,128,256]{2,1,0:T(8,128)(2,1)} %get-tuple-element.33), channel_id=1, source_target_pairs={{0,64},{16,80},{32,96},{48,112},{64,0},{80,16},{96,32},{112,48},{1... | collective-permute-start | bytes 2359304 | tf_op jit(solution)/shard_map/ppermute | solution.py:21
  108.0 39.5 %collective-permute-start.8 = (bf16[12,256,128]{2,1,0:T(8,128)(2,1)}, bf16[12,256,128]{2,1,0:T(8,128)(2,1)S(1)}, u32[]{:S(2)}, u32[]{:S(2)}) collective-permute-start(bf16[12,256,128]{2,1,0:T(8,128)(2,1)} %get-tuple-element.31), channel_id=1, source_target_pairs={{0,8},{1,9},{2,10},{3,11},{4,12},{5,13},{6,14},{7,15},{8,0},{9,1},... | collective-permute-start | bytes 2359304 | tf_op jit(solution)/shard_map/ppermute | solution.py:21
  114.5 38.8 %copy-start.8 = (s32[104,2]{0,1:T(2,128)S(1)}, s32[104,2]{0,1:T(2,128)}, u32[]{:S(2)}) copy-start(s32[104,2]{0,1:T(2,128)} %param.15) | copy-start | bytes 2500
  114.5 76.9 %collective-permute-start.7 = (bf16[36,128,128]{2,1,0:T(8,128)(2,1)}, bf16[36,128,128]{2,1,0:T(8,128)(2,1)}, u32[]{:S(2)}, u32[]{:S(2)}) collective-permute-start(bf16[36,128,128]{2,1,0:T(8,128)(2,1)} %forward.5), channel_id=1, source_target_pairs={{0,8},{1,9},{2,10},{3,11},{4,12},{5,13},{6,14},{7,15},{8,0},{9,1},... | collective-permute-start | bytes 3538952 | tf_op jit(solution)/shard_map/ppermute | solution.py:21
  116.9 39.1 %all-to-all-start = ((f32[16,1,256]{2,1,0:T(1,128)}), f32[16,1,256]{2,1,0:T(1,128)S(1)}, u32[]{:S(2)}, u32[]{:S(2)}) async-start(f32[16,1,256]{2,1,0:T(1,128)} %broadcast_select_fusion), calls=%async_computation | async-start | bytes 32768 | tf_op jit(solution)/shard_map/all_to_all | solution.py:365
  142.0 0.9 copy-start.1
  144.8 36.9 %collective-permute-start.11 = (bf16[12,128,128]{2,1,0:T(8,128)(2,1)}, bf16[12,128,128]{2,1,0:T(8,128)(2,1)S(1)}, u32[]{:S(2)}, u32[]{:S(2)}) collective-permute-start(bf16[12,128,128]{2,1,0:T(8,128)(2,1)} %forward.7), channel_id=1, source_target_pairs={{0,8},{1,9},{2,10},{3,11},{4,12},{5,13},{6,14},{7,15},{8,0},{9,1},... | collective-permute-start | bytes 1179656 | tf_op jit(solution)/shard_map/ppermute | solution.py:21
  147.5 0.9 copy-start.2
  150.4 36.2 %collective-permute-start.9 = (bf16[12,128,128]{2,1,0:T(8,128)(2,1)}, bf16[12,128,128]{2,1,0:T(8,128)(2,1)S(1)}, u32[]{:S(2)}, u32[]{:S(2)}) collective-permute-start(bf16[12,128,128]{2,1,0:T(8,128)(2,1)} %forward.6), channel_id=1, source_target_pairs={{0,64},{16,80},{32,96},{48,112},{64,0},{80,16},{96,32},{112,48},{1... | collective-permute-start | bytes 1179656 | tf_op jit(solution)/shard_map/ppermute | solution.py:21
  156.8 19.5 %all-to-all-start.1 = ((f32[128,1,256]{2,1,0:T(1,128)}), f32[128,1,256]{2,1,0:T(1,128)S(1)}, u32[]{:S(2)}, u32[]{:S(2)}) async-start(f32[128,1,256]{2,1,0:T(1,128)} %broadcast_in_dim.24), calls=%async_computation.1 | async-start | bytes 262144 | tf_op jit(solution)/shard_map/all_to_all | solution.py:367
  181.7 0.8 copy-start.5
  186.6 0.8 copy-start.6
  199.0 1.1 copy-start.3
  208.9 133.8 %all-to-all-start.2 = ((bf16[256,128,128]{2,1,0:T(8,128)(2,1)}), bf16[256,128,128]{2,1,0:T(8,128)(2,1)}, u32[]{:S(2)}, u32[]{:S(2)}) async-start(bf16[256,128,128]{2,1,0:T(8,128)(2,1)} %finish_cols.3), calls=%async_computation.2 | async-start | bytes 16777216 | tf_op jit(solution)/shard_map/all_to_all | solution.py:406
  217.3 107.1 %collective-permute-start = (bf16[4,128,256]{2,1,0:T(8,128)(2,1)}, bf16[4,128,256]{2,1,0:T(8,128)(2,1)S(1)}, u32[]{:S(2)}, u32[]{:S(2)}) collective-permute-start(bf16[4,128,256]{2,1,0:T(8,128)(2,1)} %get-tuple-element.20), channel_id=1, source_target_pairs={{0,64},{16,80},{32,96},{48,112},{64,0},{80,16},{96,32},{112,48},{1... | collective-permute-start | bytes 786440 | tf_op jit(solution)/shard_map/ppermute | solution.py:21
  324.4 0.7 copy-start.7
  327.2 14.8 %collective-permute-start.1 = (bf16[4,128,256]{2,1,0:T(8,128)(2,1)}, bf16[4,128,256]{2,1,0:T(8,128)(2,1)S(1)}, u32[]{:S(2)}, u32[]{:S(2)}) collective-permute-start(bf16[4,128,256]{2,1,0:T(8,128)(2,1)} %join_features.1), channel_id=1, source_target_pairs={{0,1},{1,2},{2,3},{3,0},{4,5},{5,6},{6,7},{7,4},{8,9},{9,10},{10,1... | collective-permute-start | bytes 786440 | tf_op jit(solution)/shard_map/ppermute | solution.py:395
  327.2 14.8 %collective-permute-start.2 = (bf16[4,128,256]{2,1,0:T(8,128)(2,1)}, bf16[4,128,256]{2,1,0:T(8,128)(2,1)S(1)}, u32[]{:S(2)}, u32[]{:S(2)}) collective-permute-start(bf16[4,128,256]{2,1,0:T(8,128)(2,1)} %join_features.1), channel_id=1, source_target_pairs={{0,2},{1,3},{2,0},{3,1},{4,6},{5,7},{6,4},{7,5},{8,10},{9,11},{10,... | collective-permute-start | bytes 786440 | tf_op jit(solution)/shard_map/ppermute | solution.py:395
  327.9 14.7 %collective-permute-start.3 = (bf16[4,128,256]{2,1,0:T(8,128)(2,1)}, bf16[4,128,256]{2,1,0:T(8,128)(2,1)S(1)}, u32[]{:S(2)}, u32[]{:S(2)}) collective-permute-start(bf16[4,128,256]{2,1,0:T(8,128)(2,1)} %join_features.1), channel_id=1, source_target_pairs={{0,3},{1,0},{2,1},{3,2},{4,7},{5,4},{6,5},{7,6},{8,11},{9,8},{10,9... | collective-permute-start | bytes 786440 | tf_op jit(solution)/shard_map/ppermute | solution.py:395
  342.6 10.9 %copy-start.4 = (bf16[4,4,128,256]{3,2,1,0:T(8,128)(2,1)}, bf16[4,4,128,256]{3,2,1,0:T(8,128)(2,1)S(1)}, u32[]{:S(2)}) copy-start(bf16[4,4,128,256]{3,2,1,0:T(8,128)(2,1)S(1)} %bitcast_dynamic-update-slice_fusion) | copy-start | bytes 3145732

commit v2 on v1

v2 whole, which is shorter than its diff:
```python
import functools

import jax
import jax.numpy as jnp
from jax import lax
from jax.experimental import pallas as pl
from jax.experimental.pallas import tpu as pltpu
from jax.sharding import PartitionSpec as P


TILE = 256
HALF = 128
STEP = 8
LANES = 4
ROW_FIRST = 48
CHUNKS = (8, 16), (24, 24), (16, 16)
BF16 = jnp.bfloat16
F32 = jnp.float32
PARAMS = pltpu.CompilerParams(vmem_limit_bytes=60 << 20)
ANYWHERE = pl.BlockSpec(memory_space=pl.ANY)


def flipped(value, axis, mask):
    pairs = [(source, source ^ mask) for source in range(lax.axis_size(axis))]
    return lax.ppermute(value, axis, pairs)


def full(shape):
    return pl.BlockSpec(shape, lambda *_: (0,) * len(shape))


def iota(shape, axis):
    return lax.broadcasted_iota(jnp.int32, shape, axis)


def position():
    row_half = lax.axis_size("row") // 2
    col_half = lax.axis_size("col") // 2
    row_index = lax.axis_index("row")
    col_index = lax.axis_index("col")
    return (
        lax.div(row_index, row_half),
        lax.rem(row_index, row_half),
        lax.div(col_index, col_half),
        lax.rem(col_index, col_half),
    )


def build_tables(partner_ref, row_tables, col_tables):
    row_side, row_group, col_side, col_group = position()
    tiles_row = row_tables.shape[0]
    tiles_col = col_tables.shape[0]
    coarse_nodes = partner_ref.shape[0] * HALF // 2
    rotated = (iota((1, TILE), 1) + HALF) & (TILE - 1)
    level = iota((TILE, TILE), 0)

    def vector(start, shift):
        first = partner_ref[pl.ds(start, 1), :]
        second = partner_ref[pl.ds(start + 1, 1), :]
        return jnp.concatenate([first, second], axis=1) - shift

    def table(values):
        return (jnp.broadcast_to(values, (TILE, TILE)) == level).astype(F32).astype(BF16)

    for i in range(tiles_row):
        k = row_group * tiles_row + i
        slots = vector(coarse_nodes // HALF + 2 * k, k * TILE)
        row_tables[i] = table(jnp.where(row_side == 1, slots, rotated))
    for j in range(tiles_col):
        k = col_group * tiles_col + j
        nodes = vector(2 * k, coarse_nodes + k * TILE)
        col_tables[j] = table(jnp.where(col_side == 1, nodes, rotated))


def pair_kernel(
    starts, counts, with_features, index_ref, pert_ref, lane_ref, tiles, partner_ref, perts, *rest
):
    if with_features:
        features, rest = rest[0], rest[1:]
    _, row_given, row_kept, col_given, col_kept, row_tables, col_tables, rows = rest
    tiles_col = col_tables.shape[0]
    step = pl.program_id(0)
    row_steps = counts[0] // STEP
    pert_count = pert_ref.shape[0]
    first = jnp.where(
        step < row_steps, starts[0] + step * STEP, starts[1] + (step - row_steps) * STEP
    )

    @pl.when(step == 0)
    def _():
        build_tables(partner_ref, row_tables, col_tables)

    hits = sum(
        ((pert_ref[p] >= first) & (pert_ref[p] < first + STEP)).astype(jnp.int32)
        for p in range(pert_count)
    )

    @pl.when(hits > 0)
    def _():
        for t in range(STEP):
            found = sum((pert_ref[p] == first + t).astype(jnp.int32) for p in range(pert_count))

            @pl.when(found > 0)
            def _():
                total = tiles[t].astype(F32)
                for p in range(pert_count):
                    total = total + jnp.where(pert_ref[p] == first + t, perts[p].astype(F32), 0.0)
                tiles[t] = total.astype(BF16)

    def put(t, both, given, kept, row_first):
        cross = both[:HALF, HALF:], both[HALF:, :HALF]
        given[0, t] = both[:HALF, :HALF]
        given[1, t] = cross[0 if row_first else 1]
        kept[0, t] = cross[1 if row_first else 0]
        kept[1, t] = both[HALF:, HALF:]

    def compute(given, kept, row_first):
        for t in range(STEP):
            i = lax.div(index_ref[first + t], tiles_col)
            rows[t] = jnp.dot(row_tables[i], tiles[t], preferred_element_type=F32).astype(BF16)
        for t in range(STEP):
            j = lax.rem(index_ref[first + t], tiles_col)
            both = jnp.dot(rows[t], col_tables[j], preferred_element_type=F32).astype(BF16)
            put(t, both, given, kept, row_first)

    @pl.when(step < row_steps)
    def _():
        compute(row_given, row_kept, True)
        if with_features:
            for t in range(features.shape[0]):
                table = row_tables[lane_ref[0] * features.shape[0] + t]
                both = jnp.dot(table, features[t], preferred_element_type=F32).astype(BF16)
                put(STEP + t, both, row_given, row_kept, True)

    @pl.when(step >= row_steps)
    def _():
        compute(col_given, col_kept, False)


def pair_tiles(
    starts, counts, index, pert_slot, lane, tile_values, partner, pert_values, features, sizes, token
):
    tiles_row, tiles_col = sizes
    row_steps, col_steps = counts[0] // STEP, counts[1] // STEP
    row_block, col_block = starts[0] // STEP, starts[1] // STEP
    with_features = features is not None
    extra = features.shape[0] // LANES if with_features else 0

    def tile_map(s, *_):
        return (jnp.where(s < row_steps, row_block + s, col_block + s - row_steps), 0, 0)

    shapes = [
        jax.ShapeDtypeStruct((2, count, HALF, HALF), BF16)
        for count in (counts[0] + extra,) * 2 + (counts[1],) * 2
    ]
    if with_features:
        row_out = full(shapes[0].shape)
    else:
        row_out = pl.BlockSpec(
            (2, STEP, HALF, HALF), lambda s, *_: (0, jnp.minimum(s, row_steps - 1), 0, 0)
        )
    col_out = pl.BlockSpec(
        (2, STEP, HALF, HALF), lambda s, *_: (0, jnp.maximum(s - row_steps, 0), 0, 0)
    )
    in_specs = [
        pl.BlockSpec((STEP, TILE, TILE), tile_map),
        full(partner.shape),
        full(pert_values.shape),
    ]
    operands = [tile_values, partner, pert_values]
    if with_features:
        in_specs.append(
            pl.BlockSpec((extra,) + features.shape[1:], lambda s, a, b, lane: (lane[0], 0, 0))
        )
        operands.append(features)
    return pl.pallas_call(
        functools.partial(pair_kernel, starts, counts, with_features),
        out_shape=shapes,
        grid_spec=pltpu.PrefetchScalarGridSpec(
            num_scalar_prefetch=3,
            grid=(row_steps + col_steps,),
            in_specs=in_specs + [ANYWHERE],
            out_specs=[row_out, row_out, col_out, col_out],
            scratch_shapes=[
                pltpu.VMEM((tiles_row, TILE, TILE), BF16),
                pltpu.VMEM((tiles_col, TILE, TILE), BF16),
                pltpu.VMEM((STEP, TILE, TILE), BF16),
            ],
        ),
        compiler_params=PARAMS,
        name="pair_tiles",
    )(index, pert_slot, lane, *operands, token)


def sum_kernel(bounds, tiles_col, index_ref, *rest):
    pieces, sums, total = rest[:-2], rest[-2], rest[-1]
    step = pl.program_id(0)

    @pl.when(step == 0)
    def _():
        total[...] = jnp.zeros_like(total)

    for number, (begin, steps, start, row_first) in enumerate(bounds):
        given, kept = pieces[2 * number], pieces[2 * number + 1]

        @pl.when((step >= begin) & (step < begin + steps))
        def _():
            for t in range(STEP):
                i = lax.div(index_ref[start + (step - begin) * STEP + t], tiles_col)
                cross = given[1, t].astype(F32), kept[0, t].astype(F32)
                given_part, kept_part = cross if row_first else cross[::-1]
                total[0, i] += given[0, t].astype(F32) + given_part
                total[1, i] += kept[1, t].astype(F32) + kept_part

    @pl.when(step == pl.num_programs(0) - 1)
    def _():
        row_side = position()[0]
        for i in range(total.shape[1]):
            given_line = jnp.sum(total[0, i].T, axis=0, keepdims=True)
            kept_line = jnp.sum(total[1, i].T, axis=0, keepdims=True)
            sums[i : i + 1, :HALF] = jnp.where(row_side == 1, given_line, kept_line)
            sums[i : i + 1, HALF:] = jnp.where(row_side == 1, kept_line, given_line)


def sum_rows(pieces, index, sizes):
    tiles_row, tiles_col = sizes
    bounds, specs, operands = [], [], []
    begin = 0
    for piece in pieces:
        steps = piece["count"] // STEP

        def block_map(s, *_, begin=begin, steps=steps):
            return (0, jnp.clip(s - begin, 0, steps - 1), 0, 0)

        specs += [pl.BlockSpec((2, STEP, HALF, HALF), block_map)] * 2
        operands += [piece["given"], piece["kept"]]
        bounds.append((begin, steps, piece["start"], piece["row_first"]))
        begin += steps
    return pl.pallas_call(
        functools.partial(sum_kernel, bounds, tiles_col),
        out_shape=jax.ShapeDtypeStruct((tiles_row, TILE), F32),
        grid_spec=pltpu.PrefetchScalarGridSpec(
            num_scalar_prefetch=1,
            grid=(begin,),
            in_specs=specs,
            out_specs=full((tiles_row, TILE)),
            scratch_shapes=[pltpu.VMEM((2, tiles_row, HALF, HALF), F32)],
        ),
        compiler_params=PARAMS,
        name="sum_rows",
    )(index, *operands)


def line_kernel(spread, _, out):
    line = jnp.sum(spread[...], axis=0, keepdims=True)
    out[...] = jnp.broadcast_to(line, out.shape)


def line_copies(spread, devices, token):
    return pl.pallas_call(
        line_kernel,
        out_shape=jax.ShapeDtypeStruct((devices, TILE), F32),
        in_specs=[pl.BlockSpec(memory_space=pltpu.VMEM), ANYWHERE],
        out_specs=pl.BlockSpec(memory_space=pltpu.VMEM),
        compiler_params=PARAMS,
        name="line_copies",
    )(spread, token)


def forward_kernel(steps, *refs):
    row_kept, row_came, col_kept, col_came = refs[:4]
    row_given, col_given = refs[-2:]
    step = pl.program_id(0)

    def both(kept, came, given):
        given[...] = (kept[0].astype(F32) + came[0].astype(F32)).astype(BF16)

    pl.when(step < steps[0])(lambda: both(row_kept, row_came, row_given))
    pl.when(step < steps[1])(lambda: both(col_kept, col_came, col_given))


def quadrant(which, steps):
    return pl.BlockSpec(
        (1, STEP, HALF, HALF), lambda s, *_: (which, jnp.minimum(s, steps - 1), 0, 0)
    )


def plain(steps):
    return pl.BlockSpec((STEP, HALF, HALF), lambda s, *_: (jnp.minimum(s, steps - 1), 0, 0))


def forward(pair, tokens):
    steps = [piece["count"] // STEP for piece in pair]
    operands = [piece[key] for piece in pair for key in ("kept", "came")]
    return pl.pallas_call(
        functools.partial(forward_kernel, steps),
        out_shape=[jax.ShapeDtypeStruct((piece["count"], HALF, HALF), BF16) for piece in pair],
        grid=(max(steps),),
        in_specs=[quadrant(0, steps[k // 2]) for k in range(4)] + [ANYWHERE] * len(tokens),
        out_specs=[plain(steps[0]), plain(steps[1])],
        compiler_params=PARAMS,
        name="forward",
    )(*operands, *tokens)


def zero_kernel(_, out):
    out[...] = jnp.zeros_like(out)


def zero_buffer(count, token):
    return pl.pallas_call(
        zero_kernel,
        out_shape=jax.ShapeDtypeStruct((count, HALF, HALF), BF16),
        grid=(count // 64,),
        in_specs=[ANYWHERE],
        out_specs=pl.BlockSpec((64, HALF, HALF), lambda s: (s, 0, 0)),
        compiler_params=PARAMS,
        name="zero_buffer",
    )(token)


def store_roots(raw, scale):
    half = raw.shape[0] // 2
    total = raw[:half] + raw[half:]
    roots = 1.0 / jnp.sqrt(1.0 + total / (total.shape[0] * total.shape[1]))
    scale[0] = roots[:, :HALF]
    scale[1] = roots[:, HALF:]


def upright(line):
    return jnp.broadcast_to(line, (HALF, HALF)).T


def finish_kernel(starts, counts, index_ref, place_ref, *refs):
    pieces, raw = (refs[0:3], refs[3:6]), refs[6]
    out, scale, row_scale, col_scale, done, sem = refs[-6:]
    tiles_row = row_scale.shape[0]
    tiles_col = col_scale.shape[0]
    step = pl.program_id(0)

    @pl.when(step == 0)
    def _():
        row_side, row_group, col_side, col_group = position()
        store_roots(raw, scale)
        for i in range(tiles_row):
            row_scale[i] = upright(scale[row_side, pl.ds(row_group * tiles_row + i, 1), :])
        for j in range(tiles_col):
            line = scale[col_side, pl.ds(col_group * tiles_col + j, 1), :]
            col_scale[j] = jnp.broadcast_to(line, (8, HALF))

    for number in range(2):
        kept, came, last = pieces[number]
        base = number * counts[0]

        @pl.when(step < counts[number] // STEP)
        def _():
            for t in range(STEP):
                m = step * STEP + t
                n = starts[number] + m
                i = lax.div(index_ref[n], tiles_col)
                j = lax.rem(index_ref[n], tiles_col)
                total = kept[0, t].astype(F32) + came[0, t].astype(F32) + last[t].astype(F32)
                done[base + m] = (total * row_scale[i] * col_scale[j, 0:1]).astype(BF16)
                pltpu.make_async_copy(done.at[base + m], out.at[place_ref[n]], sem).start()

    @pl.when(step == pl.num_programs(0) - 1)
    def _():
        pltpu.make_async_copy(done, out.at[pl.ds(0, done.shape[0])], sem).wait()


def finish(pair, index, place, raw, buffer, sizes, token):
    tiles_row, tiles_col = sizes
    starts = [piece["start"] for piece in pair]
    counts = [piece["count"] for piece in pair]
    specs, operands = [], []
    for piece in pair:
        steps = piece["count"] // STEP
        specs += [quadrant(1, steps), quadrant(1, steps), plain(steps)]
        operands += [piece["kept"], piece["came"], piece["last"]]
    return pl.pallas_call(
        functools.partial(finish_kernel, starts, counts),
        out_shape=jax.ShapeDtypeStruct(buffer.shape, BF16),
        grid_spec=pltpu.PrefetchScalarGridSpec(
            num_scalar_prefetch=2,
            grid=(max(counts) // STEP,),
            in_specs=specs + [full(raw.shape), ANYWHERE, ANYWHERE],
            out_specs=ANYWHERE,
            scratch_shapes=[
                pltpu.VMEM((2, raw.shape[0] // 2, HALF), F32),
                pltpu.VMEM((tiles_row, HALF, HALF), F32),
                pltpu.VMEM((tiles_col, 8, HALF), F32),
                pltpu.VMEM((sum(counts), HALF, HALF), BF16),
                pltpu.SemaphoreType.DMA,
            ],
        ),
        input_output_aliases={9: 0},
        compiler_params=PARAMS,
        name="finish",
    )(index, place, *operands, raw, buffer, token)


def join_kernel(tiles_row, lane_ref, kept, came, weight, raw, _, out, scale):
    row_side, row_group, _, _ = position()
    part = out.shape[0]
    store_roots(raw, scale)
    for t in range(part):
        merged = [
            (kept[h, t].astype(F32) + came[h, t].astype(F32)).astype(BF16) for h in range(2)
        ]
        joined = jnp.dot(
            jnp.concatenate(merged, axis=1), weight[...], preferred_element_type=F32
        )
        k = row_group * tiles_row + lane_ref[0] * part + t
        column = upright(scale[row_side, pl.ds(k, 1), :])
        out[t] = (joined * jnp.concatenate([column] * 2, axis=1)).astype(BF16)


def join_features(lane, piece, weight, raw, tiles_row, token):
    part = tiles_row // LANES
    block = pl.BlockSpec((2, part, HALF, HALF), lambda s, *_: (0, piece["count"] // part, 0, 0))
    shape = (part, HALF, weight.shape[1])
    return pl.pallas_call(
        functools.partial(join_kernel, tiles_row),
        out_shape=jax.ShapeDtypeStruct(shape, BF16),
        grid_spec=pltpu.PrefetchScalarGridSpec(
            num_scalar_prefetch=1,
            grid=(1,),
            in_specs=[block, block, full(weight.shape), full(raw.shape), ANYWHERE],
            out_specs=full(shape),
            scratch_shapes=[pltpu.VMEM((2, raw.shape[0] // 2, HALF), F32)],
        ),
        compiler_params=PARAMS,
        name="join_features",
    )(lane, piece["kept"], piece["came"], weight, raw, token)


def copy_kernel(parts, source, out, held, read_sem, write_sem):
    size = source.shape[0] // parts

    def window(k):
        return pl.ds(k * size, size)

    def read(k):
        return pltpu.make_async_copy(source.at[window(k)], held.at[window(k)], read_sem.at[k])

    def write(k):
        return pltpu.make_async_copy(held.at[window(k)], out.at[window(k)], write_sem.at[k])

    for k in range(parts):
        read(k).start()
    for k in range(parts):
        read(k).wait()
        write(k).start()
    for k in range(parts):
        write(k).wait()


def copied(source):
    parts = 16
    return pl.pallas_call(
        functools.partial(copy_kernel, parts),
        out_shape=jax.ShapeDtypeStruct(source.shape, source.dtype),
        in_specs=[ANYWHERE],
        out_specs=ANYWHERE,
        scratch_shapes=[
            pltpu.VMEM(source.shape, source.dtype),
            pltpu.SemaphoreType.DMA((parts,)),
            pltpu.SemaphoreType.DMA((parts,)),
        ],
        compiler_params=PARAMS,
        name="copied",
    )(source)


def level(features, join_weight, partner, tile_index, tile_values, pert_slot, pert_values, routes):
    row_count = lax.axis_size("row")
    col_count = lax.axis_size("col")
    devices = row_count * col_count
    masks = ("row", row_count // 2), ("col", col_count // 2)
    slot_count = tile_values.shape[0]
    width = features.shape[1]
    tiles_row = features.shape[0] // TILE
    tiles_col = partner.shape[0] // TILE // col_count
    sizes = tiles_row, tiles_col
    capacity = routes.shape[1]
    part = tiles_row // LANES
    chunks = len(CHUNKS)
    lane = (lax.axis_index("col") % LANES).reshape(1)
    partner = partner.reshape(-1, HALF)
    feature_tiles = features.reshape(tiles_row, TILE, width)

    starts = [0, ROW_FIRST]
    token = pert_values
    pairs = []
    for chunk in range(chunks):
        counts = CHUNKS[chunk]
        row_given, row_kept, col_given, col_kept = pair_tiles(
            tuple(starts), counts, tile_index, pert_slot, lane, tile_values, partner,
            pert_values, feature_tiles if chunk == 0 else None, sizes, token,
        )
        token = col_kept
        pair = []
        for kind, (given, kept) in enumerate(((row_given, row_kept), (col_given, col_kept))):
            came = flipped(given, *masks[kind])
            pair.append(
                dict(
                    row_first=kind == 0, start=starts[kind], count=counts[kind],
                    given=given, kept=kept, came=came,
                )
            )
            starts[kind] += counts[kind]
        pairs.append(pair)

    own = sum_rows([piece for pair in pairs for piece in pair], tile_index, sizes)
    token = own
    spread = lax.all_to_all(own, "col", split_axis=0, concat_axis=0, tiled=True)

    targets = routes[:, 0]
    order = jnp.arange(slot_count, dtype=jnp.int32)
    same = (targets[:, None] == targets[None, :]) & (order[None, :] < order[:, None])
    place = targets * capacity + jnp.sum(same.astype(jnp.int32), axis=1)

    for chunk, pair in enumerate(pairs):
        tokens = [token]
        if chunk == chunks - 1:
            lines = line_copies(spread, devices, token)
            raw = lax.all_to_all(
                lines, ("row", "col"), split_axis=0, concat_axis=0, tiled=True
            )
            buffer = zero_buffer(devices * capacity, lines)
            tokens = [buffer]
        given = forward(pair, tokens)
        token = given[0]
        for kind in range(2):
            pair[kind]["last"] = flipped(given[kind], *masks[1 - kind])

    def finished(chunk, buffer, token):
        return finish(pairs[chunk], tile_index, place, raw, buffer, sizes, token)

    buffer = finished(0, buffer, token)
    joined = join_features(lane, pairs[0][0], join_weight, raw, tiles_row, buffer)
    buffer = finished(1, buffer, joined)
    parts = jnp.zeros((LANES, part, HALF, width), BF16)
    for shift in range(LANES):
        shared = joined
        if shift > 0:
            ring = [
                (source, source // LANES * LANES + (source + shift) % LANES)
                for source in range(col_count)
            ]
            shared = lax.ppermute(joined, "col", ring)
        parts = lax.dynamic_update_slice(
            parts, shared[None], ((lane[0] - shift) % LANES, 0, 0, 0)
        )
    buffer = finished(2, buffer, parts)
    coarse_features = parts.reshape(tiles_row * HALF, width)
    arrived = lax.all_to_all(buffer, ("row", "col"), split_axis=0, concat_axis=0, tiled=True)
    return (coarse_features, copied(arrived))


def solution(mesh):
    both = P(("row", "col"))
    placed = (
        P("row", None),
        P(),
        P(),
        both,
        P(("row", "col"), None, None),
        both,
        P(("row", "col"), None, None),
        P(("row", "col"), None),
    )
    return jax.shard_map(
        level,
        mesh=mesh,
        in_specs=placed,
        out_specs=(P("row", None), P(("row", "col"), None, None)),
        check_vma=False,
    )
```

time: 355 us -> 297 us (0.84)
  waiting for transfers between devices: 190 us -> 57.7 us
  blocking collectives: 0 us -> 106 us
  Pallas kernels: 90.5 us -> 74.4 us
  local copies, waits for them, and re-layouts: 20.1 us -> 10.1 us
  starting transfers between devices: 49.9 us -> 45.4 us
    ppermute x9 -> x12, waiting for transfers between devices: 167 us -> 46.7 us  [flipped(): return lax.ppermute(value, axis, pairs)]
    all_to_all x0 -> x1, blocking collectives: none -> 106 us  [level(): lax.all_to_all(buffer, ('row', 'col'), split_axis=0, concat_axis=0, tiled...]
    pallas_call x14 -> x12, Pallas kernels: 83.6 us -> 68.3 us  [the longest x3 25.8 us: pair_tiles(): pl.pallas_call(functools.partial(pair_kernel, starts, counts, with_featur...]
    unnamed x21 -> x24, local copies, waits for them, and re-layouts: 18.3 us -> 4.03 us
    all_to_all x3 -> x2, waiting for transfers between devices: 11.3 us -> 1.54 us  [the longest x1 1.54 us: level(): lax.all_to_all(lines, ('row', 'col'), split_axis=0, concat_axis=0, tiled=...]
    all_to_all x3 -> x2, starting transfers between devices: 24.6 us -> 16.7 us  [the longest x1 10.7 us: level(): lax.all_to_all(lines, ('row', 'col'), split_axis=0, concat_axis=0, tiled=...]
    ppermute x9 -> x12, starting transfers between devices: 22 us -> 25.9 us  [flipped(): return lax.ppermute(value, axis, pairs)]
  transfers between devices with their start and end apart: 15 -> 17, of which waited for: 7 -> 7; matrix products, arithmetic and copies ran while one was open for 1% -> 3% of each run, Pallas kernels for 18% -> 14%
where the time goes in v2:
time: 297 us; the launch traced here: 295 us
  blocking collectives  106 us (36%)
  Pallas kernels  74.4 us (25%)
  waiting for transfers between devices  57.7 us (19%)
  starting transfers between devices  45.4 us (15%)
  local copies, waits for them, and re-layouts  10.1 us (3%)
    all_to_all x1, blocking collectives, level(): lax.all_to_all(buffer, ('row', 'col'), split_axis=0, concat_axis=0, tiled...  106 us
    ppermute x12, waiting for transfers between devices, flipped(): return lax.ppermute(value, axis, pairs)  46.7 us
    ppermute x12, starting transfers between devices, flipped(): return lax.ppermute(value, axis, pairs)  25.9 us
    pallas_call x3, Pallas kernels, pair_tiles(): pl.pallas_call(functools.partial(pair_kernel, starts, counts, with_featur...  25.8 us
    pallas_call x1, Pallas kernels, sum_rows(): pl.pallas_call(functools.partial(sum_kernel, bounds, tiles_col), out_shap...  13.4 us
    pallas_call x3, Pallas kernels, finish(): pl.pallas_call(functools.partial(finish_kernel, starts, counts), out_shap...  12.6 us
    all_to_all x1, starting transfers between devices, level(): lax.all_to_all(lines, ('row', 'col'), split_axis=0, concat_axis=0, tiled=...  10.7 us
    ppermute x3, waiting for transfers between devices, level(): shared = lax.ppermute(joined, 'col', ring)  9.46 us
  transfers between devices with their start and end apart: 17, of which 7 were waited for; matrix products, arithmetic and copies ran while one was open for 3% of the time, Pallas kernels for 14%

profile of v2, /device:TPU:32, one launch (start us, length us, event | category | flops | bytes accessed | tf_op | source)
XLA Modules:
  0.0 294.9 jit_solution(16953396108610684818)
XLA Ops:
  0.6 7.4 %pair_tiles.3 = (bf16[2,12,128,128]{3,2,1,0:T(8,128)(2,1)}, bf16[2,12,128,128]{3,2,1,0:T(8,128)(2,1)}, bf16[2,16,128,128]{3,2,1,0:T(8,128)(2,1)}, bf16[2,16,128,128]{3,2,1,0:T(8,128)(2,1)}) custom-call(s32[104]{0:T(128)} %index_ref.13, s32[4]{0:T(128)} %pert_ref.5, s32[1]{0:T(128)} %bitcast.lane_ref, bf16[104,256,256]{2,1,0:T(8,128)(2,1)} %tiles.5, ...), custom_call_target="tpu_custom_call" | custom-call | tf_op jit(solution)/shard_map/pair_tiles/pallas_call | solution.py:176
  8.0 10.5 %pair_tiles.4 = (bf16[2,24,128,128]{3,2,1,0:T(8,128)(2,1)}, bf16[2,24,128,128]{3,2,1,0:T(8,128)(2,1)}, bf16[2,24,128,128]{3,2,1,0:T(8,128)(2,1)}, bf16[2,24,128,128]{3,2,1,0:T(8,128)(2,1)}) custom-call(s32[104]{0:T(128)} %index_ref.13, s32[4]{0:T(128)} %pert_ref.5, s32[1]{0:T(128)} %bitcast.lane_ref, bf16[104,256,256]{2,1,0:T(8,128)(2,1)} %tiles.5, ...), custom_call_target="tpu_custom_call" | custom-call | tf_op jit(solution)/shard_map/pair_tiles/pallas_call | solution.py:176
  18.5 3.0 %collective-permute-start.1 = (bf16[2,24,128,128]{3,2,1,0:T(8,128)(2,1)}, bf16[2,24,128,128]{3,2,1,0:T(8,128)(2,1)S(1)}, u32[]{:S(2)}, u32[]{:S(2)}) collective-permute-start(bf16[2,24,128,128]{3,2,1,0:T(8,128)(2,1)} %get-tuple-element.24.rest_4_), channel_id=1, source_target_pairs={{0,64},{16,80},{32,96},{48,112},{64,0},{80,16},{96,32},{112,48},{1... | collective-permute-start | bytes 4718600 | tf_op jit(solution)/shard_map/ppermute | solution.py:25
  21.6 0.5 collective-permute-start
  22.1 3.0 %collective-permute-start.2 = (bf16[2,24,128,128]{3,2,1,0:T(8,128)(2,1)}, bf16[2,24,128,128]{3,2,1,0:T(8,128)(2,1)}, u32[]{:S(2)}, u32[]{:S(2)}) collective-permute-start(bf16[2,24,128,128]{3,2,1,0:T(8,128)(2,1)} %get-tuple-element.26.rest_6_), channel_id=1, source_target_pairs={{0,8},{1,9},{2,10},{3,11},{4,12},{5,13},{6,14},{7,15},{8,0},{9,1},... | collective-permute-start | bytes 4718600 | tf_op jit(solution)/shard_map/ppermute | solution.py:25
  25.1 0.5 collective-permute-start.3
  25.6 7.9 %pair_tiles.5 = (bf16[2,16,128,128]{3,2,1,0:T(8,128)(2,1)}, bf16[2,16,128,128]{3,2,1,0:T(8,128)(2,1)}, bf16[2,16,128,128]{3,2,1,0:T(8,128)(2,1)}, bf16[2,16,128,128]{3,2,1,0:T(8,128)(2,1)}) custom-call(s32[104]{0:T(128)} %index_ref.13, s32[4]{0:T(128)} %pert_ref.5, s32[1]{0:T(128)} %bitcast.lane_ref, bf16[104,256,256]{2,1,0:T(8,128)(2,1)} %tiles.5, ...), custom_call_target="tpu_custom_call" | custom-call | tf_op jit(solution)/shard_map/pair_tiles/pallas_call | solution.py:176
  33.5 3.0 %collective-permute-start.6 = (bf16[2,16,128,128]{3,2,1,0:T(8,128)(2,1)}, bf16[2,16,128,128]{3,2,1,0:T(8,128)(2,1)S(1)}, u32[]{:S(2)}, u32[]{:S(2)}) collective-permute-start(bf16[2,16,128,128]{3,2,1,0:T(8,128)(2,1)} %get-tuple-element.28.rest_8_), channel_id=1, source_target_pairs={{0,64},{16,80},{32,96},{48,112},{64,0},{80,16},{96,32},{112,48},{1... | collective-permute-start | bytes 3145736 | tf_op jit(solution)/shard_map/ppermute | solution.py:25
  36.5 37.9 %collective-permute-done.refs_1_.came = bf16[2,12,128,128]{3,2,1,0:T(8,128)(2,1)S(1)} collective-permute-done((bf16[2,12,128,128]{3,2,1,0:T(8,128)(2,1)}, bf16[2,12,128,128]{3,2,1,0:T(8,128)(2,1)S(1)}, u32[]{:S(2)}, u32[]{:S(2)}) %collective-permute-start) | collective-permute-done | bytes 786464 | tf_op jit(solution)/shard_map/ppermute | solution.py:25
  74.4 3.0 %collective-permute-start.7 = (bf16[2,16,128,128]{3,2,1,0:T(8,128)(2,1)}, bf16[2,16,128,128]{3,2,1,0:T(8,128)(2,1)}, u32[]{:S(2)}, u32[]{:S(2)}) collective-permute-start(bf16[2,16,128,128]{3,2,1,0:T(8,128)(2,1)} %get-tuple-element.30.rest_10_), channel_id=1, source_target_pairs={{0,8},{1,9},{2,10},{3,11},{4,12},{5,13},{6,14},{7,15},{8,0},{9,1},... | collective-permute-start | bytes 3145736 | tf_op jit(solution)/shard_map/ppermute | solution.py:25
  77.4 13.4 %sum_rows.1.refs_4_ = f32[16,256]{1,0:T(8,128)} custom-call(s32[104]{0:T(128)} %index_ref.13, bf16[2,12,128,128]{3,2,1,0:T(8,128)(2,1)} %get-tuple-element.21.rest_0_, bf16[2,12,128,128]{3,2,1,0:T(8,128)(2,1)} %get-tuple-element.20.rest_1_.refs_0_.kept, bf16[2,16,128,128]{3,2,1,0:T(8,128)(2,1)} %get-tuple-element.22.rest_2_, ...), custom_call_target="tpu_custom_call" | custom-call | tf_op jit(solution)/shard_map/sum_rows/pallas_call | solution.py:239
  90.8 1.3 copy.15
  92.2 6.0 %all-to-all-start = ((f32[16,1,256]{2,1,0:T(1,128)}), f32[16,1,256]{2,1,0:T(1,128)S(1)}, u32[]{:S(2)}, u32[]{:S(2)}) async-start(f32[16,1,256]{2,1,0:T(1,128)} %copy.15), calls=%async_computation | async-start | bytes 32768 | tf_op jit(solution)/shard_map/all_to_all | solution.py:516
  98.1 0.0 collective-permute-done.3.refs_3_.refs_4_
  98.2 2.3 forward.3
  100.4 3.2 %collective-permute-start.5 = (bf16[16,128,128]{2,1,0:T(8,128)(2,1)}, bf16[16,128,128]{2,1,0:T(8,128)(2,1)S(1)}, u32[]{:S(2)}, u32[]{:S(2)}) collective-permute-start(bf16[16,128,128]{2,1,0:T(8,128)(2,1)} %get-tuple-element.34), channel_id=1, source_target_pairs={{0,64},{16,80},{32,96},{48,112},{64,0},{80,16},{96,32},{112,48},{1... | collective-permute-start | bytes 1572872 | tf_op jit(solution)/shard_map/ppermute | solution.py:25
  103.6 0.0 collective-permute-done.1.refs_1_
  103.6 2.2 collective-permute-start.4
  105.8 0.2 convert_reduce_fusion
  106.0 0.0 all-to-all-done
  106.0 0.6 copy.22
  106.6 0.0 collective-permute-done.2.refs_3_.refs_4_
  106.6 3.9 %forward.4 = (bf16[24,128,128]{2,1,0:T(8,128)(2,1)}, bf16[24,128,128]{2,1,0:T(8,128)(2,1)}) custom-call(bf16[2,24,128,128]{3,2,1,0:T(8,128)(2,1)} %get-tuple-element.25.rest_5_.refs_0_, bf16[2,24,128,128]{3,2,1,0:T(8,128)(2,1)} %copy-done.1, bf16[2,24,128,128]{3,2,1,0:T(8,128)(2,1)} %get-tuple-element.27.rest_0_.rest_7_.refs_2_.refs_3_, ...), custom_call_target="tpu_custom_call" | custom-call | tf_op jit(solution)/shard_map/forward/pallas_call | solution.py:295
  110.5 1.4 line_copies.1._
  111.8 1.7 copy.16
  113.5 10.7 %all-to-all-start.1 = ((f32[128,1,256]{2,1,0:T(1,128)}), f32[128,1,256]{2,1,0:T(1,128)S(1)}, u32[]{:S(2)}, u32[]{:S(2)}) async-start(f32[128,1,256]{2,1,0:T(1,128)} %copy.16), calls=%async_computation.1 | async-start | bytes 262144 | tf_op jit(solution)/shard_map/all_to_all | solution.py:527
  124.3 0.5 multiply_add_fusion.place_ref
  124.8 3.9 %zero_buffer.1.refs_4_.refs_7_ = bf16[256,128,128]{2,1,0:T(8,128)(2,1)} custom-call(f32[128,256]{1,0:T(8,128)} %line_copies.1._), custom_call_target="tpu_custom_call" | custom-call | tf_op jit(solution)/shard_map/zero_buffer/pallas_call | solution.py:311
  128.7 0.0 collective-permute-done.6.refs_1_
  128.7 0.0 collective-permute-done.7.refs_3_.refs_4_
  128.7 0.9 copy-done.2
  129.6 2.4 forward.5
  132.1 1.5 all-to-all-done.1
  133.6 0.7 copy.21
  134.3 0.0 collective-permute-done.4.refs_2_
  134.3 0.0 collective-permute-done.5.refs_5_
  134.3 0.7 copy-done.9
  135.0 0.2 copy-done.8
  135.2 3.5 %finish.3._.refs_7_ = bf16[256,128,128]{2,1,0:T(8,128)(2,1)} custom-call(s32[104]{0:T(128)} %index_ref.13, s32[104]{0:T(128)} %multiply_add_fusion.place_ref, bf16[2,12,128,128]{3,2,1,0:T(8,128)(2,1)} %get-tuple-element.20.rest_1_.refs_0_.kept, bf16[2,12,128,128]{3,2,1,0:T(8,128)(2,1)} %copy-done, ...), custom_call_target="tpu_custom_call", output_to_operand_aliasing={{}: (9, {})} | custom-call | tf_op jit(solution)/shard_map/finish/pallas_call | solution.py:380
  138.7 0.0 copy-start.6
  138.7 2.2 join_features.1.refs_8_
  140.9 0.6 collective-permute-start.8
  141.5 2.2 collective-permute-start.9
  143.7 2.6 collective-permute-start.13
  146.3 0.9 collective-permute-start.11
  147.2 3.0 %collective-permute-start.14 = (bf16[24,128,128]{2,1,0:T(8,128)(2,1)}, bf16[24,128,128]{2,1,0:T(8,128)(2,1)S(1)}, u32[]{:S(2)}, u32[]{:S(2)}) collective-permute-start(bf16[24,128,128]{2,1,0:T(8,128)(2,1)} %get-tuple-element.37), channel_id=1, source_target_pairs={{0,64},{16,80},{32,96},{48,112},{64,0},{80,16},{96,32},{112,48},{1... | collective-permute-start | bytes 2359304 | tf_op jit(solution)/shard_map/ppermute | solution.py:25
  150.2 0.1 broadcast_in_dim.17
  150.3 1.0 bitcast_dynamic-update-slice_fusion.3
  151.3 0.9 collective-permute-start.12
  152.2 3.7 %collective-permute-done.9 = bf16[4,128,256]{2,1,0:T(8,128)(2,1)} collective-permute-done((bf16[4,128,256]{2,1,0:T(8,128)(2,1)}, bf16[4,128,256]{2,1,0:T(8,128)(2,1)}, u32[]{:S(2)}, u32[]{:S(2)}) %collective-permute-start.9) | collective-permute-done | bytes 262176 | tf_op jit(solution)/shard_map/ppermute | solution.py:551
  155.9 0.0 collective-permute-start.10
  156.0 1.0 bitcast_dynamic-update-slice_fusion.2
  156.9 1.0 bitcast_dynamic-update-slice_fusion.1
  157.9 5.7 %collective-permute-done.10 = bf16[4,128,256]{2,1,0:T(8,128)(2,1)S(1)} collective-permute-done((bf16[4,128,256]{2,1,0:T(8,128)(2,1)}, bf16[4,128,256]{2,1,0:T(8,128)(2,1)S(1)}, u32[]{:S(2)}, u32[]{:S(2)}) %collective-permute-start.10) | collective-permute-done | bytes 262176 | tf_op jit(solution)/shard_map/ppermute | solution.py:551
  163.7 0.0 copy-start.3
  163.7 2.0 collective-permute-done.13.refs_2_
  165.6 3.7 %collective-permute-done.14.refs_5_ = bf16[24,128,128]{2,1,0:T(8,128)(2,1)S(1)} collective-permute-done((bf16[24,128,128]{2,1,0:T(8,128)(2,1)}, bf16[24,128,128]{2,1,0:T(8,128)(2,1)S(1)}, u32[]{:S(2)}, u32[]{:S(2)}) %collective-permute-start.14) | collective-permute-done | bytes 786464 | tf_op jit(solution)/shard_map/ppermute | solution.py:25
  169.4 0.9 copy-done.5
  170.3 5.3 %finish.4.refs_7_ = bf16[256,128,128]{2,1,0:T(8,128)(2,1)} custom-call(s32[104]{0:T(128)} %index_ref.13, s32[104]{0:T(128)} %multiply_add_fusion.place_ref, bf16[2,24,128,128]{3,2,1,0:T(8,128)(2,1)} %get-tuple-element.25.rest_5_.refs_0_, bf16[2,24,128,128]{3,2,1,0:T(8,128)(2,1)} %copy-done.1, ...), custom_call_target="tpu_custom_call", output_to_operand_aliasing={{}: (9, {})} | custom-call | tf_op jit(solution)/shard_map/finish/pallas_call | solution.py:380
  175.6 0.0 collective-permute-done.11.refs_2_
  175.6 3.2 %collective-permute-done.12.refs_5_ = bf16[16,128,128]{2,1,0:T(8,128)(2,1)} collective-permute-done((bf16[16,128,128]{2,1,0:T(8,128)(2,1)}, bf16[16,128,128]{2,1,0:T(8,128)(2,1)}, u32[]{:S(2)}, u32[]{:S(2)}) %collective-permute-start.12) | collective-permute-done | bytes 524320 | tf_op jit(solution)/shard_map/ppermute | solution.py:25
  178.7 3.8 %finish.5 = bf16[256,128,128]{2,1,0:T(8,128)(2,1)} custom-call(s32[104]{0:T(128)} %index_ref.13, s32[104]{0:T(128)} %multiply_add_fusion.place_ref, bf16[2,16,128,128]{3,2,1,0:T(8,128)(2,1)} %get-tuple-element.29.rest_9_.refs_0_, bf16[2,16,128,128]{3,2,1,0:T(8,128)(2,1)} %copy-done.2, ...), custom_call_target="tpu_custom_call", output_to_operand_aliasing={{}: (9, {})} | custom-call | tf_op jit(solution)/shard_map/finish/pallas_call | solution.py:380
  182.5 105.6 %all_to_all.27.source = bf16[256,128,128]{2,1,0:T(8,128)(2,1)} all-to-all(bf16[256,128,128]{2,1,0:T(8,128)(2,1)} %finish.5), channel_id=1, replica_groups=mesh['row'=8,'col'=16] {'row','col'}, dimensions={0} | all-to-all | bytes 16777216 | tf_op jit(solution)/shard_map/all_to_all | solution.py:557
  288.1 6.6 %copied.1 = bf16[256,128,128]{2,1,0:T(8,128)(2,1)} custom-call(bf16[256,128,128]{2,1,0:T(8,128)(2,1)} %all_to_all.27.source), custom_call_target="tpu_custom_call" | custom-call | tf_op jit(solution)/shard_map/copied/pallas_call | solution.py:460
  (19 shorter events, 0.1 us)
Async XLA Ops:
  18.5 85.1 %collective-permute-start.1 = (bf16[2,24,128,128]{3,2,1,0:T(8,128)(2,1)}, bf16[2,24,128,128]{3,2,1,0:T(8,128)(2,1)S(1)}, u32[]{:S(2)}, u32[]{:S(2)}) collective-permute-start(bf16[2,24,128,128]{3,2,1,0:T(8,128)(2,1)} %get-tuple-element.24.rest_4_), channel_id=1, source_target_pairs={{0,64},{16,80},{32,96},{48,112},{64,0},{80,16},{96,32},{112,48},{1... | collective-permute-start | bytes 4718600 | tf_op jit(solution)/shard_map/ppermute | solution.py:25
  21.6 52.8 %collective-permute-start = (bf16[2,12,128,128]{3,2,1,0:T(8,128)(2,1)}, bf16[2,12,128,128]{3,2,1,0:T(8,128)(2,1)S(1)}, u32[]{:S(2)}, u32[]{:S(2)}) collective-permute-start(bf16[2,12,128,128]{3,2,1,0:T(8,128)(2,1)} %get-tuple-element.21.rest_0_), channel_id=1, source_target_pairs={{0,64},{16,80},{32,96},{48,112},{64,0},{80,16},{96,32},{112,48},{1... | collective-permute-start | bytes 2359304 | tf_op jit(solution)/shard_map/ppermute | solution.py:25
  22.1 84.5 %collective-permute-start.2 = (bf16[2,24,128,128]{3,2,1,0:T(8,128)(2,1)}, bf16[2,24,128,128]{3,2,1,0:T(8,128)(2,1)}, u32[]{:S(2)}, u32[]{:S(2)}) collective-permute-start(bf16[2,24,128,128]{3,2,1,0:T(8,128)(2,1)} %get-tuple-element.26.rest_6_), channel_id=1, source_target_pairs={{0,8},{1,9},{2,10},{3,11},{4,12},{5,13},{6,14},{7,15},{8,0},{9,1},... | collective-permute-start | bytes 4718600 | tf_op jit(solution)/shard_map/ppermute | solution.py:25
  25.1 73.0 %collective-permute-start.3 = (bf16[2,16,128,128]{3,2,1,0:T(8,128)(2,1)}, bf16[2,16,128,128]{3,2,1,0:T(8,128)(2,1)}, u32[]{:S(2)}, u32[]{:S(2)}) collective-permute-start(bf16[2,16,128,128]{3,2,1,0:T(8,128)(2,1)} %get-tuple-element.22.rest_2_), channel_id=1, source_target_pairs={{0,8},{1,9},{2,10},{3,11},{4,12},{5,13},{6,14},{7,15},{8,0},{9,1},... | collective-permute-start | bytes 3145736 | tf_op jit(solution)/shard_map/ppermute | solution.py:25
  33.5 95.2 %collective-permute-start.6 = (bf16[2,16,128,128]{3,2,1,0:T(8,128)(2,1)}, bf16[2,16,128,128]{3,2,1,0:T(8,128)(2,1)S(1)}, u32[]{:S(2)}, u32[]{:S(2)}) collective-permute-start(bf16[2,16,128,128]{3,2,1,0:T(8,128)(2,1)} %get-tuple-element.28.rest_8_), channel_id=1, source_target_pairs={{0,64},{16,80},{32,96},{48,112},{64,0},{80,16},{96,32},{112,48},{1... | collective-permute-start | bytes 3145736 | tf_op jit(solution)/shard_map/ppermute | solution.py:25
  74.4 23.8 %copy-start = (bf16[2,12,128,128]{3,2,1,0:T(8,128)(2,1)}, bf16[2,12,128,128]{3,2,1,0:T(8,128)(2,1)S(1)}, u32[]{:S(2)}) copy-start(bf16[2,12,128,128]{3,2,1,0:T(8,128)(2,1)S(1)} %collective-permute-done.refs_1_.came) | copy-start | bytes 2359300
  74.4 54.3 %collective-permute-start.7 = (bf16[2,16,128,128]{3,2,1,0:T(8,128)(2,1)}, bf16[2,16,128,128]{3,2,1,0:T(8,128)(2,1)}, u32[]{:S(2)}, u32[]{:S(2)}) collective-permute-start(bf16[2,16,128,128]{3,2,1,0:T(8,128)(2,1)} %get-tuple-element.30.rest_10_), channel_id=1, source_target_pairs={{0,8},{1,9},{2,10},{3,11},{4,12},{5,13},{6,14},{7,15},{8,0},{9,1},... | collective-permute-start | bytes 3145736 | tf_op jit(solution)/shard_map/ppermute | solution.py:25
  77.4 26.2 %copy-start.10 = (s32[104,2]{0,1:T(2,128)S(1)}, s32[104,2]{0,1:T(2,128)}, u32[]{:S(2)}) copy-start(s32[104,2]{0,1:T(2,128)} %param.15) | copy-start | bytes 2500
  92.2 13.8 %all-to-all-start = ((f32[16,1,256]{2,1,0:T(1,128)}), f32[16,1,256]{2,1,0:T(1,128)S(1)}, u32[]{:S(2)}, u32[]{:S(2)}) async-start(f32[16,1,256]{2,1,0:T(1,128)} %copy.15), calls=%async_computation | async-start | bytes 32768 | tf_op jit(solution)/shard_map/all_to_all | solution.py:516
  100.4 33.8 %collective-permute-start.5 = (bf16[16,128,128]{2,1,0:T(8,128)(2,1)}, bf16[16,128,128]{2,1,0:T(8,128)(2,1)S(1)}, u32[]{:S(2)}, u32[]{:S(2)}) collective-permute-start(bf16[16,128,128]{2,1,0:T(8,128)(2,1)} %get-tuple-element.34), channel_id=1, source_target_pairs={{0,64},{16,80},{32,96},{48,112},{64,0},{80,16},{96,32},{112,48},{1... | collective-permute-start | bytes 1572872 | tf_op jit(solution)/shard_map/ppermute | solution.py:25
  103.6 3.0 %copy-start.1 = (bf16[2,24,128,128]{3,2,1,0:T(8,128)(2,1)}, bf16[2,24,128,128]{3,2,1,0:T(8,128)(2,1)S(1)}, u32[]{:S(2)}) copy-start(bf16[2,24,128,128]{3,2,1,0:T(8,128)(2,1)S(1)} %collective-permute-done.1.refs_1_) | copy-start | bytes 4718596
  103.6 30.6 %collective-permute-start.4 = (bf16[8,128,128]{2,1,0:T(8,128)(2,1)}, bf16[8,128,128]{2,1,0:T(8,128)(2,1)S(1)}, u32[]{:S(2)}, u32[]{:S(2)}) collective-permute-start(bf16[8,128,128]{2,1,0:T(8,128)(2,1)} %get-tuple-element.32.refs_4_), channel_id=1, source_target_pairs={{0,8},{1,9},{2,10},{3,11},{4,12},{5,13},{6,14},{7,15},{8,0},{9,1},... | collective-permute-start | bytes 786440 | tf_op jit(solution)/shard_map/ppermute | solution.py:25
  113.5 20.1 %all-to-all-start.1 = ((f32[128,1,256]{2,1,0:T(1,128)}), f32[128,1,256]{2,1,0:T(1,128)S(1)}, u32[]{:S(2)}, u32[]{:S(2)}) async-start(f32[128,1,256]{2,1,0:T(1,128)} %copy.16), calls=%async_computation.1 | async-start | bytes 262144 | tf_op jit(solution)/shard_map/all_to_all | solution.py:527
  128.7 1.0 copy-start.2
  134.3 0.7 copy-start.9
  134.3 0.9 copy-start.8
  138.7 5.0 %copy-start.6 = (bf16[24,128,128]{2,1,0:T(8,128)(2,1)S(1)}, bf16[24,128,128]{2,1,0:T(8,128)(2,1)}, u32[]{:S(2)}) copy-start(bf16[24,128,128]{2,1,0:T(8,128)(2,1)} %get-tuple-element.33._) | copy-start | bytes 2359300
  138.7 7.6 %copy-start.7 = (bf16[16,128,128]{2,1,0:T(8,128)(2,1)S(1)}, bf16[16,128,128]{2,1,0:T(8,128)(2,1)}, u32[]{:S(2)}) copy-start(bf16[16,128,128]{2,1,0:T(8,128)(2,1)} %get-tuple-element.35.refs_8_) | copy-start | bytes 1572868
  140.9 10.4 %collective-permute-start.8 = (bf16[4,128,256]{2,1,0:T(8,128)(2,1)}, bf16[4,128,256]{2,1,0:T(8,128)(2,1)}, u32[]{:S(2)}, u32[]{:S(2)}) collective-permute-start(bf16[4,128,256]{2,1,0:T(8,128)(2,1)} %join_features.1.refs_8_), channel_id=1, source_target_pairs={{0,1},{1,2},{2,3},{3,0},{4,5},{5,6},{6,7},{7,4},{8,9},{9,10},{10,1... | collective-permute-start | bytes 786440 | tf_op jit(solution)/shard_map/ppermute | solution.py:551
  141.5 14.4 %collective-permute-start.9 = (bf16[4,128,256]{2,1,0:T(8,128)(2,1)}, bf16[4,128,256]{2,1,0:T(8,128)(2,1)}, u32[]{:S(2)}, u32[]{:S(2)}) collective-permute-start(bf16[4,128,256]{2,1,0:T(8,128)(2,1)} %join_features.1.refs_8_), channel_id=1, source_target_pairs={{0,2},{1,3},{2,0},{3,1},{4,6},{5,7},{6,4},{7,5},{8,10},{9,11},{10,... | collective-permute-start | bytes 786440 | tf_op jit(solution)/shard_map/ppermute | solution.py:551
  143.7 21.9 %collective-permute-start.13 = (bf16[24,128,128]{2,1,0:T(8,128)(2,1)S(1)}, bf16[24,128,128]{2,1,0:T(8,128)(2,1)S(1)}, u32[]{:S(2)}, u32[]{:S(2)}) collective-permute-start(bf16[24,128,128]{2,1,0:T(8,128)(2,1)S(1)} %copy-done.6), channel_id=1, source_target_pairs={{0,8},{1,9},{2,10},{3,11},{4,12},{5,13},{6,14},{7,15},{8,0},{9,1},... | collective-permute-start | bytes 2359304 | tf_op jit(solution)/shard_map/ppermute | solution.py:25
  146.3 29.3 %collective-permute-start.11 = (bf16[16,128,128]{2,1,0:T(8,128)(2,1)S(1)}, bf16[16,128,128]{2,1,0:T(8,128)(2,1)}, u32[]{:S(2)}, u32[]{:S(2)}) collective-permute-start(bf16[16,128,128]{2,1,0:T(8,128)(2,1)S(1)} %copy-done.7), channel_id=1, source_target_pairs={{0,8},{1,9},{2,10},{3,11},{4,12},{5,13},{6,14},{7,15},{8,0},{9,1},... | collective-permute-start | bytes 1572872 | tf_op jit(solution)/shard_map/ppermute | solution.py:25
  147.2 22.1 %collective-permute-start.14 = (bf16[24,128,128]{2,1,0:T(8,128)(2,1)}, bf16[24,128,128]{2,1,0:T(8,128)(2,1)S(1)}, u32[]{:S(2)}, u32[]{:S(2)}) collective-permute-start(bf16[24,128,128]{2,1,0:T(8,128)(2,1)} %get-tuple-element.37), channel_id=1, source_target_pairs={{0,64},{16,80},{32,96},{48,112},{64,0},{80,16},{96,32},{112,48},{1... | collective-permute-start | bytes 2359304 | tf_op jit(solution)/shard_map/ppermute | solution.py:25
  151.3 27.4 %collective-permute-start.12 = (bf16[16,128,128]{2,1,0:T(8,128)(2,1)}, bf16[16,128,128]{2,1,0:T(8,128)(2,1)}, u32[]{:S(2)}, u32[]{:S(2)}) collective-permute-start(bf16[16,128,128]{2,1,0:T(8,128)(2,1)} %get-tuple-element.36), channel_id=1, source_target_pairs={{0,64},{16,80},{32,96},{48,112},{64,0},{80,16},{96,32},{112,48},{1... | collective-permute-start | bytes 1572872 | tf_op jit(solution)/shard_map/ppermute | solution.py:25
  155.9 7.7 %collective-permute-start.10 = (bf16[4,128,256]{2,1,0:T(8,128)(2,1)}, bf16[4,128,256]{2,1,0:T(8,128)(2,1)S(1)}, u32[]{:S(2)}, u32[]{:S(2)}) collective-permute-start(bf16[4,128,256]{2,1,0:T(8,128)(2,1)} %join_features.1.refs_8_), channel_id=1, source_target_pairs={{0,3},{1,0},{2,1},{3,2},{4,7},{5,4},{6,5},{7,6},{8,11},{9,8},{10,9... | collective-permute-start | bytes 786440 | tf_op jit(solution)/shard_map/ppermute | solution.py:551
  163.7 11.9 %copy-start.3 = (bf16[4,4,128,256]{3,2,1,0:T(8,128)(2,1)}, bf16[4,4,128,256]{3,2,1,0:T(8,128)(2,1)S(1)}, u32[]{:S(2)}) copy-start(bf16[4,4,128,256]{3,2,1,0:T(8,128)(2,1)S(1)} %bitcast_dynamic-update-slice_fusion.refs_8_) | copy-start | bytes 3145732
  165.6 3.7 %copy-start.4 = (bf16[24,128,128]{2,1,0:T(8,128)(2,1)}, bf16[24,128,128]{2,1,0:T(8,128)(2,1)S(1)}, u32[]{:S(2)}) copy-start(bf16[24,128,128]{2,1,0:T(8,128)(2,1)S(1)} %collective-permute-done.13.refs_2_) | copy-start | bytes 2359300
  169.4 0.9 copy-start.5

commit v3 on v2

--- a/solution.py
+++ b/solution.py
@@ -16,7 +16,7 @@
 CHUNKS = (8, 16), (24, 24), (16, 16)
 BF16 = jnp.bfloat16
 F32 = jnp.float32
-PARAMS = pltpu.CompilerParams(vmem_limit_bytes=60 << 20)
+PARAMS = pltpu.CompilerParams(vmem_limit_bytes=66_500_000)
 ANYWHERE = pl.BlockSpec(memory_space=pl.ANY)
 
 
@@ -52,7 +52,7 @@
     tiles_col = col_tables.shape[0]
     coarse_nodes = partner_ref.shape[0] * HALF // 2
     rotated = (iota((1, TILE), 1) + HALF) & (TILE - 1)
-    level = iota((TILE, TILE), 0)
+    level = iota((TILE, TILE), 0).astype(F32).astype(BF16)
 
     def vector(start, shift):
         first = partner_ref[pl.ds(start, 1), :]
@@ -60,7 +60,9 @@
         return jnp.concatenate([first, second], axis=1) - shift
 
     def table(values):
-        return (jnp.broadcast_to(values, (TILE, TILE)) == level).astype(F32).astype(BF16)
+        line = values.astype(F32).astype(BF16)
+        same = jnp.broadcast_to(line, (TILE, TILE)) == level
+        return jnp.where(same, jnp.ones((), BF16), jnp.zeros((), BF16))
 
     for i in range(tiles_row):
         k = row_group * tiles_row + i
@@ -434,25 +436,17 @@
     )(lane, piece["kept"], piece["came"], weight, raw, token)
 
 
-def copy_kernel(parts, source, out, held, read_sem, write_sem):
+def copy_kernel(parts, source, out, sem):
     size = source.shape[0] // parts
 
-    def window(k):
-        return pl.ds(k * size, size)
-
-    def read(k):
-        return pltpu.make_async_copy(source.at[window(k)], held.at[window(k)], read_sem.at[k])
-
-    def write(k):
-        return pltpu.make_async_copy(held.at[window(k)], out.at[window(k)], write_sem.at[k])
+    def move(k):
+        window = pl.ds(k * size, size)
+        return pltpu.make_async_copy(source.at[window], out.at[window], sem.at[k])
 
     for k in range(parts):
-        read(k).start()
+        move(k).start()
     for k in range(parts):
-        read(k).wait()
-        write(k).start()
-    for k in range(parts):
-        write(k).wait()
+        move(k).wait()
 
 
 def copied(source):
@@ -462,12 +456,8 @@
         out_shape=jax.ShapeDtypeStruct(source.shape, source.dtype),
         in_specs=[ANYWHERE],
         out_specs=ANYWHERE,
-        scratch_shapes=[
-            pltpu.VMEM(source.shape, source.dtype),
-            pltpu.SemaphoreType.DMA((parts,)),
-            pltpu.SemaphoreType.DMA((parts,)),
-        ],
-        compiler_params=PARAMS,
+        scratch_shapes=[pltpu.SemaphoreType.DMA((parts,))],
+        compiler_params=pltpu.CompilerParams(vmem_limit_bytes=1 << 20),
         name="copied",
     )(source)
 
@@ -512,7 +502,6 @@
         pairs.append(pair)
 
     own = sum_rows([piece for pair in pairs for piece in pair], tile_index, sizes)
-    token = own
     spread = lax.all_to_all(own, "col", split_axis=0, concat_axis=0, tiled=True)
 
     targets = routes[:, 0]
@@ -520,16 +509,12 @@
     same = (targets[:, None] == targets[None, :]) & (order[None, :] < order[:, None])
     place = targets * capacity + jnp.sum(same.astype(jnp.int32), axis=1)
 
-    for chunk, pair in enumerate(pairs):
-        tokens = [token]
-        if chunk == chunks - 1:
-            lines = line_copies(spread, devices, token)
-            raw = lax.all_to_all(
-                lines, ("row", "col"), split_axis=0, concat_axis=0, tiled=True
-            )
-            buffer = zero_buffer(devices * capacity, lines)
-            tokens = [buffer]
-        given = forward(pair, tokens)
+    buffer = zero_buffer(devices * capacity, own)
+    lines = line_copies(spread, devices, buffer)
+    raw = lax.all_to_all(lines, ("row", "col"), split_axis=0, concat_axis=0, tiled=True)
+    token = lines
+    for pair in pairs:
+        given = forward(pair, [token])
         token = given[0]
         for kind in range(2):
             pair[kind]["last"] = flipped(given[kind], *masks[1 - kind])

time: 297 us -> 296 us (level)
  waiting for transfers between devices: 57.7 us -> 67.1 us
  starting transfers between devices: 45.4 us -> 39.9 us
  Pallas kernels: 74.4 us -> 70.5 us
    all_to_all x1, waiting for transfers between devices: 1.54 us -> 8.73 us  [level(): lax.all_to_all(lines, ('row', 'col'), split_axis=0, concat_axis=0, tiled=...]
    all_to_all x1, starting transfers between devices: 10.7 us -> 6.83 us  [level(): lax.all_to_all(lines, ('row', 'col'), split_axis=0, concat_axis=0, tiled=...]
    ppermute x3, waiting for transfers between devices: 9.46 us -> 6.18 us  [level(): shared = lax.ppermute(joined, 'col', ring)]
    pallas_call x1, Pallas kernels: 6.57 us -> 3.41 us  [copied(): pl.pallas_call(functools.partial(copy_kernel, parts), out_shape=jax.Shape...]
  transfers between devices with their start and end apart: 17 -> 17, of which waited for: 7 -> 8; matrix products, arithmetic and copies ran while one was open for 3% -> 3% of each run, Pallas kernels for 14% -> 14%
where the time goes in v3:
time: 296 us; the launch traced here: 294 us
  blocking collectives  105 us (35%)
  Pallas kernels  70.5 us (24%)
  waiting for transfers between devices  67.1 us (23%)
  starting transfers between devices  39.9 us (13%)
  local copies, waits for them, and re-layouts  10 us (3%)
    all_to_all x1, blocking collectives, level(): lax.all_to_all(buffer, ('row', 'col'), split_axis=0, concat_axis=0, tiled...  105 us
    ppermute x12, waiting for transfers between devices, flipped(): return lax.ppermute(value, axis, pairs)  49.3 us
    pallas_call x3, Pallas kernels, pair_tiles(): pl.pallas_call(functools.partial(pair_kernel, starts, counts, with_featur...  25.2 us
    ppermute x12, starting transfers between devices, flipped(): return lax.ppermute(value, axis, pairs)  23.7 us
    pallas_call x1, Pallas kernels, sum_rows(): pl.pallas_call(functools.partial(sum_kernel, bounds, tiles_col), out_shap...  13.3 us
    pallas_call x3, Pallas kernels, finish(): pl.pallas_call(functools.partial(finish_kernel, starts, counts), out_shap...  12.6 us
    all_to_all x1, waiting for transfers between devices, level(): lax.all_to_all(lines, ('row', 'col'), split_axis=0, concat_axis=0, tiled=...  8.73 us
    pallas_call x3, Pallas kernels, forward(): pl.pallas_call(functools.partial(forward_kernel, steps), out_shape=[jax.S...  8.56 us
  transfers between devices with their start and end apart: 17, of which 8 were waited for; matrix products, arithmetic and copies ran while one was open for 3% of the time, Pallas kernels for 14%

profile of v3, /device:TPU:32, one launch (start us, length us, event | category | flops | bytes accessed | tf_op | source)
XLA Modules:
  0.0 294.1 jit_solution(11469509579251867394)
XLA Ops:
  0.6 7.2 %pair_tiles.3 = (bf16[2,12,128,128]{3,2,1,0:T(8,128)(2,1)}, bf16[2,12,128,128]{3,2,1,0:T(8,128)(2,1)}, bf16[2,16,128,128]{3,2,1,0:T(8,128)(2,1)}, bf16[2,16,128,128]{3,2,1,0:T(8,128)(2,1)}) custom-call(s32[104]{0:T(128)} %index_ref.13, s32[4]{0:T(128)} %pert_ref.5, s32[1]{0:T(128)} %bitcast.lane_ref, bf16[104,256,256]{2,1,0:T(8,128)(2,1)} %tiles.5, ...), custom_call_target="tpu_custom_call" | custom-call | tf_op jit(solution)/shard_map/pair_tiles/pallas_call | solution.py:178
  7.8 10.3 %pair_tiles.4 = (bf16[2,24,128,128]{3,2,1,0:T(8,128)(2,1)}, bf16[2,24,128,128]{3,2,1,0:T(8,128)(2,1)}, bf16[2,24,128,128]{3,2,1,0:T(8,128)(2,1)}, bf16[2,24,128,128]{3,2,1,0:T(8,128)(2,1)}) custom-call(s32[104]{0:T(128)} %index_ref.13, s32[4]{0:T(128)} %pert_ref.5, s32[1]{0:T(128)} %bitcast.lane_ref, bf16[104,256,256]{2,1,0:T(8,128)(2,1)} %tiles.5, ...), custom_call_target="tpu_custom_call" | custom-call | tf_op jit(solution)/shard_map/pair_tiles/pallas_call | solution.py:178
  18.2 3.0 %collective-permute-start.6 = (bf16[2,24,128,128]{3,2,1,0:T(8,128)(2,1)}, bf16[2,24,128,128]{3,2,1,0:T(8,128)(2,1)}, u32[]{:S(2)}, u32[]{:S(2)}) collective-permute-start(bf16[2,24,128,128]{3,2,1,0:T(8,128)(2,1)} %get-tuple-element.24.rest_4_), channel_id=1, source_target_pairs={{0,64},{16,80},{32,96},{48,112},{64,0},{80,16},{96,32},{112,48},{1... | collective-permute-start | bytes 4718600 | tf_op jit(solution)/shard_map/ppermute | solution.py:25
  21.2 0.5 collective-permute-start
  21.7 3.0 %collective-permute-start.1 = (bf16[2,16,128,128]{3,2,1,0:T(8,128)(2,1)}, bf16[2,16,128,128]{3,2,1,0:T(8,128)(2,1)}, u32[]{:S(2)}, u32[]{:S(2)}) collective-permute-start(bf16[2,16,128,128]{3,2,1,0:T(8,128)(2,1)} %get-tuple-element.22.rest_2_), channel_id=1, source_target_pairs={{0,8},{1,9},{2,10},{3,11},{4,12},{5,13},{6,14},{7,15},{8,0},{9,1},... | collective-permute-start | bytes 3145736 | tf_op jit(solution)/shard_map/ppermute | solution.py:25
  24.7 0.5 collective-permute-start.7
  25.2 7.7 %pair_tiles.5 = (bf16[2,16,128,128]{3,2,1,0:T(8,128)(2,1)}, bf16[2,16,128,128]{3,2,1,0:T(8,128)(2,1)}, bf16[2,16,128,128]{3,2,1,0:T(8,128)(2,1)}, bf16[2,16,128,128]{3,2,1,0:T(8,128)(2,1)}) custom-call(s32[104]{0:T(128)} %index_ref.13, s32[4]{0:T(128)} %pert_ref.5, s32[1]{0:T(128)} %bitcast.lane_ref, bf16[104,256,256]{2,1,0:T(8,128)(2,1)} %tiles.5, ...), custom_call_target="tpu_custom_call" | custom-call | tf_op jit(solution)/shard_map/pair_tiles/pallas_call | solution.py:178
  32.9 3.0 %collective-permute-start.4 = (bf16[2,16,128,128]{3,2,1,0:T(8,128)(2,1)}, bf16[2,16,128,128]{3,2,1,0:T(8,128)(2,1)}, u32[]{:S(2)}, u32[]{:S(2)}) collective-permute-start(bf16[2,16,128,128]{3,2,1,0:T(8,128)(2,1)} %get-tuple-element.28.rest_8_), channel_id=1, source_target_pairs={{0,64},{16,80},{32,96},{48,112},{64,0},{80,16},{96,32},{112,48},{1... | collective-permute-start | bytes 3145736 | tf_op jit(solution)/shard_map/ppermute | solution.py:25
  36.0 38.1 %collective-permute-done.refs_1_.came = bf16[2,12,128,128]{3,2,1,0:T(8,128)(2,1)} collective-permute-done((bf16[2,12,128,128]{3,2,1,0:T(8,128)(2,1)}, bf16[2,12,128,128]{3,2,1,0:T(8,128)(2,1)}, u32[]{:S(2)}, u32[]{:S(2)}) %collective-permute-start) | collective-permute-done | bytes 786464 | tf_op jit(solution)/shard_map/ppermute | solution.py:25
  74.1 3.0 %collective-permute-start.5 = (bf16[2,16,128,128]{3,2,1,0:T(8,128)(2,1)}, bf16[2,16,128,128]{3,2,1,0:T(8,128)(2,1)}, u32[]{:S(2)}, u32[]{:S(2)}) collective-permute-start(bf16[2,16,128,128]{3,2,1,0:T(8,128)(2,1)} %get-tuple-element.30.rest_10_), channel_id=1, source_target_pairs={{0,8},{1,9},{2,10},{3,11},{4,12},{5,13},{6,14},{7,15},{8,0},{9,1},... | collective-permute-start | bytes 3145736 | tf_op jit(solution)/shard_map/ppermute | solution.py:25
  77.1 13.3 %sum_rows.1._ = f32[16,256]{1,0:T(8,128)} custom-call(s32[104]{0:T(128)} %index_ref.13, bf16[2,12,128,128]{3,2,1,0:T(8,128)(2,1)} %get-tuple-element.21.rest_0_, bf16[2,12,128,128]{3,2,1,0:T(8,128)(2,1)} %get-tuple-element.20.rest_1_.refs_0_.kept, bf16[2,16,128,128]{3,2,1,0:T(8,128)(2,1)} %get-tuple-element.22.rest_2_, ...), custom_call_target="tpu_custom_call" | custom-call | tf_op jit(solution)/shard_map/sum_rows/pallas_call | solution.py:241
  90.4 1.3 copy.15
  91.8 6.0 %all-to-all-start = ((f32[16,1,256]{2,1,0:T(1,128)}), f32[16,1,256]{2,1,0:T(1,128)S(1)}, u32[]{:S(2)}, u32[]{:S(2)}) async-start(f32[16,1,256]{2,1,0:T(1,128)} %copy.15), calls=%async_computation | async-start | bytes 32768 | tf_op jit(solution)/shard_map/all_to_all | solution.py:505
  97.8 3.9 %zero_buffer.1._.refs_7_ = bf16[256,128,128]{2,1,0:T(8,128)(2,1)} custom-call(f32[16,256]{1,0:T(8,128)} %sum_rows.1._), custom_call_target="tpu_custom_call" | custom-call | tf_op jit(solution)/shard_map/zero_buffer/pallas_call | solution.py:313
  101.6 2.9 all-to-all-done
  104.6 0.6 copy.22
  105.2 1.4 line_copies.1.refs_4_
  106.6 0.0 collective-permute-done.1.refs_3_.refs_4_
  106.6 2.2 forward.3
  108.8 3.0 %collective-permute-start.3 = (bf16[16,128,128]{2,1,0:T(8,128)(2,1)}, bf16[16,128,128]{2,1,0:T(8,128)(2,1)S(1)}, u32[]{:S(2)}, u32[]{:S(2)}) collective-permute-start(bf16[16,128,128]{2,1,0:T(8,128)(2,1)} %get-tuple-element.33), channel_id=1, source_target_pairs={{0,64},{16,80},{32,96},{48,112},{64,0},{80,16},{96,32},{112,48},{1... | collective-permute-start | bytes 1572872 | tf_op jit(solution)/shard_map/ppermute | solution.py:25
  111.8 0.0 copy-done.2
  111.8 0.0 collective-permute-done.6.refs_1_
  111.8 2.6 collective-permute-start.2
  114.4 0.2 convert_reduce_fusion
  114.6 1.7 copy.16
  116.3 6.8 %all-to-all-start.1 = ((f32[128,1,256]{2,1,0:T(1,128)}), f32[128,1,256]{2,1,0:T(1,128)S(1)}, u32[]{:S(2)}, u32[]{:S(2)}) async-start(f32[128,1,256]{2,1,0:T(1,128)} %copy.16), calls=%async_computation.1 | async-start | bytes 262144 | tf_op jit(solution)/shard_map/all_to_all | solution.py:514
  123.1 0.6 multiply_add_fusion.place_ref
  123.7 8.7 %all-to-all-done.1 = f32[128,1,256]{2,1,0:T(1,128)S(1)} async-done(((f32[128,1,256]{2,1,0:T(1,128)}), f32[128,1,256]{2,1,0:T(1,128)S(1)}, u32[]{:S(2)}, u32[]{:S(2)}) %all-to-all-start.1) | async-done | bytes 131104 | tf_op jit(solution)/shard_map/all_to_all | solution.py:514
  132.4 0.7 copy.21
  133.1 0.0 collective-permute-done.7.refs_3_.refs_4_
  133.1 3.9 %forward.4 = (bf16[24,128,128]{2,1,0:T(8,128)(2,1)}, bf16[24,128,128]{2,1,0:T(8,128)(2,1)}) custom-call(bf16[2,24,128,128]{3,2,1,0:T(8,128)(2,1)} %get-tuple-element.25.rest_5_.refs_0_, bf16[2,24,128,128]{3,2,1,0:T(8,128)(2,1)} %collective-permute-done.6.refs_1_, bf16[2,24,128,128]{3,2,1,0:T(8,128)(2,1)} %get-tuple-element.27.rest_0_.rest_7_.refs_2_.refs_3_, ...), custom_call_target="tpu_custom_call" | custom-call | tf_op jit(solution)/shard_map/forward/pallas_call | solution.py:297
  137.0 0.0 collective-permute-done.4.refs_1_
  137.0 0.0 collective-permute-done.5.refs_3_.refs_4_
  137.0 2.5 forward.5
  139.4 0.0 collective-permute-done.2.refs_2_
  139.4 0.0 collective-permute-done.3.refs_5_
  139.4 0.0 copy-start.1
  139.4 0.8 copy-done.1
  140.2 3.5 %finish.3._.refs_7_ = bf16[256,128,128]{2,1,0:T(8,128)(2,1)} custom-call(s32[104]{0:T(128)} %index_ref.13, s32[104]{0:T(128)} %multiply_add_fusion.place_ref, bf16[2,12,128,128]{3,2,1,0:T(8,128)(2,1)} %get-tuple-element.20.rest_1_.refs_0_.kept, bf16[2,12,128,128]{3,2,1,0:T(8,128)(2,1)} %collective-permute-done.refs_1_.came, ...), custom_call_target="tpu_custom_call", output_to_operand_aliasing={{}: (9, {})} | custom-call | tf_op jit(solution)/shard_map/finish/pallas_call | solution.py:382
  143.8 0.0 copy-start
  143.8 2.1 join_features.1.refs_8_
  145.9 0.6 collective-permute-start.8
  146.6 1.5 collective-permute-start.9
  148.1 1.1 collective-permute-start.13
  149.1 1.2 collective-permute-start.10
  150.4 1.4 collective-permute-start.14
  151.8 1.1 broadcast_in_dim.17
  152.8 1.7 bitcast_dynamic-update-slice_fusion.3
  154.5 6.2 %collective-permute-done.8 = bf16[4,128,256]{2,1,0:T(8,128)(2,1)S(1)} collective-permute-done((bf16[4,128,256]{2,1,0:T(8,128)(2,1)}, bf16[4,128,256]{2,1,0:T(8,128)(2,1)S(1)}, u32[]{:S(2)}, u32[]{:S(2)}) %collective-permute-start.8) | collective-permute-done | bytes 262176 | tf_op jit(solution)/shard_map/ppermute | solution.py:536
  160.7 1.1 collective-permute-start.11
  161.8 0.0 collective-permute-done.9
  161.8 1.5 collective-permute-start.12
  163.2 0.7 bitcast_dynamic-update-slice_fusion.2
  164.0 0.7 bitcast_dynamic-update-slice_fusion.1
  164.7 0.0 collective-permute-done.10
  164.7 0.7 bitcast_dynamic-update-slice_fusion.refs_8_
  165.4 4.9 %collective-permute-done.13.refs_2_ = bf16[24,128,128]{2,1,0:T(8,128)(2,1)} collective-permute-done((bf16[24,128,128]{2,1,0:T(8,128)(2,1)}, bf16[24,128,128]{2,1,0:T(8,128)(2,1)}, u32[]{:S(2)}, u32[]{:S(2)}) %collective-permute-start.13) | collective-permute-done | bytes 786464 | tf_op jit(solution)/shard_map/ppermute | solution.py:25
  170.3 2.3 collective-permute-done.14.refs_5_
  172.6 5.3 %finish.4.refs_7_ = bf16[256,128,128]{2,1,0:T(8,128)(2,1)} custom-call(s32[104]{0:T(128)} %index_ref.13, s32[104]{0:T(128)} %multiply_add_fusion.place_ref, bf16[2,24,128,128]{3,2,1,0:T(8,128)(2,1)} %get-tuple-element.25.rest_5_.refs_0_, bf16[2,24,128,128]{3,2,1,0:T(8,128)(2,1)} %collective-permute-done.6.refs_1_, ...), custom_call_target="tpu_custom_call", output_to_operand_aliasing={{}: (9, {})} | custom-call | tf_op jit(solution)/shard_map/finish/pallas_call | solution.py:382
  177.9 2.2 collective-permute-done.11.refs_2_
  180.1 1.7 collective-permute-done.12.refs_5_
  181.8 3.8 %finish.5 = bf16[256,128,128]{2,1,0:T(8,128)(2,1)} custom-call(s32[104]{0:T(128)} %index_ref.13, s32[104]{0:T(128)} %multiply_add_fusion.place_ref, bf16[2,16,128,128]{3,2,1,0:T(8,128)(2,1)} %get-tuple-element.29.rest_9_.refs_0_, bf16[2,16,128,128]{3,2,1,0:T(8,128)(2,1)} %collective-permute-done.4.refs_1_, ...), custom_call_target="tpu_custom_call", output_to_operand_aliasing={{}: (9, {})} | custom-call | tf_op jit(solution)/shard_map/finish/pallas_call | solution.py:382
  185.6 104.9 %all_to_all.27.source = bf16[256,128,128]{2,1,0:T(8,128)(2,1)S(1)} all-to-all(bf16[256,128,128]{2,1,0:T(8,128)(2,1)} %finish.5), channel_id=1, replica_groups=mesh['row'=8,'col'=16] {'row','col'}, dimensions={0} | all-to-all | bytes 16777216 | tf_op jit(solution)/shard_map/all_to_all | solution.py:542
  290.5 3.4 %copied.1 = bf16[256,128,128]{2,1,0:T(8,128)(2,1)} custom-call(bf16[256,128,128]{2,1,0:T(8,128)(2,1)S(1)} %all_to_all.27.source), custom_call_target="tpu_custom_call" | custom-call | tf_op jit(solution)/shard_map/copied/pallas_call | solution.py:454
  (3 shorter events, 0.0 us)
Async XLA Ops:
  18.2 93.6 %collective-permute-start.6 = (bf16[2,24,128,128]{3,2,1,0:T(8,128)(2,1)}, bf16[2,24,128,128]{3,2,1,0:T(8,128)(2,1)}, u32[]{:S(2)}, u32[]{:S(2)}) collective-permute-start(bf16[2,24,128,128]{3,2,1,0:T(8,128)(2,1)} %get-tuple-element.24.rest_4_), channel_id=1, source_target_pairs={{0,64},{16,80},{32,96},{48,112},{64,0},{80,16},{96,32},{112,48},{1... | collective-permute-start | bytes 4718600 | tf_op jit(solution)/shard_map/ppermute | solution.py:25
  21.2 52.9 %collective-permute-start = (bf16[2,12,128,128]{3,2,1,0:T(8,128)(2,1)}, bf16[2,12,128,128]{3,2,1,0:T(8,128)(2,1)}, u32[]{:S(2)}, u32[]{:S(2)}) collective-permute-start(bf16[2,12,128,128]{3,2,1,0:T(8,128)(2,1)} %get-tuple-element.21.rest_0_), channel_id=1, source_target_pairs={{0,64},{16,80},{32,96},{48,112},{64,0},{80,16},{96,32},{112,48},{1... | collective-permute-start | bytes 2359304 | tf_op jit(solution)/shard_map/ppermute | solution.py:25
  21.7 84.8 %collective-permute-start.1 = (bf16[2,16,128,128]{3,2,1,0:T(8,128)(2,1)}, bf16[2,16,128,128]{3,2,1,0:T(8,128)(2,1)}, u32[]{:S(2)}, u32[]{:S(2)}) collective-permute-start(bf16[2,16,128,128]{3,2,1,0:T(8,128)(2,1)} %get-tuple-element.22.rest_2_), channel_id=1, source_target_pairs={{0,8},{1,9},{2,10},{3,11},{4,12},{5,13},{6,14},{7,15},{8,0},{9,1},... | collective-permute-start | bytes 3145736 | tf_op jit(solution)/shard_map/ppermute | solution.py:25
  24.7 108.4 %collective-permute-start.7 = (bf16[2,24,128,128]{3,2,1,0:T(8,128)(2,1)}, bf16[2,24,128,128]{3,2,1,0:T(8,128)(2,1)}, u32[]{:S(2)}, u32[]{:S(2)}) collective-permute-start(bf16[2,24,128,128]{3,2,1,0:T(8,128)(2,1)} %get-tuple-element.26.rest_6_), channel_id=1, source_target_pairs={{0,8},{1,9},{2,10},{3,11},{4,12},{5,13},{6,14},{7,15},{8,0},{9,1},... | collective-permute-start | bytes 4718600 | tf_op jit(solution)/shard_map/ppermute | solution.py:25
  32.9 104.0 %collective-permute-start.4 = (bf16[2,16,128,128]{3,2,1,0:T(8,128)(2,1)}, bf16[2,16,128,128]{3,2,1,0:T(8,128)(2,1)}, u32[]{:S(2)}, u32[]{:S(2)}) collective-permute-start(bf16[2,16,128,128]{3,2,1,0:T(8,128)(2,1)} %get-tuple-element.28.rest_8_), channel_id=1, source_target_pairs={{0,64},{16,80},{32,96},{48,112},{64,0},{80,16},{96,32},{112,48},{1... | collective-permute-start | bytes 3145736 | tf_op jit(solution)/shard_map/ppermute | solution.py:25
  74.1 62.8 %collective-permute-start.5 = (bf16[2,16,128,128]{3,2,1,0:T(8,128)(2,1)}, bf16[2,16,128,128]{3,2,1,0:T(8,128)(2,1)}, u32[]{:S(2)}, u32[]{:S(2)}) collective-permute-start(bf16[2,16,128,128]{3,2,1,0:T(8,128)(2,1)} %get-tuple-element.30.rest_10_), channel_id=1, source_target_pairs={{0,8},{1,9},{2,10},{3,11},{4,12},{5,13},{6,14},{7,15},{8,0},{9,1},... | collective-permute-start | bytes 3145736 | tf_op jit(solution)/shard_map/ppermute | solution.py:25
  91.8 12.8 %all-to-all-start = ((f32[16,1,256]{2,1,0:T(1,128)}), f32[16,1,256]{2,1,0:T(1,128)S(1)}, u32[]{:S(2)}, u32[]{:S(2)}) async-start(f32[16,1,256]{2,1,0:T(1,128)} %copy.15), calls=%async_computation | async-start | bytes 32768 | tf_op jit(solution)/shard_map/all_to_all | solution.py:505
  97.8 14.0 %copy-start.2 = (s32[104,2]{0,1:T(2,128)S(1)}, s32[104,2]{0,1:T(2,128)}, u32[]{:S(2)}) copy-start(s32[104,2]{0,1:T(2,128)} %param.15) | copy-start | bytes 2500
  108.8 30.6 %collective-permute-start.3 = (bf16[16,128,128]{2,1,0:T(8,128)(2,1)}, bf16[16,128,128]{2,1,0:T(8,128)(2,1)S(1)}, u32[]{:S(2)}, u32[]{:S(2)}) collective-permute-start(bf16[16,128,128]{2,1,0:T(8,128)(2,1)} %get-tuple-element.33), channel_id=1, source_target_pairs={{0,64},{16,80},{32,96},{48,112},{64,0},{80,16},{96,32},{112,48},{1... | collective-permute-start | bytes 1572872 | tf_op jit(solution)/shard_map/ppermute | solution.py:25
  111.8 27.6 %collective-permute-start.2 = (bf16[8,128,128]{2,1,0:T(8,128)(2,1)}, bf16[8,128,128]{2,1,0:T(8,128)(2,1)}, u32[]{:S(2)}, u32[]{:S(2)}) collective-permute-start(bf16[8,128,128]{2,1,0:T(8,128)(2,1)} %get-tuple-element.32.refs_4_), channel_id=1, source_target_pairs={{0,8},{1,9},{2,10},{3,11},{4,12},{5,13},{6,14},{7,15},{8,0},{9,1},... | collective-permute-start | bytes 786440 | tf_op jit(solution)/shard_map/ppermute | solution.py:25
  116.3 16.2 %all-to-all-start.1 = ((f32[128,1,256]{2,1,0:T(1,128)}), f32[128,1,256]{2,1,0:T(1,128)S(1)}, u32[]{:S(2)}, u32[]{:S(2)}) async-start(f32[128,1,256]{2,1,0:T(1,128)} %copy.16), calls=%async_computation.1 | async-start | bytes 262144 | tf_op jit(solution)/shard_map/all_to_all | solution.py:514
  139.4 0.8 copy-start.1
  143.8 16.9 %copy-start = (bf16[16,128,128]{2,1,0:T(8,128)(2,1)S(1)}, bf16[16,128,128]{2,1,0:T(8,128)(2,1)}, u32[]{:S(2)}) copy-start(bf16[16,128,128]{2,1,0:T(8,128)(2,1)} %get-tuple-element.35.refs_8_) | copy-start | bytes 1572868
  145.9 14.8 %collective-permute-start.8 = (bf16[4,128,256]{2,1,0:T(8,128)(2,1)}, bf16[4,128,256]{2,1,0:T(8,128)(2,1)S(1)}, u32[]{:S(2)}, u32[]{:S(2)}) collective-permute-start(bf16[4,128,256]{2,1,0:T(8,128)(2,1)} %join_features.1.refs_8_), channel_id=1, source_target_pairs={{0,1},{1,2},{2,3},{3,0},{4,5},{5,6},{6,7},{7,4},{8,9},{9,10},{10,1... | collective-permute-start | bytes 786440 | tf_op jit(solution)/shard_map/ppermute | solution.py:536
  146.6 15.2 %collective-permute-start.9 = (bf16[4,128,256]{2,1,0:T(8,128)(2,1)}, bf16[4,128,256]{2,1,0:T(8,128)(2,1)S(1)}, u32[]{:S(2)}, u32[]{:S(2)}) collective-permute-start(bf16[4,128,256]{2,1,0:T(8,128)(2,1)} %join_features.1.refs_8_), channel_id=1, source_target_pairs={{0,2},{1,3},{2,0},{3,1},{4,6},{5,7},{6,4},{7,5},{8,10},{9,11},{10,... | collective-permute-start | bytes 786440 | tf_op jit(solution)/shard_map/ppermute | solution.py:536
  148.1 22.2 %collective-permute-start.13 = (bf16[24,128,128]{2,1,0:T(8,128)(2,1)}, bf16[24,128,128]{2,1,0:T(8,128)(2,1)}, u32[]{:S(2)}, u32[]{:S(2)}) collective-permute-start(bf16[24,128,128]{2,1,0:T(8,128)(2,1)} %get-tuple-element.34.refs_4_), channel_id=1, source_target_pairs={{0,8},{1,9},{2,10},{3,11},{4,12},{5,13},{6,14},{7,15},{8,0},{9,1},... | collective-permute-start | bytes 2359304 | tf_op jit(solution)/shard_map/ppermute | solution.py:25
  149.1 15.5 %collective-permute-start.10 = (bf16[4,128,256]{2,1,0:T(8,128)(2,1)}, bf16[4,128,256]{2,1,0:T(8,128)(2,1)S(1)}, u32[]{:S(2)}, u32[]{:S(2)}) collective-permute-start(bf16[4,128,256]{2,1,0:T(8,128)(2,1)} %join_features.1.refs_8_), channel_id=1, source_target_pairs={{0,3},{1,0},{2,1},{3,2},{4,7},{5,4},{6,5},{7,6},{8,11},{9,8},{10,9... | collective-permute-start | bytes 786440 | tf_op jit(solution)/shard_map/ppermute | solution.py:536
  150.4 22.2 %collective-permute-start.14 = (bf16[24,128,128]{2,1,0:T(8,128)(2,1)}, bf16[24,128,128]{2,1,0:T(8,128)(2,1)}, u32[]{:S(2)}, u32[]{:S(2)}) collective-permute-start(bf16[24,128,128]{2,1,0:T(8,128)(2,1)} %get-tuple-element.37), channel_id=1, source_target_pairs={{0,64},{16,80},{32,96},{48,112},{64,0},{80,16},{96,32},{112,48},{1... | collective-permute-start | bytes 2359304 | tf_op jit(solution)/shard_map/ppermute | solution.py:25
  160.7 19.4 %collective-permute-start.11 = (bf16[16,128,128]{2,1,0:T(8,128)(2,1)S(1)}, bf16[16,128,128]{2,1,0:T(8,128)(2,1)}, u32[]{:S(2)}, u32[]{:S(2)}) collective-permute-start(bf16[16,128,128]{2,1,0:T(8,128)(2,1)S(1)} %copy-done), channel_id=1, source_target_pairs={{0,8},{1,9},{2,10},{3,11},{4,12},{5,13},{6,14},{7,15},{8,0},{9,1},... | collective-permute-start | bytes 1572872 | tf_op jit(solution)/shard_map/ppermute | solution.py:25
  161.8 20.1 %collective-permute-start.12 = (bf16[16,128,128]{2,1,0:T(8,128)(2,1)}, bf16[16,128,128]{2,1,0:T(8,128)(2,1)}, u32[]{:S(2)}, u32[]{:S(2)}) collective-permute-start(bf16[16,128,128]{2,1,0:T(8,128)(2,1)} %get-tuple-element.36), channel_id=1, source_target_pairs={{0,64},{16,80},{32,96},{48,112},{64,0},{80,16},{96,32},{112,48},{1... | collective-permute-start | bytes 1572872 | tf_op jit(solution)/shard_map/ppermute | solution.py:25

commit v4 on v3

--- a/solution.py
+++ b/solution.py
@@ -14,6 +14,7 @@
 LANES = 4
 ROW_FIRST = 48
 CHUNKS = (8, 16), (24, 24), (16, 16)
+SPLITS = 1, 2, 2
 BF16 = jnp.bfloat16
 F32 = jnp.float32
 PARAMS = pltpu.CompilerParams(vmem_limit_bytes=66_500_000)
@@ -269,55 +270,65 @@
     )(spread, token)
 
 
-def forward_kernel(steps, *refs):
+def forward_kernel(steps, parts, *refs):
     row_kept, row_came, col_kept, col_came = refs[:4]
-    row_given, col_given = refs[-2:]
+    row_given, col_given = refs[-2 * parts : -parts], refs[-parts:]
     step = pl.program_id(0)
+    size = HALF // parts
 
     def both(kept, came, given):
-        given[...] = (kept[0].astype(F32) + came[0].astype(F32)).astype(BF16)
+        total = (kept[0].astype(F32) + came[0].astype(F32)).astype(BF16)
+        for h in range(parts):
+            given[h][...] = total[:, h * size : (h + 1) * size]
 
     pl.when(step < steps[0])(lambda: both(row_kept, row_came, row_given))
     pl.when(step < steps[1])(lambda: both(col_kept, col_came, col_given))
 
 
-def quadrant(which, steps):
+def quadrant(which, steps, size=HALF, h=0):
     return pl.BlockSpec(
-        (1, STEP, HALF, HALF), lambda s, *_: (which, jnp.minimum(s, steps - 1), 0, 0)
+        (1, STEP, size, HALF), lambda s, *_: (which, jnp.minimum(s, steps - 1), h, 0)
     )
 
 
-def plain(steps):
-    return pl.BlockSpec((STEP, HALF, HALF), lambda s, *_: (jnp.minimum(s, steps - 1), 0, 0))
-
-
-def forward(pair, tokens):
+def plain(steps, size=HALF, h=0):
+    return pl.BlockSpec((STEP, size, HALF), lambda s, *_: (jnp.minimum(s, steps - 1), h, 0))
+
+
+def forward(pair, parts, tokens):
     steps = [piece["count"] // STEP for piece in pair]
     operands = [piece[key] for piece in pair for key in ("kept", "came")]
-    return pl.pallas_call(
-        functools.partial(forward_kernel, steps),
-        out_shape=[jax.ShapeDtypeStruct((piece["count"], HALF, HALF), BF16) for piece in pair],
+    size = HALF // parts
+    return pl.pallas_call(
+        functools.partial(forward_kernel, steps, parts),
+        out_shape=[
+            jax.ShapeDtypeStruct((piece["count"], size, HALF), BF16)
+            for piece in pair
+            for _ in range(parts)
+        ],
         grid=(max(steps),),
         in_specs=[quadrant(0, steps[k // 2]) for k in range(4)] + [ANYWHERE] * len(tokens),
-        out_specs=[plain(steps[0]), plain(steps[1])],
+        out_specs=[plain(steps[k], size) for k in range(2) for _ in range(parts)],
         compiler_params=PARAMS,
         name="forward",
     )(*operands, *tokens)
 
 
-def zero_kernel(_, out):
-    out[...] = jnp.zeros_like(out)
-
-
-def zero_buffer(count, token):
+def zero_kernel(_, *outs):
+    for out in outs:
+        out[...] = jnp.zeros_like(out)
+
+
+def zero_buffers(count, token):
+    block = pl.BlockSpec((64, HALF // 2, HALF), lambda s: (s, 0, 0))
     return pl.pallas_call(
         zero_kernel,
-        out_shape=jax.ShapeDtypeStruct((count, HALF, HALF), BF16),
+        out_shape=[jax.ShapeDtypeStruct((count, HALF // 2, HALF), BF16)] * 2,
         grid=(count // 64,),
         in_specs=[ANYWHERE],
-        out_specs=pl.BlockSpec((64, HALF, HALF), lambda s: (s, 0, 0)),
+        out_specs=[block, block],
         compiler_params=PARAMS,
-        name="zero_buffer",
+        name="zero_buffers",
     )(token)
 
 
@@ -333,10 +344,11 @@
     return jnp.broadcast_to(line, (HALF, HALF)).T
 
 
-def finish_kernel(starts, counts, index_ref, place_ref, *refs):
-    pieces, raw = (refs[0:3], refs[3:6]), refs[6]
+def finish_kernel(starts, counts, h, index_ref, place_ref, *refs):
+    total_pieces = len(starts)
+    raw = refs[3 * total_pieces]
     out, scale, row_scale, col_scale, done, sem = refs[-6:]
-    tiles_row = row_scale.shape[0]
+    tiles_row, size, _ = row_scale.shape
     tiles_col = col_scale.shape[0]
     step = pl.program_id(0)
 
@@ -345,42 +357,47 @@
         row_side, row_group, col_side, col_group = position()
         store_roots(raw, scale)
         for i in range(tiles_row):
-            row_scale[i] = upright(scale[row_side, pl.ds(row_group * tiles_row + i, 1), :])
+            column = upright(scale[row_side, pl.ds(row_group * tiles_row + i, 1), :])
+            row_scale[i] = column[h * size : (h + 1) * size]
         for j in range(tiles_col):
             line = scale[col_side, pl.ds(col_group * tiles_col + j, 1), :]
             col_scale[j] = jnp.broadcast_to(line, (8, HALF))
 
-    for number in range(2):
-        kept, came, last = pieces[number]
-        base = number * counts[0]
+    base = 0
+    for number in range(total_pieces):
+        kept, came, last = refs[3 * number : 3 * number + 3]
 
         @pl.when(step < counts[number] // STEP)
-        def _():
+        def _(kept=kept, came=came, last=last, base=base, start=starts[number]):
             for t in range(STEP):
                 m = step * STEP + t
-                n = starts[number] + m
-                i = lax.div(index_ref[n], tiles_col)
-                j = lax.rem(index_ref[n], tiles_col)
+                i = lax.div(index_ref[start + m], tiles_col)
+                j = lax.rem(index_ref[start + m], tiles_col)
                 total = kept[0, t].astype(F32) + came[0, t].astype(F32) + last[t].astype(F32)
                 done[base + m] = (total * row_scale[i] * col_scale[j, 0:1]).astype(BF16)
-                pltpu.make_async_copy(done.at[base + m], out.at[place_ref[n]], sem).start()
+                target = out.at[place_ref[start + m]]
+                pltpu.make_async_copy(done.at[base + m], target, sem).start()
+
+        base += counts[number]
 
     @pl.when(step == pl.num_programs(0) - 1)
     def _():
         pltpu.make_async_copy(done, out.at[pl.ds(0, done.shape[0])], sem).wait()
 
 
-def finish(pair, index, place, raw, buffer, sizes, token):
+def finish(pieces, h, index, place, raw, buffer, sizes, token):
     tiles_row, tiles_col = sizes
-    starts = [piece["start"] for piece in pair]
-    counts = [piece["count"] for piece in pair]
+    size = buffer.shape[1]
+    starts = [piece["start"] for piece in pieces]
+    counts = [piece["count"] for piece in pieces]
     specs, operands = [], []
-    for piece in pair:
+    for piece in pieces:
         steps = piece["count"] // STEP
-        specs += [quadrant(1, steps), quadrant(1, steps), plain(steps)]
-        operands += [piece["kept"], piece["came"], piece["last"]]
-    return pl.pallas_call(
-        functools.partial(finish_kernel, starts, counts),
+        split = len(piece["last"]) > 1
+        specs += [quadrant(1, steps, size, h)] * 2 + [plain(steps, size, 0 if split else h)]
+        operands += [piece["kept"], piece["came"], piece["last"][h if split else 0]]
+    return pl.pallas_call(
+        functools.partial(finish_kernel, starts, counts, h),
         out_shape=jax.ShapeDtypeStruct(buffer.shape, BF16),
         grid_spec=pltpu.PrefetchScalarGridSpec(
             num_scalar_prefetch=2,
@@ -389,13 +406,13 @@
             out_specs=ANYWHERE,
             scratch_shapes=[
                 pltpu.VMEM((2, raw.shape[0] // 2, HALF), F32),
-                pltpu.VMEM((tiles_row, HALF, HALF), F32),
+                pltpu.VMEM((tiles_row, size, HALF), F32),
                 pltpu.VMEM((tiles_col, 8, HALF), F32),
-                pltpu.VMEM((sum(counts), HALF, HALF), BF16),
+                pltpu.VMEM((sum(counts), size, HALF), BF16),
                 pltpu.SemaphoreType.DMA,
             ],
         ),
-        input_output_aliases={9: 0},
+        input_output_aliases={3 + len(operands): 0},
         compiler_params=PARAMS,
         name="finish",
     )(index, place, *operands, raw, buffer, token)
@@ -436,12 +453,39 @@
     )(lane, piece["kept"], piece["came"], weight, raw, token)
 
 
-def copy_kernel(parts, source, out, sem):
-    size = source.shape[0] // parts
+def assemble_kernel(*refs):
+    shared, out = refs[:LANES], refs[-1]
+    part = shared[0].shape[0]
+    lane = lax.rem(lax.axis_index("col"), LANES)
+    for shift in range(LANES):
+        owner = lax.rem(lane + LANES - shift, LANES)
+        out[pl.ds(owner * part, part)] = shared[shift][...]
+
+
+def assemble(shared, token):
+    part = shared[0].shape[0]
+    inner = shared[0].shape[1:]
+    shape = (LANES * part,) + inner
+    return pl.pallas_call(
+        assemble_kernel,
+        out_shape=jax.ShapeDtypeStruct(shape, BF16),
+        grid=(1,),
+        in_specs=[full((part,) + inner)] * LANES + [ANYWHERE],
+        out_specs=full(shape),
+        compiler_params=pltpu.CompilerParams(vmem_limit_bytes=8 << 20),
+        name="assemble",
+    )(*shared, token)
+
+
+def copy_kernel(parts, h, source, *refs):
+    out, sem = refs[-2:]
+    count = source.shape[0] // parts
+    size = source.shape[1]
 
     def move(k):
-        window = pl.ds(k * size, size)
-        return pltpu.make_async_copy(source.at[window], out.at[window], sem.at[k])
+        window = pl.ds(k * count, count)
+        target = out.at[window, pl.ds(h * size, size)]
+        return pltpu.make_async_copy(source.at[window], target, sem.at[k])
 
     for k in range(parts):
         move(k).start()
@@ -449,17 +493,20 @@
         move(k).wait()
 
 
-def copied(source):
+def copied(source, h, out):
     parts = 16
-    return pl.pallas_call(
-        functools.partial(copy_kernel, parts),
-        out_shape=jax.ShapeDtypeStruct(source.shape, source.dtype),
-        in_specs=[ANYWHERE],
+    shape = (source.shape[0], 2 * source.shape[1], source.shape[2])
+    operands = [source] if out is None else [source, out]
+    return pl.pallas_call(
+        functools.partial(copy_kernel, parts, h),
+        out_shape=jax.ShapeDtypeStruct(shape, source.dtype),
+        in_specs=[ANYWHERE] * len(operands),
         out_specs=ANYWHERE,
         scratch_shapes=[pltpu.SemaphoreType.DMA((parts,))],
+        input_output_aliases={} if out is None else {1: 0},
         compiler_params=pltpu.CompilerParams(vmem_limit_bytes=1 << 20),
         name="copied",
-    )(source)
+    )(*operands)
 
 
 def level(features, join_weight, partner, tile_index, tile_values, pert_slot, pert_values, routes):
@@ -473,7 +520,6 @@
     tiles_col = partner.shape[0] // TILE // col_count
     sizes = tiles_row, tiles_col
     capacity = routes.shape[1]
-    part = tiles_row // LANES
     chunks = len(CHUNKS)
     lane = (lax.axis_index("col") % LANES).reshape(1)
     partner = partner.reshape(-1, HALF)
@@ -509,38 +555,44 @@
     same = (targets[:, None] == targets[None, :]) & (order[None, :] < order[:, None])
     place = targets * capacity + jnp.sum(same.astype(jnp.int32), axis=1)
 
-    buffer = zero_buffer(devices * capacity, own)
-    lines = line_copies(spread, devices, buffer)
-    raw = lax.all_to_all(lines, ("row", "col"), split_axis=0, concat_axis=0, tiled=True)
-    token = lines
-    for pair in pairs:
-        given = forward(pair, [token])
+    buffers = list(zero_buffers(devices * capacity, own))
+    token = buffers[0]
+    for chunk, pair in enumerate(pairs):
+        splits = SPLITS[chunk]
+        given = forward(pair, splits, [token])
         token = given[0]
         for kind in range(2):
-            pair[kind]["last"] = flipped(given[kind], *masks[1 - kind])
-
-    def finished(chunk, buffer, token):
-        return finish(pairs[chunk], tile_index, place, raw, buffer, sizes, token)
-
-    buffer = finished(0, buffer, token)
-    joined = join_features(lane, pairs[0][0], join_weight, raw, tiles_row, buffer)
-    buffer = finished(1, buffer, joined)
-    parts = jnp.zeros((LANES, part, HALF, width), BF16)
-    for shift in range(LANES):
-        shared = joined
-        if shift > 0:
-            ring = [
-                (source, source // LANES * LANES + (source + shift) % LANES)
-                for source in range(col_count)
-            ]
-            shared = lax.ppermute(joined, "col", ring)
-        parts = lax.dynamic_update_slice(
-            parts, shared[None], ((lane[0] - shift) % LANES, 0, 0, 0)
-        )
-    buffer = finished(2, buffer, parts)
-    coarse_features = parts.reshape(tiles_row * HALF, width)
-    arrived = lax.all_to_all(buffer, ("row", "col"), split_axis=0, concat_axis=0, tiled=True)
-    return (coarse_features, copied(arrived))
+            pair[kind]["last"] = []
+            for h in range(splits):
+                last = flipped(given[kind * splits + h], *masks[1 - kind])
+                pair[kind]["last"].append(last)
+        if chunk == 0:
+            token = line_copies(spread, devices, token)
+            raw = lax.all_to_all(token, ("row", "col"), split_axis=0, concat_axis=0, tiled=True)
+
+    def finished(pieces, h, token):
+        return finish(pieces, h, tile_index, place, raw, buffers[h], sizes, token)
+
+    def delivered(h):
+        return lax.all_to_all(buffers[h], ("row", "col"), split_axis=0, concat_axis=0, tiled=True)
+
+    joined = join_features(lane, pairs[0][0], join_weight, raw, tiles_row, token)
+    shared = [joined]
+    for shift in range(1, LANES):
+        ring = [
+            (source, source // LANES * LANES + (source + shift) % LANES)
+            for source in range(col_count)
+        ]
+        shared.append(lax.ppermute(joined, "col", ring))
+    buffers[0] = finished(pairs[0] + pairs[1], 0, joined)
+    buffers[0] = finished(pairs[2], 0, joined)
+    buffers[1] = finished(pairs[0] + pairs[1] + pairs[2], 1, buffers[0])
+    first = delivered(0)
+    second = delivered(1)
+    coarse_features = assemble(shared, buffers[1]).reshape(tiles_row * HALF, width)
+    result = copied(first, 0, None)
+    result = copied(second, 1, result)
+    return (coarse_features, result)
 
 
 def solution(mesh):

time: 296 us -> 564 us (1.91)
  Pallas kernels: 70.5 us -> 326 us
  blocking collectives: 105 us -> 21.6 us
  waiting for transfers between devices: 67.1 us -> 145 us
  starting transfers between devices: 39.9 us -> 60.3 us
    pallas_call x8 -> x10, Pallas kernels: 28.4 us -> 284 us  [the longest x2 257 us: copied(): pl.pallas_call(functools.partial(copy_kernel, parts, h), out_shape=jax.Sh...]
    all_to_all x1, blocking collectives: 105 us -> 21.6 us  [level(): spread = lax.all_to_all(own, 'col', split_axis=0, concat_axis=0, tiled=True)]
    ppermute x3, waiting for transfers between devices: 6.18 us -> 54.3 us  [level(): shared.append(lax.ppermute(joined, 'col', ring))]
    ppermute x12 -> x16, waiting for transfers between devices: 49.3 us -> 82.3 us  [flipped(): return lax.ppermute(value, axis, pairs)]
    ppermute x12 -> x16, starting transfers between devices: 23.7 us -> 33.4 us  [flipped(): return lax.ppermute(value, axis, pairs)]
    all_to_all x2 -> x3, starting transfers between devices: 12.8 us -> 22.3 us  [the longest x2 14.2 us: delivered(): lax.all_to_all(buffers[h], ('row', 'col'), split_axis=0, concat_axis=0, t...]
    all_to_all x2 -> x3, waiting for transfers between devices: 11.7 us -> 8.74 us  [the longest x1 8.74 us: level(): lax.all_to_all(token, ('row', 'col'), split_axis=0, concat_axis=0, tiled=...]
  transfers between devices with their start and end apart: 17 -> 22, of which waited for: 8 -> 6; matrix products, arithmetic and copies ran while one was open for 3% -> 1% of each run, Pallas kernels for 14% -> 33%
where the time goes in v4:
time: 564 us; the launch traced here: 562 us
  Pallas kernels  326 us (58%)
  waiting for transfers between devices  145 us (26%)
  starting transfers between devices  60.3 us (11%)
  blocking collectives  21.6 us (4%)
  local copies, waits for them, and re-layouts  7.4 us (1%)
    pallas_call x2, Pallas kernels, copied(): pl.pallas_call(functools.partial(copy_kernel, parts, h), out_shape=jax.Sh...  257 us
    ppermute x16, waiting for transfers between devices, flipped(): return lax.ppermute(value, axis, pairs)  82.3 us
    ppermute x3, waiting for transfers between devices, level(): shared.append(lax.ppermute(joined, 'col', ring))  54.3 us
    ppermute x16, starting transfers between devices, flipped(): return lax.ppermute(value, axis, pairs)  33.4 us
    pallas_call x3, Pallas kernels, pair_tiles(): pl.pallas_call(functools.partial(pair_kernel, starts, counts, with_featur...  25.2 us
    all_to_all x1, blocking collectives, level(): spread = lax.all_to_all(own, 'col', split_axis=0, concat_axis=0, tiled=True)  21.6 us
    all_to_all x2, starting transfers between devices, delivered(): lax.all_to_all(buffers[h], ('row', 'col'), split_axis=0, concat_axis=0, t...  14.2 us
    pallas_call x3, Pallas kernels, finish(): pl.pallas_call(functools.partial(finish_kernel, starts, counts, h), out_s...  13.8 us
  transfers between devices with their start and end apart: 22, of which 6 were waited for; matrix products, arithmetic and copies ran while one was open for 1% of the time, Pallas kernels for 33%

profile of v4, /device:TPU:32, one launch (start us, length us, event | category | flops | bytes accessed | tf_op | source)
XLA Modules:
  0.0 562.4 jit_solution(7432636015343912395)
XLA Ops:
  0.6 7.2 %pair_tiles.3 = (bf16[2,12,128,128]{3,2,1,0:T(8,128)(2,1)}, bf16[2,12,128,128]{3,2,1,0:T(8,128)(2,1)}, bf16[2,16,128,128]{3,2,1,0:T(8,128)(2,1)}, bf16[2,16,128,128]{3,2,1,0:T(8,128)(2,1)}) custom-call(s32[104]{0:T(128)} %index_ref.13, s32[4]{0:T(128)} %pert_ref.5, s32[1]{0:T(128)} %bitcast.lane_ref, bf16[104,256,256]{2,1,0:T(8,128)(2,1)} %tiles.5, ...), custom_call_target="tpu_custom_call" | custom-call | tf_op jit(solution)/shard_map/pair_tiles/pallas_call | solution.py:179
  7.8 2.8 collective-permute-start
  10.6 10.4 %pair_tiles.4 = (bf16[2,24,128,128]{3,2,1,0:T(8,128)(2,1)}, bf16[2,24,128,128]{3,2,1,0:T(8,128)(2,1)}, bf16[2,24,128,128]{3,2,1,0:T(8,128)(2,1)}, bf16[2,24,128,128]{3,2,1,0:T(8,128)(2,1)}) custom-call(s32[104]{0:T(128)} %index_ref.13, s32[4]{0:T(128)} %pert_ref.5, s32[1]{0:T(128)} %bitcast.lane_ref, bf16[104,256,256]{2,1,0:T(8,128)(2,1)} %tiles.5, ...), custom_call_target="tpu_custom_call" | custom-call | tf_op jit(solution)/shard_map/pair_tiles/pallas_call | solution.py:179
  21.0 0.9 collective-permute-start.4
  21.9 2.8 collective-permute-start.5
  24.7 0.8 collective-permute-start.1
  25.5 7.7 %pair_tiles.5 = (bf16[2,16,128,128]{3,2,1,0:T(8,128)(2,1)}, bf16[2,16,128,128]{3,2,1,0:T(8,128)(2,1)}, bf16[2,16,128,128]{3,2,1,0:T(8,128)(2,1)}, bf16[2,16,128,128]{3,2,1,0:T(8,128)(2,1)}) custom-call(s32[104]{0:T(128)} %index_ref.13, s32[4]{0:T(128)} %pert_ref.5, s32[1]{0:T(128)} %bitcast.lane_ref, bf16[104,256,256]{2,1,0:T(8,128)(2,1)} %tiles.5, ...), custom_call_target="tpu_custom_call" | custom-call | tf_op jit(solution)/shard_map/pair_tiles/pallas_call | solution.py:179
  33.2 2.6 collective-permute-start.2
  35.7 0.0 collective-permute-done.refs_1_.came
  35.7 3.5 collective-permute-start.3
  39.2 13.3 %sum_rows.1._ = f32[16,256]{1,0:T(8,128)} custom-call(s32[104]{0:T(128)} %index_ref.13, bf16[2,12,128,128]{3,2,1,0:T(8,128)(2,1)} %get-tuple-element.27.rest_0_, bf16[2,12,128,128]{3,2,1,0:T(8,128)(2,1)} %get-tuple-element.26.rest_1_.refs_0_.kept, bf16[2,16,128,128]{3,2,1,0:T(8,128)(2,1)} %get-tuple-element.28.rest_2_, ...), custom_call_target="tpu_custom_call" | custom-call | tf_op jit(solution)/shard_map/sum_rows/pallas_call | solution.py:242
  52.5 3.9 zero_buffers.1
  56.4 27.1 %collective-permute-done.1.refs_3_.refs_4_ = bf16[2,16,128,128]{3,2,1,0:T(8,128)(2,1)} collective-permute-done((bf16[2,16,128,128]{3,2,1,0:T(8,128)(2,1)}, bf16[2,16,128,128]{3,2,1,0:T(8,128)(2,1)}, u32[]{:S(2)}, u32[]{:S(2)}) %collective-permute-start.1) | collective-permute-done | bytes 1048608 | tf_op jit(solution)/shard_map/ppermute | solution.py:26
  83.5 2.2 forward.3
  85.7 2.8 collective-permute-start.9
  88.6 21.6 %all_to_all.32 = f32[16,1,256]{2,1,0:T(1,128)S(1)} all-to-all(f32[16,1,256]{2,1,0:T(1,128)S(1)} %copy.16), channel_id=1, replica_groups=mesh['row'=8,'col'=16] {'col'}, dimensions={0} | all-to-all | bytes 32768 | tf_op jit(solution)/shard_map/all_to_all | solution.py:551
  110.2 0.6 copy.23
  110.8 1.4 line_copies.1.refs_4_
  112.1 0.0 collective-permute-done.4.refs_1_.refs_7_
  112.1 3.0 collective-permute-start.10
  115.2 0.0 collective-permute-done.5.refs_3_.refs_10_
  115.2 3.8 forward.4
  119.0 0.5 collective-permute-start.18
  119.5 0.0 collective-permute-done.2.refs_1_.refs_13_
  119.5 2.5 collective-permute-start.17
  122.1 2.5 forward.5
  124.6 3.1 collective-permute-start.16
  127.7 0.0 collective-permute-done.9.refs_2_
  127.7 1.0 collective-permute-start.15
  128.7 0.2 convert_reduce_fusion
  128.8 1.7 copy.17
  130.5 8.1 %all-to-all-start.1 = ((f32[128,1,256]{2,1,0:T(1,128)}), f32[128,1,256]{2,1,0:T(1,128)S(1)}, u32[]{:S(2)}, u32[]{:S(2)}) async-start(f32[128,1,256]{2,1,0:T(1,128)} %copy.17), calls=%async_computation.1 | async-start | bytes 262144 | tf_op jit(solution)/shard_map/all_to_all | solution.py:571
  138.7 0.6 multiply_add_fusion.place_ref
  139.3 8.7 %all-to-all-done.1 = f32[128,1,256]{2,1,0:T(1,128)S(1)} async-done(((f32[128,1,256]{2,1,0:T(1,128)}), f32[128,1,256]{2,1,0:T(1,128)S(1)}, u32[]{:S(2)}, u32[]{:S(2)}) %all-to-all-start.1) | async-done | bytes 131104 | tf_op jit(solution)/shard_map/all_to_all | solution.py:571
  148.0 0.7 copy.22
  148.7 2.1 join_features.1.refs_14_.refs_8_.refs_0_
  150.7 0.0 collective-permute-done.17.refs_8_
  150.8 0.8 copy-done.2
  151.5 5.0 finish.3.refs_7_
  156.6 0.0 collective-permute-done.16.refs_5_
  156.6 3.2 finish.4.refs_20_
  159.8 6.1 %all-to-all-start.3 = ((bf16[256,64,128]{2,1,0:T(8,128)(2,1)}), bf16[256,64,128]{2,1,0:T(8,128)(2,1)}, u32[]{:S(2)}, u32[]{:S(2)}) async-start(bf16[256,64,128]{2,1,0:T(8,128)(2,1)} %finish.4.refs_20_), calls=%async_computation.3 | async-start | bytes 8388608 | tf_op jit(solution)/shard_map/all_to_all | solution.py:577
  166.0 2.7 collective-permute-start.11
  168.7 3.0 collective-permute-start.12
  171.7 0.9 collective-permute-start.13
  172.6 0.5 collective-permute-start.14
  173.2 55.2 %collective-permute-done.13.refs_14_ = bf16[16,64,128]{2,1,0:T(8,128)(2,1)S(1)} collective-permute-done((bf16[16,64,128]{2,1,0:T(8,128)(2,1)S(1)}, bf16[16,64,128]{2,1,0:T(8,128)(2,1)S(1)}, u32[]{:S(2)}, u32[]{:S(2)}) %collective-permute-start.13) | collective-permute-done | bytes 262176 | tf_op jit(solution)/shard_map/ppermute | solution.py:26
  228.3 0.7 copy-done.4
  229.0 0.0 collective-permute-done.12.refs_11_
  229.0 0.1 copy-done.5
  229.2 0.6 copy-done.3
  229.8 5.5 finish.5.refs_4_
  235.3 0.0 all-to-all-done.3.source
  235.3 8.0 %all-to-all-start.2 = ((bf16[256,64,128]{2,1,0:T(8,128)(2,1)}), bf16[256,64,128]{2,1,0:T(8,128)(2,1)}, u32[]{:S(2)}, u32[]{:S(2)}) async-start(bf16[256,64,128]{2,1,0:T(8,128)(2,1)} %finish.5.refs_4_), calls=%async_computation.2 | async-start | bytes 8388608 | tf_op jit(solution)/shard_map/all_to_all | solution.py:577
  243.4 2.9 collective-permute-start.8
  246.3 0.7 collective-permute-start.7
  247.1 0.9 collective-permute-start.6
  248.0 47.9 %collective-permute-done.8.refs_3_ = bf16[4,128,256]{2,1,0:T(8,128)(2,1)S(1)} collective-permute-done((bf16[4,128,256]{2,1,0:T(8,128)(2,1)S(1)}, bf16[4,128,256]{2,1,0:T(8,128)(2,1)S(1)}, u32[]{:S(2)}, u32[]{:S(2)}) %collective-permute-start.8) | collective-permute-done | bytes 262176 | tf_op jit(solution)/shard_map/ppermute | solution.py:586
  295.9 2.3 collective-permute-done.7.refs_2_
  298.2 4.2 collective-permute-done.6.refs_1_
  302.3 2.2 copy-done
  304.5 1.1 assemble.1
  305.6 128.3 %copied.2.refs_0_ = bf16[256,128,128]{2,1,0:T(8,128)(2,1)} custom-call(bf16[256,64,128]{2,1,0:T(8,128)(2,1)} %all-to-all-done.3.source), custom_call_target="tpu_custom_call" | custom-call | tf_op jit(solution)/shard_map/copied/pallas_call | solution.py:500
  433.9 128.3 %copied.3 = bf16[256,128,128]{2,1,0:T(8,128)(2,1)} custom-call(bf16[256,64,128]{2,1,0:T(8,128)(2,1)} %all-to-all-done.2.source, bf16[256,128,128]{2,1,0:T(8,128)(2,1)} %copied.2.refs_0_), custom_call_target="tpu_custom_call", output_to_operand_aliasing={{}: (1, {})} | custom-call | tf_op jit(solution)/shard_map/copied/pallas_call | solution.py:500
  (28 shorter events, 0.1 us)
Async XLA Ops:
  7.8 27.9 %collective-permute-start = (bf16[2,12,128,128]{3,2,1,0:T(8,128)(2,1)}, bf16[2,12,128,128]{3,2,1,0:T(8,128)(2,1)}, u32[]{:S(2)}, u32[]{:S(2)}) collective-permute-start(bf16[2,12,128,128]{3,2,1,0:T(8,128)(2,1)} %get-tuple-element.27.rest_0_), channel_id=1, source_target_pairs={{0,64},{16,80},{32,96},{48,112},{64,0},{80,16},{96,32},{112,48},{1... | collective-permute-start | bytes 2359304 | tf_op jit(solution)/shard_map/ppermute | solution.py:26
  21.0 91.1 %collective-permute-start.4 = (bf16[2,24,128,128]{3,2,1,0:T(8,128)(2,1)}, bf16[2,24,128,128]{3,2,1,0:T(8,128)(2,1)}, u32[]{:S(2)}, u32[]{:S(2)}) collective-permute-start(bf16[2,24,128,128]{3,2,1,0:T(8,128)(2,1)} %get-tuple-element.30.rest_4_), channel_id=1, source_target_pairs={{0,64},{16,80},{32,96},{48,112},{64,0},{80,16},{96,32},{112,48},{1... | collective-permute-start | bytes 4718600 | tf_op jit(solution)/shard_map/ppermute | solution.py:26
  21.9 93.2 %collective-permute-start.5 = (bf16[2,24,128,128]{3,2,1,0:T(8,128)(2,1)}, bf16[2,24,128,128]{3,2,1,0:T(8,128)(2,1)}, u32[]{:S(2)}, u32[]{:S(2)}) collective-permute-start(bf16[2,24,128,128]{3,2,1,0:T(8,128)(2,1)} %get-tuple-element.32.rest_6_), channel_id=1, source_target_pairs={{0,8},{1,9},{2,10},{3,11},{4,12},{5,13},{6,14},{7,15},{8,0},{9,1},... | collective-permute-start | bytes 4718600 | tf_op jit(solution)/shard_map/ppermute | solution.py:26
  24.7 58.8 %collective-permute-start.1 = (bf16[2,16,128,128]{3,2,1,0:T(8,128)(2,1)}, bf16[2,16,128,128]{3,2,1,0:T(8,128)(2,1)}, u32[]{:S(2)}, u32[]{:S(2)}) collective-permute-start(bf16[2,16,128,128]{3,2,1,0:T(8,128)(2,1)} %get-tuple-element.28.rest_2_), channel_id=1, source_target_pairs={{0,8},{1,9},{2,10},{3,11},{4,12},{5,13},{6,14},{7,15},{8,0},{9,1},... | collective-permute-start | bytes 3145736 | tf_op jit(solution)/shard_map/ppermute | solution.py:26
  33.2 86.4 %collective-permute-start.2 = (bf16[2,16,128,128]{3,2,1,0:T(8,128)(2,1)}, bf16[2,16,128,128]{3,2,1,0:T(8,128)(2,1)}, u32[]{:S(2)}, u32[]{:S(2)}) collective-permute-start(bf16[2,16,128,128]{3,2,1,0:T(8,128)(2,1)} %get-tuple-element.34.rest_8_), channel_id=1, source_target_pairs={{0,64},{16,80},{32,96},{48,112},{64,0},{80,16},{96,32},{112,48},{1... | collective-permute-start | bytes 3145736 | tf_op jit(solution)/shard_map/ppermute | solution.py:26
  35.7 86.4 %collective-permute-start.3 = (bf16[2,16,128,128]{3,2,1,0:T(8,128)(2,1)}, bf16[2,16,128,128]{3,2,1,0:T(8,128)(2,1)}, u32[]{:S(2)}, u32[]{:S(2)}) collective-permute-start(bf16[2,16,128,128]{3,2,1,0:T(8,128)(2,1)} %get-tuple-element.36.rest_10_), channel_id=1, source_target_pairs={{0,8},{1,9},{2,10},{3,11},{4,12},{5,13},{6,14},{7,15},{8,0},{9,1},... | collective-permute-start | bytes 3145736 | tf_op jit(solution)/shard_map/ppermute | solution.py:26
  52.5 36.0 %copy-start.6 = (f32[16,256]{1,0:T(8,128)S(1)}, f32[16,256]{1,0:T(8,128)}, u32[]{:S(2)}) copy-start(f32[16,256]{1,0:T(8,128)} %sum_rows.1._) | copy-start | bytes 49156
  85.7 36.4 %copy-start.11 = (s32[104,2]{0,1:T(2,128)S(1)}, s32[104,2]{0,1:T(2,128)}, u32[]{:S(2)}) copy-start(s32[104,2]{0,1:T(2,128)} %param.15) | copy-start | bytes 2500
  85.7 42.0 %collective-permute-start.9 = (bf16[8,128,128]{2,1,0:T(8,128)(2,1)}, bf16[8,128,128]{2,1,0:T(8,128)(2,1)}, u32[]{:S(2)}, u32[]{:S(2)}) collective-permute-start(bf16[8,128,128]{2,1,0:T(8,128)(2,1)} %get-tuple-element.39._), channel_id=1, source_target_pairs={{0,8},{1,9},{2,10},{3,11},{4,12},{5,13},{6,14},{7,15},{8,0},{9,1},... | collective-permute-start | bytes 786440 | tf_op jit(solution)/shard_map/ppermute | solution.py:26
  112.1 38.6 %collective-permute-start.10 = (bf16[16,128,128]{2,1,0:T(8,128)(2,1)}, bf16[16,128,128]{2,1,0:T(8,128)(2,1)S(1)}, u32[]{:S(2)}, u32[]{:S(2)}) collective-permute-start(bf16[16,128,128]{2,1,0:T(8,128)(2,1)} %get-tuple-element.42), channel_id=1, source_target_pairs={{0,64},{16,80},{32,96},{48,112},{64,0},{80,16},{96,32},{112,48},{1... | collective-permute-start | bytes 1572872 | tf_op jit(solution)/shard_map/ppermute | solution.py:26
  119.0 31.7 %collective-permute-start.18 = (bf16[24,64,128]{2,1,0:T(8,128)(2,1)}, bf16[24,64,128]{2,1,0:T(8,128)(2,1)}, u32[]{:S(2)}, u32[]{:S(2)}) collective-permute-start(bf16[24,64,128]{2,1,0:T(8,128)(2,1)} %get-tuple-element.49), channel_id=1, source_target_pairs={{0,64},{16,80},{32,96},{48,112},{64,0},{80,16},{96,32},{112,48},{1... | collective-permute-start | bytes 1179656 | tf_op jit(solution)/shard_map/ppermute | solution.py:26
  119.5 31.2 %collective-permute-start.17 = (bf16[24,64,128]{2,1,0:T(8,128)(2,1)}, bf16[24,64,128]{2,1,0:T(8,128)(2,1)}, u32[]{:S(2)}, u32[]{:S(2)}) collective-permute-start(bf16[24,64,128]{2,1,0:T(8,128)(2,1)} %get-tuple-element.40.refs_4_), channel_id=1, source_target_pairs={{0,8},{1,9},{2,10},{3,11},{4,12},{5,13},{6,14},{7,15},{8,0},{9,1},... | collective-permute-start | bytes 1179656 | tf_op jit(solution)/shard_map/ppermute | solution.py:26
  124.6 31.9 %collective-permute-start.16 = (bf16[16,64,128]{2,1,0:T(8,128)(2,1)}, bf16[16,64,128]{2,1,0:T(8,128)(2,1)}, u32[]{:S(2)}, u32[]{:S(2)}) collective-permute-start(bf16[16,64,128]{2,1,0:T(8,128)(2,1)} %get-tuple-element.48), channel_id=1, source_target_pairs={{0,64},{16,80},{32,96},{48,112},{64,0},{80,16},{96,32},{112,48},{1... | collective-permute-start | bytes 786440 | tf_op jit(solution)/shard_map/ppermute | solution.py:26
  127.7 28.9 %collective-permute-start.15 = (bf16[16,64,128]{2,1,0:T(8,128)(2,1)}, bf16[16,64,128]{2,1,0:T(8,128)(2,1)}, u32[]{:S(2)}, u32[]{:S(2)}) collective-permute-start(bf16[16,64,128]{2,1,0:T(8,128)(2,1)} %get-tuple-element.41._), channel_id=1, source_target_pairs={{0,8},{1,9},{2,10},{3,11},{4,12},{5,13},{6,14},{7,15},{8,0},{9,1},... | collective-permute-start | bytes 786440 | tf_op jit(solution)/shard_map/ppermute | solution.py:26
  130.5 17.5 %all-to-all-start.1 = ((f32[128,1,256]{2,1,0:T(1,128)}), f32[128,1,256]{2,1,0:T(1,128)S(1)}, u32[]{:S(2)}, u32[]{:S(2)}) async-start(f32[128,1,256]{2,1,0:T(1,128)} %copy.17), calls=%async_computation.1 | async-start | bytes 262144 | tf_op jit(solution)/shard_map/all_to_all | solution.py:571
  150.7 0.8 copy-start.2
  159.8 6.2 %copy-start.8 = (bf16[24,64,128]{2,1,0:T(8,128)(2,1)S(1)}, bf16[24,64,128]{2,1,0:T(8,128)(2,1)}, u32[]{:S(2)}) copy-start(bf16[24,64,128]{2,1,0:T(8,128)(2,1)} %get-tuple-element.43) | copy-start | bytes 1179652
  159.8 8.9 %copy-start.7 = (bf16[24,64,128]{2,1,0:T(8,128)(2,1)S(1)}, bf16[24,64,128]{2,1,0:T(8,128)(2,1)}, u32[]{:S(2)}) copy-start(bf16[24,64,128]{2,1,0:T(8,128)(2,1)} %get-tuple-element.44) | copy-start | bytes 1179652
  159.8 11.9 %copy-start.10 = (bf16[16,64,128]{2,1,0:T(8,128)(2,1)S(1)}, bf16[16,64,128]{2,1,0:T(8,128)(2,1)}, u32[]{:S(2)}) copy-start(bf16[16,64,128]{2,1,0:T(8,128)(2,1)} %get-tuple-element.45) | copy-start | bytes 786436
  159.8 12.8 %copy-start.9 = (bf16[16,64,128]{2,1,0:T(8,128)(2,1)S(1)}, bf16[16,64,128]{2,1,0:T(8,128)(2,1)}, u32[]{:S(2)}) copy-start(bf16[16,64,128]{2,1,0:T(8,128)(2,1)} %get-tuple-element.46) | copy-start | bytes 786436
  159.8 75.5 %all-to-all-start.3 = ((bf16[256,64,128]{2,1,0:T(8,128)(2,1)}), bf16[256,64,128]{2,1,0:T(8,128)(2,1)}, u32[]{:S(2)}, u32[]{:S(2)}) async-start(bf16[256,64,128]{2,1,0:T(8,128)(2,1)} %finish.4.refs_20_), calls=%async_computation.3 | async-start | bytes 8388608 | tf_op jit(solution)/shard_map/all_to_all | solution.py:577
  166.0 62.3 %collective-permute-start.11 = (bf16[24,64,128]{2,1,0:T(8,128)(2,1)S(1)}, bf16[24,64,128]{2,1,0:T(8,128)(2,1)S(1)}, u32[]{:S(2)}, u32[]{:S(2)}) collective-permute-start(bf16[24,64,128]{2,1,0:T(8,128)(2,1)S(1)} %copy-done.8), channel_id=1, source_target_pairs={{0,8},{1,9},{2,10},{3,11},{4,12},{5,13},{6,14},{7,15},{8,0},{9,1},... | collective-permute-start | bytes 1179656 | tf_op jit(solution)/shard_map/ppermute | solution.py:26
  168.7 60.3 %collective-permute-start.12 = (bf16[24,64,128]{2,1,0:T(8,128)(2,1)S(1)}, bf16[24,64,128]{2,1,0:T(8,128)(2,1)}, u32[]{:S(2)}, u32[]{:S(2)}) collective-permute-start(bf16[24,64,128]{2,1,0:T(8,128)(2,1)S(1)} %copy-done.7), channel_id=1, source_target_pairs={{0,64},{16,80},{32,96},{48,112},{64,0},{80,16},{96,32},{112,48},{1... | collective-permute-start | bytes 1179656 | tf_op jit(solution)/shard_map/ppermute | solution.py:26
  171.7 56.6 %collective-permute-start.13 = (bf16[16,64,128]{2,1,0:T(8,128)(2,1)S(1)}, bf16[16,64,128]{2,1,0:T(8,128)(2,1)S(1)}, u32[]{:S(2)}, u32[]{:S(2)}) collective-permute-start(bf16[16,64,128]{2,1,0:T(8,128)(2,1)S(1)} %copy-done.10), channel_id=1, source_target_pairs={{0,8},{1,9},{2,10},{3,11},{4,12},{5,13},{6,14},{7,15},{8,0},{9,1},... | collective-permute-start | bytes 786440 | tf_op jit(solution)/shard_map/ppermute | solution.py:26
  172.6 55.7 %collective-permute-start.14 = (bf16[16,64,128]{2,1,0:T(8,128)(2,1)S(1)}, bf16[16,64,128]{2,1,0:T(8,128)(2,1)S(1)}, u32[]{:S(2)}, u32[]{:S(2)}) collective-permute-start(bf16[16,64,128]{2,1,0:T(8,128)(2,1)S(1)} %copy-done.9), channel_id=1, source_target_pairs={{0,64},{16,80},{32,96},{48,112},{64,0},{80,16},{96,32},{112,48},{1... | collective-permute-start | bytes 786440 | tf_op jit(solution)/shard_map/ppermute | solution.py:26
  228.3 0.7 copy-start.4
  228.3 0.8 copy-start.5
  229.0 0.7 copy-start.3
  235.3 8.1 %copy-start.1 = (bf16[4,128,256]{2,1,0:T(8,128)(2,1)S(1)}, bf16[4,128,256]{2,1,0:T(8,128)(2,1)}, u32[]{:S(2)}) copy-start(bf16[4,128,256]{2,1,0:T(8,128)(2,1)} %join_features.1.refs_14_.refs_8_.refs_0_) | copy-start | bytes 786436
  235.3 198.6 %all-to-all-start.2 = ((bf16[256,64,128]{2,1,0:T(8,128)(2,1)}), bf16[256,64,128]{2,1,0:T(8,128)(2,1)}, u32[]{:S(2)}, u32[]{:S(2)}) async-start(bf16[256,64,128]{2,1,0:T(8,128)(2,1)} %finish.5.refs_4_), calls=%async_computation.2 | async-start | bytes 8388608 | tf_op jit(solution)/shard_map/all_to_all | solution.py:577
  243.4 52.5 %collective-permute-start.8 = (bf16[4,128,256]{2,1,0:T(8,128)(2,1)S(1)}, bf16[4,128,256]{2,1,0:T(8,128)(2,1)S(1)}, u32[]{:S(2)}, u32[]{:S(2)}) collective-permute-start(bf16[4,128,256]{2,1,0:T(8,128)(2,1)S(1)} %copy-done.1), channel_id=1, source_target_pairs={{0,3},{1,0},{2,1},{3,2},{4,7},{5,4},{6,5},{7,6},{8,11},{9,8},{10,9... | collective-permute-start | bytes 786440 | tf_op jit(solution)/shard_map/ppermute | solution.py:586
  246.3 51.8 %collective-permute-start.7 = (bf16[4,128,256]{2,1,0:T(8,128)(2,1)S(1)}, bf16[4,128,256]{2,1,0:T(8,128)(2,1)S(1)}, u32[]{:S(2)}, u32[]{:S(2)}) collective-permute-start(bf16[4,128,256]{2,1,0:T(8,128)(2,1)S(1)} %copy-done.1), channel_id=1, source_target_pairs={{0,2},{1,3},{2,0},{3,1},{4,6},{5,7},{6,4},{7,5},{8,10},{9,11},{10,... | collective-permute-start | bytes 786440 | tf_op jit(solution)/shard_map/ppermute | solution.py:586
  247.1 55.3 %collective-permute-start.6 = (bf16[4,128,256]{2,1,0:T(8,128)(2,1)S(1)}, bf16[4,128,256]{2,1,0:T(8,128)(2,1)S(1)}, u32[]{:S(2)}, u32[]{:S(2)}) collective-permute-start(bf16[4,128,256]{2,1,0:T(8,128)(2,1)S(1)} %copy-done.1), channel_id=1, source_target_pairs={{0,1},{1,2},{2,3},{3,0},{4,5},{5,6},{6,7},{7,4},{8,9},{9,10},{10,1... | collective-permute-start | bytes 786440 | tf_op jit(solution)/shard_map/ppermute | solution.py:586
  302.3 2.2 copy-start

commit v5 on v3

--- a/solution.py
+++ b/solution.py
@@ -436,6 +436,30 @@
     )(lane, piece["kept"], piece["came"], weight, raw, token)
 
 
+def assemble_kernel(*refs):
+    shared, out = refs[:LANES], refs[-1]
+    part = shared[0].shape[0]
+    lane = lax.rem(lax.axis_index("col"), LANES)
+    for shift in range(LANES):
+        owner = lax.rem(lane + LANES - shift, LANES)
+        out[pl.ds(owner * part, part)] = shared[shift][...]
+
+
+def assemble(shared, token):
+    part = shared[0].shape[0]
+    inner = shared[0].shape[1:]
+    shape = (LANES * part,) + inner
+    return pl.pallas_call(
+        assemble_kernel,
+        out_shape=jax.ShapeDtypeStruct(shape, BF16),
+        grid=(1,),
+        in_specs=[full((part,) + inner)] * LANES + [ANYWHERE],
+        out_specs=full(shape),
+        compiler_params=PARAMS,
+        name="assemble",
+    )(*shared, token)
+
+
 def copy_kernel(parts, source, out, sem):
     size = source.shape[0] // parts
 
@@ -473,7 +497,6 @@
     tiles_col = partner.shape[0] // TILE // col_count
     sizes = tiles_row, tiles_col
     capacity = routes.shape[1]
-    part = tiles_row // LANES
     chunks = len(CHUNKS)
     lane = (lax.axis_index("col") % LANES).reshape(1)
     partner = partner.reshape(-1, HALF)
@@ -510,14 +533,15 @@
     place = targets * capacity + jnp.sum(same.astype(jnp.int32), axis=1)
 
     buffer = zero_buffer(devices * capacity, own)
-    lines = line_copies(spread, devices, buffer)
-    raw = lax.all_to_all(lines, ("row", "col"), split_axis=0, concat_axis=0, tiled=True)
-    token = lines
-    for pair in pairs:
+    token = buffer
+    for chunk, pair in enumerate(pairs):
         given = forward(pair, [token])
         token = given[0]
         for kind in range(2):
             pair[kind]["last"] = flipped(given[kind], *masks[1 - kind])
+        if chunk == 0:
+            token = line_copies(spread, devices, token)
+            raw = lax.all_to_all(token, ("row", "col"), split_axis=0, concat_axis=0, tiled=True)
 
     def finished(chunk, buffer, token):
         return finish(pairs[chunk], tile_index, place, raw, buffer, sizes, token)
@@ -525,20 +549,16 @@
     buffer = finished(0, buffer, token)
     joined = join_features(lane, pairs[0][0], join_weight, raw, tiles_row, buffer)
     buffer = finished(1, buffer, joined)
-    parts = jnp.zeros((LANES, part, HALF, width), BF16)
-    for shift in range(LANES):
-        shared = joined
-        if shift > 0:
-            ring = [
-                (source, source // LANES * LANES + (source + shift) % LANES)
-                for source in range(col_count)
-            ]
-            shared = lax.ppermute(joined, "col", ring)
-        parts = lax.dynamic_update_slice(
-            parts, shared[None], ((lane[0] - shift) % LANES, 0, 0, 0)
-        )
-    buffer = finished(2, buffer, parts)
-    coarse_features = parts.reshape(tiles_row * HALF, width)
+    shared = [joined]
+    for shift in range(1, LANES):
+        ring = [
+            (source, source // LANES * LANES + (source + shift) % LANES)
+            for source in range(col_count)
+        ]
+        shared.append(lax.ppermute(joined, "col", ring))
+    assembled = assemble(shared, buffer)
+    buffer = finished(2, buffer, assembled)
+    coarse_features = assembled.reshape(tiles_row * HALF, width)
     arrived = lax.all_to_all(buffer, ("row", "col"), split_axis=0, concat_axis=0, tiled=True)
     return (coarse_features, copied(arrived))
 

time: 296 us -> 299 us (1.010)
  local copies, waits for them, and re-layouts: 10 us -> 3.4 us
  waiting for transfers between devices: 67.1 us -> 72.9 us
    dynamic_update_slice x4 -> x0, local copies, waits for them, and re-layouts: 3.83 us -> none  [level(): lax.dynamic_update_slice(parts, shared[None], ((lane[0] - shift) % LANES,...]
  transfers between devices with their start and end apart: 17 -> 17, of which waited for: 8 -> 6; matrix products, arithmetic and copies ran while one was open for 3% -> 1% of each run, Pallas kernels for 14% -> 16%
where the time goes in v5:
time: 299 us; the launch traced here: 296 us
  blocking collectives  103 us (34%)
  waiting for transfers between devices  72.9 us (24%)
  Pallas kernels  72.8 us (24%)
  starting transfers between devices  42.8 us (14%)
  local copies, waits for them, and re-layouts  3.4 us (1%)
    all_to_all x1, blocking collectives, level(): lax.all_to_all(buffer, ('row', 'col'), split_axis=0, concat_axis=0, tiled...  103 us
    ppermute x12, waiting for transfers between devices, flipped(): return lax.ppermute(value, axis, pairs)  51.9 us
    pallas_call x3, Pallas kernels, pair_tiles(): pl.pallas_call(functools.partial(pair_kernel, starts, counts, with_featur...  25.3 us
    ppermute x12, starting transfers between devices, flipped(): return lax.ppermute(value, axis, pairs)  25.1 us
    pallas_call x1, Pallas kernels, sum_rows(): pl.pallas_call(functools.partial(sum_kernel, bounds, tiles_col), out_shap...  13.3 us
    pallas_call x3, Pallas kernels, finish(): pl.pallas_call(functools.partial(finish_kernel, starts, counts), out_shap...  12.6 us
    all_to_all x1, waiting for transfers between devices, level(): lax.all_to_all(token, ('row', 'col'), split_axis=0, concat_axis=0, tiled=...  9.18 us
    ppermute x3, waiting for transfers between devices, level(): shared.append(lax.ppermute(joined, 'col', ring))  9.14 us
  transfers between devices with their start and end apart: 17, of which 6 were waited for; matrix products, arithmetic and copies ran while one was open for 1% of the time, Pallas kernels for 16%

profile of v5, /device:TPU:32, one launch (start us, length us, event | category | flops | bytes accessed | tf_op | source)
XLA Modules:
  0.0 296.4 jit_solution(10771063171255881021)
XLA Ops:
  0.6 7.2 %pair_tiles.3 = (bf16[2,12,128,128]{3,2,1,0:T(8,128)(2,1)}, bf16[2,12,128,128]{3,2,1,0:T(8,128)(2,1)}, bf16[2,16,128,128]{3,2,1,0:T(8,128)(2,1)}, bf16[2,16,128,128]{3,2,1,0:T(8,128)(2,1)}) custom-call(s32[104]{0:T(128)} %index_ref.13, s32[4]{0:T(128)} %pert_ref.5, s32[1]{0:T(128)} %bitcast.lane_ref, bf16[104,256,256]{2,1,0:T(8,128)(2,1)} %tiles.5, ...), custom_call_target="tpu_custom_call" | custom-call | tf_op jit(solution)/shard_map/pair_tiles/pallas_call | solution.py:178
  7.8 10.4 %pair_tiles.4 = (bf16[2,24,128,128]{3,2,1,0:T(8,128)(2,1)}, bf16[2,24,128,128]{3,2,1,0:T(8,128)(2,1)}, bf16[2,24,128,128]{3,2,1,0:T(8,128)(2,1)}, bf16[2,24,128,128]{3,2,1,0:T(8,128)(2,1)}) custom-call(s32[104]{0:T(128)} %index_ref.13, s32[4]{0:T(128)} %pert_ref.5, s32[1]{0:T(128)} %bitcast.lane_ref, bf16[104,256,256]{2,1,0:T(8,128)(2,1)} %tiles.5, ...), custom_call_target="tpu_custom_call" | custom-call | tf_op jit(solution)/shard_map/pair_tiles/pallas_call | solution.py:178
  18.2 3.0 %collective-permute-start.6 = (bf16[2,24,128,128]{3,2,1,0:T(8,128)(2,1)}, bf16[2,24,128,128]{3,2,1,0:T(8,128)(2,1)}, u32[]{:S(2)}, u32[]{:S(2)}) collective-permute-start(bf16[2,24,128,128]{3,2,1,0:T(8,128)(2,1)} %get-tuple-element.24.rest_4_), channel_id=1, source_target_pairs={{0,64},{16,80},{32,96},{48,112},{64,0},{80,16},{96,32},{112,48},{1... | collective-permute-start | bytes 4718600 | tf_op jit(solution)/shard_map/ppermute | solution.py:25
  21.2 3.0 %collective-permute-start.7 = (bf16[2,24,128,128]{3,2,1,0:T(8,128)(2,1)}, bf16[2,24,128,128]{3,2,1,0:T(8,128)(2,1)}, u32[]{:S(2)}, u32[]{:S(2)}) collective-permute-start(bf16[2,24,128,128]{3,2,1,0:T(8,128)(2,1)} %get-tuple-element.26.rest_6_), channel_id=1, source_target_pairs={{0,8},{1,9},{2,10},{3,11},{4,12},{5,13},{6,14},{7,15},{8,0},{9,1},... | collective-permute-start | bytes 4718600 | tf_op jit(solution)/shard_map/ppermute | solution.py:25
  24.2 0.5 collective-permute-start
  24.8 0.5 collective-permute-start.1
  25.3 7.7 %pair_tiles.5 = (bf16[2,16,128,128]{3,2,1,0:T(8,128)(2,1)}, bf16[2,16,128,128]{3,2,1,0:T(8,128)(2,1)}, bf16[2,16,128,128]{3,2,1,0:T(8,128)(2,1)}, bf16[2,16,128,128]{3,2,1,0:T(8,128)(2,1)}) custom-call(s32[104]{0:T(128)} %index_ref.13, s32[4]{0:T(128)} %pert_ref.5, s32[1]{0:T(128)} %bitcast.lane_ref, bf16[104,256,256]{2,1,0:T(8,128)(2,1)} %tiles.5, ...), custom_call_target="tpu_custom_call" | custom-call | tf_op jit(solution)/shard_map/pair_tiles/pallas_call | solution.py:178
  33.0 3.0 %collective-permute-start.4 = (bf16[2,16,128,128]{3,2,1,0:T(8,128)(2,1)}, bf16[2,16,128,128]{3,2,1,0:T(8,128)(2,1)}, u32[]{:S(2)}, u32[]{:S(2)}) collective-permute-start(bf16[2,16,128,128]{3,2,1,0:T(8,128)(2,1)} %get-tuple-element.28.rest_8_), channel_id=1, source_target_pairs={{0,64},{16,80},{32,96},{48,112},{64,0},{80,16},{96,32},{112,48},{1... | collective-permute-start | bytes 3145736 | tf_op jit(solution)/shard_map/ppermute | solution.py:25
  36.0 38.1 %collective-permute-done.refs_1_.came = bf16[2,12,128,128]{3,2,1,0:T(8,128)(2,1)} collective-permute-done((bf16[2,12,128,128]{3,2,1,0:T(8,128)(2,1)}, bf16[2,12,128,128]{3,2,1,0:T(8,128)(2,1)}, u32[]{:S(2)}, u32[]{:S(2)}) %collective-permute-start) | collective-permute-done | bytes 786464 | tf_op jit(solution)/shard_map/ppermute | solution.py:25
  74.2 3.0 %collective-permute-start.5 = (bf16[2,16,128,128]{3,2,1,0:T(8,128)(2,1)}, bf16[2,16,128,128]{3,2,1,0:T(8,128)(2,1)}, u32[]{:S(2)}, u32[]{:S(2)}) collective-permute-start(bf16[2,16,128,128]{3,2,1,0:T(8,128)(2,1)} %get-tuple-element.30.rest_10_), channel_id=1, source_target_pairs={{0,8},{1,9},{2,10},{3,11},{4,12},{5,13},{6,14},{7,15},{8,0},{9,1},... | collective-permute-start | bytes 3145736 | tf_op jit(solution)/shard_map/ppermute | solution.py:25
  77.2 13.3 %sum_rows.1._ = f32[16,256]{1,0:T(8,128)} custom-call(s32[104]{0:T(128)} %index_ref.13, bf16[2,12,128,128]{3,2,1,0:T(8,128)(2,1)} %get-tuple-element.21.rest_0_, bf16[2,12,128,128]{3,2,1,0:T(8,128)(2,1)} %get-tuple-element.20.rest_1_.refs_0_.kept, bf16[2,16,128,128]{3,2,1,0:T(8,128)(2,1)} %get-tuple-element.22.rest_2_, ...), custom_call_target="tpu_custom_call" | custom-call | tf_op jit(solution)/shard_map/sum_rows/pallas_call | solution.py:241
  90.5 1.3 copy.15
  91.8 6.0 %all-to-all-start = ((f32[16,1,256]{2,1,0:T(1,128)}), f32[16,1,256]{2,1,0:T(1,128)S(1)}, u32[]{:S(2)}, u32[]{:S(2)}) async-start(f32[16,1,256]{2,1,0:T(1,128)} %copy.15), calls=%async_computation | async-start | bytes 32768 | tf_op jit(solution)/shard_map/all_to_all | solution.py:528
  97.8 3.9 %zero_buffer.1.refs_4_.refs_7_ = bf16[256,128,128]{2,1,0:T(8,128)(2,1)} custom-call(f32[16,256]{1,0:T(8,128)} %sum_rows.1._), custom_call_target="tpu_custom_call" | custom-call | tf_op jit(solution)/shard_map/zero_buffer/pallas_call | solution.py:313
  101.6 2.7 all-to-all-done
  104.3 0.6 copy.22
  104.9 0.0 copy-start.4
  104.9 0.0 collective-permute-done.1.refs_3_.refs_4_
  105.0 2.3 forward.3
  107.2 1.4 line_copies.1.refs_4_
  108.6 0.0 copy-start
  108.6 0.0 collective-permute-done.6.refs_1_
  108.6 0.0 collective-permute-done.7.refs_3_.refs_4_
  108.6 3.9 %forward.4 = (bf16[24,128,128]{2,1,0:T(8,128)(2,1)}, bf16[24,128,128]{2,1,0:T(8,128)(2,1)}) custom-call(bf16[2,24,128,128]{3,2,1,0:T(8,128)(2,1)} %get-tuple-element.25.rest_5_.refs_0_, bf16[2,24,128,128]{3,2,1,0:T(8,128)(2,1)} %collective-permute-done.6.refs_1_, bf16[2,24,128,128]{3,2,1,0:T(8,128)(2,1)} %get-tuple-element.27.rest_0_.rest_7_.refs_2_.refs_3_, ...), custom_call_target="tpu_custom_call" | custom-call | tf_op jit(solution)/shard_map/forward/pallas_call | solution.py:297
  112.5 2.8 collective-permute-start.12
  115.4 1.3 collective-permute-start.11
  116.7 2.2 collective-permute-start.2
  118.9 0.0 collective-permute-done.4.refs_1_
  118.9 0.7 collective-permute-start.3
  119.6 0.0 copy-done.4
  119.6 0.0 collective-permute-done.5.refs_3_.refs_4_
  119.6 2.4 forward.5
  122.0 2.8 collective-permute-start.14
  124.9 13.7 %collective-permute-done.2.refs_2_ = bf16[8,128,128]{2,1,0:T(8,128)(2,1)S(1)} collective-permute-done((bf16[8,128,128]{2,1,0:T(8,128)(2,1)}, bf16[8,128,128]{2,1,0:T(8,128)(2,1)S(1)}, u32[]{:S(2)}, u32[]{:S(2)}) %collective-permute-start.2) | collective-permute-done | bytes 262176 | tf_op jit(solution)/shard_map/ppermute | solution.py:25
  138.6 0.0 copy-start.1
  138.6 2.1 collective-permute-start.13
  140.7 0.2 convert_reduce_fusion
  140.9 0.0 copy-done
  140.9 0.8 copy.16
  141.7 9.0 %all-to-all-start.1 = ((f32[128,1,256]{2,1,0:T(1,128)}), f32[128,1,256]{2,1,0:T(1,128)S(1)}, u32[]{:S(2)}, u32[]{:S(2)}) async-start(f32[128,1,256]{2,1,0:T(1,128)} %copy.16), calls=%async_computation.1 | async-start | bytes 262144 | tf_op jit(solution)/shard_map/all_to_all | solution.py:544
  150.6 0.6 multiply_add_fusion.place_ref
  151.2 9.2 %all-to-all-done.1 = f32[128,1,256]{2,1,0:T(1,128)S(1)} async-done(((f32[128,1,256]{2,1,0:T(1,128)}), f32[128,1,256]{2,1,0:T(1,128)S(1)}, u32[]{:S(2)}, u32[]{:S(2)}) %all-to-all-start.1) | async-done | bytes 131104 | tf_op jit(solution)/shard_map/all_to_all | solution.py:544
  160.4 0.7 copy.21
  161.1 0.0 collective-permute-done.3.refs_5_
  161.1 0.0 copy-done.1
  161.1 3.5 %finish.3._.refs_7_ = bf16[256,128,128]{2,1,0:T(8,128)(2,1)} custom-call(s32[104]{0:T(128)} %index_ref.13, s32[104]{0:T(128)} %multiply_add_fusion.place_ref, bf16[2,12,128,128]{3,2,1,0:T(8,128)(2,1)} %get-tuple-element.20.rest_1_.refs_0_.kept, bf16[2,12,128,128]{3,2,1,0:T(8,128)(2,1)} %collective-permute-done.refs_1_.came, ...), custom_call_target="tpu_custom_call", output_to_operand_aliasing={{}: (9, {})} | custom-call | tf_op jit(solution)/shard_map/finish/pallas_call | solution.py:382
  164.6 2.1 join_features.1.refs_8_.refs_0_
  166.7 1.7 collective-permute-start.10
  168.4 0.0 collective-permute-done.12.refs_5_
  168.4 1.0 collective-permute-start.9
  169.5 0.0 collective-permute-done.11.refs_2_
  169.5 0.0 collective-permute-start.8
  169.5 5.3 %finish.4.refs_4_.refs_7_ = bf16[256,128,128]{2,1,0:T(8,128)(2,1)} custom-call(s32[104]{0:T(128)} %index_ref.13, s32[104]{0:T(128)} %multiply_add_fusion.place_ref, bf16[2,24,128,128]{3,2,1,0:T(8,128)(2,1)} %get-tuple-element.25.rest_5_.refs_0_, bf16[2,24,128,128]{3,2,1,0:T(8,128)(2,1)} %collective-permute-done.6.refs_1_, ...), custom_call_target="tpu_custom_call", output_to_operand_aliasing={{}: (9, {})} | custom-call | tf_op jit(solution)/shard_map/finish/pallas_call | solution.py:382
  174.8 5.5 %collective-permute-done.10.refs_3_ = bf16[4,128,256]{2,1,0:T(8,128)(2,1)S(1)} collective-permute-done((bf16[4,128,256]{2,1,0:T(8,128)(2,1)}, bf16[4,128,256]{2,1,0:T(8,128)(2,1)S(1)}, u32[]{:S(2)}, u32[]{:S(2)}) %collective-permute-start.10) | collective-permute-done | bytes 262176 | tf_op jit(solution)/shard_map/ppermute | solution.py:558
  180.2 0.0 collective-permute-done.9.refs_2_
  180.2 3.7 %collective-permute-done.8.refs_1_ = bf16[4,128,256]{2,1,0:T(8,128)(2,1)} collective-permute-done((bf16[4,128,256]{2,1,0:T(8,128)(2,1)}, bf16[4,128,256]{2,1,0:T(8,128)(2,1)}, u32[]{:S(2)}, u32[]{:S(2)}) %collective-permute-start.8) | collective-permute-done | bytes 262176 | tf_op jit(solution)/shard_map/ppermute | solution.py:558
  183.9 0.0 copy-done.2
  183.9 0.0 copy-done.3
  183.9 2.2 assemble.1.refs_8_
  186.2 0.0 collective-permute-done.14.refs_5_
  186.2 0.0 collective-permute-done.13.refs_2_
  186.2 3.8 %finish.5 = bf16[256,128,128]{2,1,0:T(8,128)(2,1)} custom-call(s32[104]{0:T(128)} %index_ref.13, s32[104]{0:T(128)} %multiply_add_fusion.place_ref, bf16[2,16,128,128]{3,2,1,0:T(8,128)(2,1)} %get-tuple-element.29.rest_9_.refs_0_, bf16[2,16,128,128]{3,2,1,0:T(8,128)(2,1)} %collective-permute-done.4.refs_1_, ...), custom_call_target="tpu_custom_call", output_to_operand_aliasing={{}: (9, {})} | custom-call | tf_op jit(solution)/shard_map/finish/pallas_call | solution.py:382
  190.0 102.9 %all_to_all.27.source = bf16[256,128,128]{2,1,0:T(8,128)(2,1)S(1)} all-to-all(bf16[256,128,128]{2,1,0:T(8,128)(2,1)} %finish.5), channel_id=1, replica_groups=mesh['row'=8,'col'=16] {'row','col'}, dimensions={0} | all-to-all | bytes 16777216 | tf_op jit(solution)/shard_map/all_to_all | solution.py:562
  292.8 3.4 %copied.1 = bf16[256,128,128]{2,1,0:T(8,128)(2,1)} custom-call(bf16[256,128,128]{2,1,0:T(8,128)(2,1)S(1)} %all_to_all.27.source), custom_call_target="tpu_custom_call" | custom-call | tf_op jit(solution)/shard_map/copied/pallas_call | solution.py:478
  (3 shorter events, 0.0 us)
Async XLA Ops:
  18.2 90.4 %collective-permute-start.6 = (bf16[2,24,128,128]{3,2,1,0:T(8,128)(2,1)}, bf16[2,24,128,128]{3,2,1,0:T(8,128)(2,1)}, u32[]{:S(2)}, u32[]{:S(2)}) collective-permute-start(bf16[2,24,128,128]{3,2,1,0:T(8,128)(2,1)} %get-tuple-element.24.rest_4_), channel_id=1, source_target_pairs={{0,64},{16,80},{32,96},{48,112},{64,0},{80,16},{96,32},{112,48},{1... | collective-permute-start | bytes 4718600 | tf_op jit(solution)/shard_map/ppermute | solution.py:25
  21.2 87.4 %collective-permute-start.7 = (bf16[2,24,128,128]{3,2,1,0:T(8,128)(2,1)}, bf16[2,24,128,128]{3,2,1,0:T(8,128)(2,1)}, u32[]{:S(2)}, u32[]{:S(2)}) collective-permute-start(bf16[2,24,128,128]{3,2,1,0:T(8,128)(2,1)} %get-tuple-element.26.rest_6_), channel_id=1, source_target_pairs={{0,8},{1,9},{2,10},{3,11},{4,12},{5,13},{6,14},{7,15},{8,0},{9,1},... | collective-permute-start | bytes 4718600 | tf_op jit(solution)/shard_map/ppermute | solution.py:25
  24.2 49.9 %collective-permute-start = (bf16[2,12,128,128]{3,2,1,0:T(8,128)(2,1)}, bf16[2,12,128,128]{3,2,1,0:T(8,128)(2,1)}, u32[]{:S(2)}, u32[]{:S(2)}) collective-permute-start(bf16[2,12,128,128]{3,2,1,0:T(8,128)(2,1)} %get-tuple-element.21.rest_0_), channel_id=1, source_target_pairs={{0,64},{16,80},{32,96},{48,112},{64,0},{80,16},{96,32},{112,48},{1... | collective-permute-start | bytes 2359304 | tf_op jit(solution)/shard_map/ppermute | solution.py:25
  24.8 80.2 %collective-permute-start.1 = (bf16[2,16,128,128]{3,2,1,0:T(8,128)(2,1)}, bf16[2,16,128,128]{3,2,1,0:T(8,128)(2,1)}, u32[]{:S(2)}, u32[]{:S(2)}) collective-permute-start(bf16[2,16,128,128]{3,2,1,0:T(8,128)(2,1)} %get-tuple-element.22.rest_2_), channel_id=1, source_target_pairs={{0,8},{1,9},{2,10},{3,11},{4,12},{5,13},{6,14},{7,15},{8,0},{9,1},... | collective-permute-start | bytes 3145736 | tf_op jit(solution)/shard_map/ppermute | solution.py:25
  33.0 85.9 %collective-permute-start.4 = (bf16[2,16,128,128]{3,2,1,0:T(8,128)(2,1)}, bf16[2,16,128,128]{3,2,1,0:T(8,128)(2,1)}, u32[]{:S(2)}, u32[]{:S(2)}) collective-permute-start(bf16[2,16,128,128]{3,2,1,0:T(8,128)(2,1)} %get-tuple-element.28.rest_8_), channel_id=1, source_target_pairs={{0,64},{16,80},{32,96},{48,112},{64,0},{80,16},{96,32},{112,48},{1... | collective-permute-start | bytes 3145736 | tf_op jit(solution)/shard_map/ppermute | solution.py:25
  74.2 45.5 %collective-permute-start.5 = (bf16[2,16,128,128]{3,2,1,0:T(8,128)(2,1)}, bf16[2,16,128,128]{3,2,1,0:T(8,128)(2,1)}, u32[]{:S(2)}, u32[]{:S(2)}) collective-permute-start(bf16[2,16,128,128]{3,2,1,0:T(8,128)(2,1)} %get-tuple-element.30.rest_10_), channel_id=1, source_target_pairs={{0,8},{1,9},{2,10},{3,11},{4,12},{5,13},{6,14},{7,15},{8,0},{9,1},... | collective-permute-start | bytes 3145736 | tf_op jit(solution)/shard_map/ppermute | solution.py:25
  91.8 12.5 %all-to-all-start = ((f32[16,1,256]{2,1,0:T(1,128)}), f32[16,1,256]{2,1,0:T(1,128)S(1)}, u32[]{:S(2)}, u32[]{:S(2)}) async-start(f32[16,1,256]{2,1,0:T(1,128)} %copy.15), calls=%async_computation | async-start | bytes 32768 | tf_op jit(solution)/shard_map/all_to_all | solution.py:528
  104.9 14.7 %copy-start.4 = (s32[104,2]{0,1:T(2,128)S(1)}, s32[104,2]{0,1:T(2,128)}, u32[]{:S(2)}) copy-start(s32[104,2]{0,1:T(2,128)} %param.15) | copy-start | bytes 2500
  108.6 32.3 %copy-start = (f32[128,256]{1,0:T(8,128)S(1)}, f32[128,256]{1,0:T(8,128)}, u32[]{:S(2)}) copy-start(f32[128,256]{1,0:T(8,128)} %line_copies.1.refs_4_) | copy-start | bytes 393220
  112.5 55.9 %collective-permute-start.12 = (bf16[24,128,128]{2,1,0:T(8,128)(2,1)}, bf16[24,128,128]{2,1,0:T(8,128)(2,1)}, u32[]{:S(2)}, u32[]{:S(2)}) collective-permute-start(bf16[24,128,128]{2,1,0:T(8,128)(2,1)} %get-tuple-element.36), channel_id=1, source_target_pairs={{0,64},{16,80},{32,96},{48,112},{64,0},{80,16},{96,32},{112,48},{1... | collective-permute-start | bytes 2359304 | tf_op jit(solution)/shard_map/ppermute | solution.py:25
  115.4 54.1 %collective-permute-start.11 = (bf16[24,128,128]{2,1,0:T(8,128)(2,1)}, bf16[24,128,128]{2,1,0:T(8,128)(2,1)}, u32[]{:S(2)}, u32[]{:S(2)}) collective-permute-start(bf16[24,128,128]{2,1,0:T(8,128)(2,1)} %get-tuple-element.34.refs_4_), channel_id=1, source_target_pairs={{0,8},{1,9},{2,10},{3,11},{4,12},{5,13},{6,14},{7,15},{8,0},{9,1},... | collective-permute-start | bytes 2359304 | tf_op jit(solution)/shard_map/ppermute | solution.py:25
  116.7 21.9 %collective-permute-start.2 = (bf16[8,128,128]{2,1,0:T(8,128)(2,1)}, bf16[8,128,128]{2,1,0:T(8,128)(2,1)S(1)}, u32[]{:S(2)}, u32[]{:S(2)}) collective-permute-start(bf16[8,128,128]{2,1,0:T(8,128)(2,1)} %get-tuple-element.32._), channel_id=1, source_target_pairs={{0,8},{1,9},{2,10},{3,11},{4,12},{5,13},{6,14},{7,15},{8,0},{9,1},... | collective-permute-start | bytes 786440 | tf_op jit(solution)/shard_map/ppermute | solution.py:25
  118.9 42.2 %collective-permute-start.3 = (bf16[16,128,128]{2,1,0:T(8,128)(2,1)}, bf16[16,128,128]{2,1,0:T(8,128)(2,1)}, u32[]{:S(2)}, u32[]{:S(2)}) collective-permute-start(bf16[16,128,128]{2,1,0:T(8,128)(2,1)} %get-tuple-element.33), channel_id=1, source_target_pairs={{0,64},{16,80},{32,96},{48,112},{64,0},{80,16},{96,32},{112,48},{1... | collective-permute-start | bytes 1572872 | tf_op jit(solution)/shard_map/ppermute | solution.py:25
  122.0 64.1 %collective-permute-start.14 = (bf16[16,128,128]{2,1,0:T(8,128)(2,1)}, bf16[16,128,128]{2,1,0:T(8,128)(2,1)}, u32[]{:S(2)}, u32[]{:S(2)}) collective-permute-start(bf16[16,128,128]{2,1,0:T(8,128)(2,1)} %get-tuple-element.37), channel_id=1, source_target_pairs={{0,64},{16,80},{32,96},{48,112},{64,0},{80,16},{96,32},{112,48},{1... | collective-permute-start | bytes 1572872 | tf_op jit(solution)/shard_map/ppermute | solution.py:25
  138.6 22.5 %copy-start.1 = (bf16[8,128,128]{2,1,0:T(8,128)(2,1)}, bf16[8,128,128]{2,1,0:T(8,128)(2,1)S(1)}, u32[]{:S(2)}) copy-start(bf16[8,128,128]{2,1,0:T(8,128)(2,1)S(1)} %collective-permute-done.2.refs_2_) | copy-start | bytes 786436
  138.6 47.6 %collective-permute-start.13 = (bf16[16,128,128]{2,1,0:T(8,128)(2,1)}, bf16[16,128,128]{2,1,0:T(8,128)(2,1)}, u32[]{:S(2)}, u32[]{:S(2)}) collective-permute-start(bf16[16,128,128]{2,1,0:T(8,128)(2,1)} %get-tuple-element.35.refs_8_), channel_id=1, source_target_pairs={{0,8},{1,9},{2,10},{3,11},{4,12},{5,13},{6,14},{7,15},{8,0},{9,1},... | collective-permute-start | bytes 1572872 | tf_op jit(solution)/shard_map/ppermute | solution.py:25
  141.7 18.7 %all-to-all-start.1 = ((f32[128,1,256]{2,1,0:T(1,128)}), f32[128,1,256]{2,1,0:T(1,128)S(1)}, u32[]{:S(2)}, u32[]{:S(2)}) async-start(f32[128,1,256]{2,1,0:T(1,128)} %copy.16), calls=%async_computation.1 | async-start | bytes 262144 | tf_op jit(solution)/shard_map/all_to_all | solution.py:544
  166.7 13.5 %collective-permute-start.10 = (bf16[4,128,256]{2,1,0:T(8,128)(2,1)}, bf16[4,128,256]{2,1,0:T(8,128)(2,1)S(1)}, u32[]{:S(2)}, u32[]{:S(2)}) collective-permute-start(bf16[4,128,256]{2,1,0:T(8,128)(2,1)} %join_features.1.refs_8_.refs_0_), channel_id=1, source_target_pairs={{0,3},{1,0},{2,1},{3,2},{4,7},{5,4},{6,5},{7,6},{8,11},{9,8},{10,9... | collective-permute-start | bytes 786440 | tf_op jit(solution)/shard_map/ppermute | solution.py:558
  168.4 11.8 %collective-permute-start.9 = (bf16[4,128,256]{2,1,0:T(8,128)(2,1)}, bf16[4,128,256]{2,1,0:T(8,128)(2,1)S(1)}, u32[]{:S(2)}, u32[]{:S(2)}) collective-permute-start(bf16[4,128,256]{2,1,0:T(8,128)(2,1)} %join_features.1.refs_8_.refs_0_), channel_id=1, source_target_pairs={{0,2},{1,3},{2,0},{3,1},{4,6},{5,7},{6,4},{7,5},{8,10},{9,11},{10,... | collective-permute-start | bytes 786440 | tf_op jit(solution)/shard_map/ppermute | solution.py:558
  169.5 14.4 %collective-permute-start.8 = (bf16[4,128,256]{2,1,0:T(8,128)(2,1)}, bf16[4,128,256]{2,1,0:T(8,128)(2,1)}, u32[]{:S(2)}, u32[]{:S(2)}) collective-permute-start(bf16[4,128,256]{2,1,0:T(8,128)(2,1)} %join_features.1.refs_8_.refs_0_), channel_id=1, source_target_pairs={{0,1},{1,2},{2,3},{3,0},{4,5},{5,6},{6,7},{7,4},{8,9},{9,10},{10,1... | collective-permute-start | bytes 786440 | tf_op jit(solution)/shard_map/ppermute | solution.py:558
  180.2 3.7 %copy-start.2 = (bf16[4,128,256]{2,1,0:T(8,128)(2,1)}, bf16[4,128,256]{2,1,0:T(8,128)(2,1)S(1)}, u32[]{:S(2)}) copy-start(bf16[4,128,256]{2,1,0:T(8,128)(2,1)S(1)} %collective-permute-done.10.refs_3_) | copy-start | bytes 786436
  180.2 3.7 %copy-start.3 = (bf16[4,128,256]{2,1,0:T(8,128)(2,1)}, bf16[4,128,256]{2,1,0:T(8,128)(2,1)S(1)}, u32[]{:S(2)}) copy-start(bf16[4,128,256]{2,1,0:T(8,128)(2,1)S(1)} %collective-permute-done.9.refs_2_) | copy-start | bytes 786436

commit v6 on v4

--- a/solution.py
+++ b/solution.py
@@ -14,7 +14,7 @@
 LANES = 4
 ROW_FIRST = 48
 CHUNKS = (8, 16), (24, 24), (16, 16)
-SPLITS = 1, 2, 2
+SPLITS = 1, 1, 2
 BF16 = jnp.bfloat16
 F32 = jnp.float32
 PARAMS = pltpu.CompilerParams(vmem_limit_bytes=66_500_000)
@@ -314,21 +314,19 @@
     )(*operands, *tokens)
 
 
-def zero_kernel(_, *outs):
-    for out in outs:
-        out[...] = jnp.zeros_like(out)
-
-
-def zero_buffers(count, token):
-    block = pl.BlockSpec((64, HALF // 2, HALF), lambda s: (s, 0, 0))
+def zero_kernel(_, out):
+    out[...] = jnp.zeros_like(out)
+
+
+def zero_buffer(count, token):
     return pl.pallas_call(
         zero_kernel,
-        out_shape=[jax.ShapeDtypeStruct((count, HALF // 2, HALF), BF16)] * 2,
+        out_shape=jax.ShapeDtypeStruct((count, HALF, HALF), BF16),
         grid=(count // 64,),
         in_specs=[ANYWHERE],
-        out_specs=[block, block],
+        out_specs=pl.BlockSpec((64, HALF, HALF), lambda s: (s, 0, 0)),
         compiler_params=PARAMS,
-        name="zero_buffers",
+        name="zero_buffer",
     )(token)
 
 
@@ -375,27 +373,27 @@
                 j = lax.rem(index_ref[start + m], tiles_col)
                 total = kept[0, t].astype(F32) + came[0, t].astype(F32) + last[t].astype(F32)
                 done[base + m] = (total * row_scale[i] * col_scale[j, 0:1]).astype(BF16)
-                target = out.at[place_ref[start + m]]
+                target = out.at[place_ref[start + m], pl.ds(h * size, size)]
                 pltpu.make_async_copy(done.at[base + m], target, sem).start()
 
         base += counts[number]
 
     @pl.when(step == pl.num_programs(0) - 1)
     def _():
-        pltpu.make_async_copy(done, out.at[pl.ds(0, done.shape[0])], sem).wait()
+        sent = out.at[pl.ds(0, done.shape[0]), pl.ds(0, size)]
+        pltpu.make_async_copy(done, sent, sem).wait()
 
 
 def finish(pieces, h, index, place, raw, buffer, sizes, token):
     tiles_row, tiles_col = sizes
-    size = buffer.shape[1]
+    size = HALF // len(pieces[0]["last"])
     starts = [piece["start"] for piece in pieces]
     counts = [piece["count"] for piece in pieces]
     specs, operands = [], []
     for piece in pieces:
         steps = piece["count"] // STEP
-        split = len(piece["last"]) > 1
-        specs += [quadrant(1, steps, size, h)] * 2 + [plain(steps, size, 0 if split else h)]
-        operands += [piece["kept"], piece["came"], piece["last"][h if split else 0]]
+        specs += [quadrant(1, steps, size, h)] * 2 + [plain(steps, size)]
+        operands += [piece["kept"], piece["came"], piece["last"][h]]
     return pl.pallas_call(
         functools.partial(finish_kernel, starts, counts, h),
         out_shape=jax.ShapeDtypeStruct(buffer.shape, BF16),
@@ -453,60 +451,58 @@
     )(lane, piece["kept"], piece["came"], weight, raw, token)
 
 
-def assemble_kernel(*refs):
-    shared, out = refs[:LANES], refs[-1]
-    part = shared[0].shape[0]
+def copy_kernel(pieces, *refs):
+    source, shared = refs[0], refs[1 : 1 + LANES]
+    out, features, held, sem, in_sem, out_sem = refs[1 + LANES :]
+    size = source.shape[0] // pieces
+    part = held.shape[1]
     lane = lax.rem(lax.axis_index("col"), LANES)
-    for shift in range(LANES):
-        owner = lax.rem(lane + LANES - shift, LANES)
-        out[pl.ds(owner * part, part)] = shared[shift][...]
-
-
-def assemble(shared, token):
-    part = shared[0].shape[0]
-    inner = shared[0].shape[1:]
-    shape = (LANES * part,) + inner
-    return pl.pallas_call(
-        assemble_kernel,
-        out_shape=jax.ShapeDtypeStruct(shape, BF16),
-        grid=(1,),
-        in_specs=[full((part,) + inner)] * LANES + [ANYWHERE],
-        out_specs=full(shape),
-        compiler_params=pltpu.CompilerParams(vmem_limit_bytes=8 << 20),
-        name="assemble",
-    )(*shared, token)
-
-
-def copy_kernel(parts, h, source, *refs):
-    out, sem = refs[-2:]
-    count = source.shape[0] // parts
-    size = source.shape[1]
 
     def move(k):
-        window = pl.ds(k * count, count)
-        target = out.at[window, pl.ds(h * size, size)]
-        return pltpu.make_async_copy(source.at[window], target, sem.at[k])
-
-    for k in range(parts):
+        window = pl.ds(k * size, size)
+        return pltpu.make_async_copy(source.at[window], out.at[window], sem.at[k])
+
+    def read(k):
+        return pltpu.make_async_copy(shared[k], held.at[k], in_sem.at[k])
+
+    def write(k):
+        owner = lax.rem(lane + LANES - k, LANES)
+        target = features.at[pl.ds(owner * part, part)]
+        return pltpu.make_async_copy(held.at[k], target, out_sem.at[k])
+
+    for k in range(LANES):
+        read(k).start()
+    for k in range(pieces):
         move(k).start()
-    for k in range(parts):
+    for k in range(LANES):
+        read(k).wait()
+        write(k).start()
+    for k in range(pieces):
         move(k).wait()
-
-
-def copied(source, h, out):
-    parts = 16
-    shape = (source.shape[0], 2 * source.shape[1], source.shape[2])
-    operands = [source] if out is None else [source, out]
-    return pl.pallas_call(
-        functools.partial(copy_kernel, parts, h),
-        out_shape=jax.ShapeDtypeStruct(shape, source.dtype),
-        in_specs=[ANYWHERE] * len(operands),
-        out_specs=ANYWHERE,
-        scratch_shapes=[pltpu.SemaphoreType.DMA((parts,))],
-        input_output_aliases={} if out is None else {1: 0},
-        compiler_params=pltpu.CompilerParams(vmem_limit_bytes=1 << 20),
+    for k in range(LANES):
+        write(k).wait()
+
+
+def copied(source, shared):
+    pieces = 16
+    part = shared[0].shape
+    return pl.pallas_call(
+        functools.partial(copy_kernel, pieces),
+        out_shape=[
+            jax.ShapeDtypeStruct(source.shape, source.dtype),
+            jax.ShapeDtypeStruct((LANES * part[0],) + part[1:], BF16),
+        ],
+        in_specs=[ANYWHERE] * (1 + LANES),
+        out_specs=[ANYWHERE, ANYWHERE],
+        scratch_shapes=[
+            pltpu.VMEM((LANES,) + part, BF16),
+            pltpu.SemaphoreType.DMA((pieces,)),
+            pltpu.SemaphoreType.DMA((LANES,)),
+            pltpu.SemaphoreType.DMA((LANES,)),
+        ],
+        compiler_params=pltpu.CompilerParams(vmem_limit_bytes=2 << 20),
         name="copied",
-    )(*operands)
+    )(source, *shared)
 
 
 def level(features, join_weight, partner, tile_index, tile_values, pert_slot, pert_values, routes):
@@ -555,8 +551,8 @@
     same = (targets[:, None] == targets[None, :]) & (order[None, :] < order[:, None])
     place = targets * capacity + jnp.sum(same.astype(jnp.int32), axis=1)
 
-    buffers = list(zero_buffers(devices * capacity, own))
-    token = buffers[0]
+    buffer = zero_buffer(devices * capacity, own)
+    token = buffer
     for chunk, pair in enumerate(pairs):
         splits = SPLITS[chunk]
         given = forward(pair, splits, [token])
@@ -570,12 +566,6 @@
             token = line_copies(spread, devices, token)
             raw = lax.all_to_all(token, ("row", "col"), split_axis=0, concat_axis=0, tiled=True)
 
-    def finished(pieces, h, token):
-        return finish(pieces, h, tile_index, place, raw, buffers[h], sizes, token)
-
-    def delivered(h):
-        return lax.all_to_all(buffers[h], ("row", "col"), split_axis=0, concat_axis=0, tiled=True)
-
     joined = join_features(lane, pairs[0][0], join_weight, raw, tiles_row, token)
     shared = [joined]
     for shift in range(1, LANES):
@@ -584,15 +574,12 @@
             for source in range(col_count)
         ]
         shared.append(lax.ppermute(joined, "col", ring))
-    buffers[0] = finished(pairs[0] + pairs[1], 0, joined)
-    buffers[0] = finished(pairs[2], 0, joined)
-    buffers[1] = finished(pairs[0] + pairs[1] + pairs[2], 1, buffers[0])
-    first = delivered(0)
-    second = delivered(1)
-    coarse_features = assemble(shared, buffers[1]).reshape(tiles_row * HALF, width)
-    result = copied(first, 0, None)
-    result = copied(second, 1, result)
-    return (coarse_features, result)
+    for chunk, pair in enumerate(pairs):
+        for h in range(SPLITS[chunk]):
+            buffer = finish(pair, h, tile_index, place, raw, buffer, sizes, joined)
+    arrived = lax.all_to_all(buffer, ("row", "col"), split_axis=0, concat_axis=0, tiled=True)
+    result, coarse_features = copied(arrived, shared)
+    return (coarse_features.reshape(tiles_row * HALF, width), result)
 
 
 def solution(mesh):

time: 564 us -> 562 us (level)
  waiting for transfers between devices: 145 us -> 174 us
  blocking collectives: 21.6 us -> 0 us
  starting transfers between devices: 60.3 us -> 52.3 us
    ppermute x3, waiting for transfers between devices: 54.3 us -> 105 us  [level(): shared.append(lax.ppermute(joined, 'col', ring))]
    ppermute x16 -> x14, waiting for transfers between devices: 82.3 us -> 57.5 us  [flipped(): return lax.ppermute(value, axis, pairs)]
    all_to_all x1 -> x0, blocking collectives: 21.6 us -> none  [level(): spread = lax.all_to_all(own, 'col', split_axis=0, concat_axis=0, tiled=True)]
    ppermute x16 -> x14, starting transfers between devices: 33.4 us -> 28.4 us  [flipped(): return lax.ppermute(value, axis, pairs)]
    pallas_call x4 -> x2, Pallas kernels: 262 us -> 259 us  [the longest x1 256 us: copied(): pl.pallas_call(functools.partial(copy_kernel, pieces), out_shape=[jax.Sha...]
    pallas_call x3 -> x4, Pallas kernels: 13.8 us -> 15.3 us  [finish(): pl.pallas_call(functools.partial(finish_kernel, starts, counts, h), out_s...]
  transfers between devices with their start and end apart: 22 -> 20, of which waited for: 6 -> 6; matrix products, arithmetic and copies ran while one was open for 1% -> 1% of each run, Pallas kernels for 33% -> 9%
where the time goes in v6:
time: 562 us; the launch traced here: 557 us
  Pallas kernels  325 us (58%)
  waiting for transfers between devices  174 us (31%)
  starting transfers between devices  52.3 us (9%)
    pallas_call x1, Pallas kernels, copied(): pl.pallas_call(functools.partial(copy_kernel, pieces), out_shape=[jax.Sha...  256 us
    ppermute x3, waiting for transfers between devices, level(): shared.append(lax.ppermute(joined, 'col', ring))  105 us
    ppermute x14, waiting for transfers between devices, flipped(): return lax.ppermute(value, axis, pairs)  57.5 us
    ppermute x14, starting transfers between devices, flipped(): return lax.ppermute(value, axis, pairs)  28.4 us
    pallas_call x3, Pallas kernels, pair_tiles(): pl.pallas_call(functools.partial(pair_kernel, starts, counts, with_featur...  25.3 us
    pallas_call x4, Pallas kernels, finish(): pl.pallas_call(functools.partial(finish_kernel, starts, counts, h), out_s...  15.3 us
    pallas_call x1, Pallas kernels, sum_rows(): pl.pallas_call(functools.partial(sum_kernel, bounds, tiles_col), out_shap...  13.3 us
  transfers between devices with their start and end apart: 20, of which 6 were waited for; matrix products, arithmetic and copies ran while one was open for 1% of the time, Pallas kernels for 9%

profile of v6, /device:TPU:32, one launch (start us, length us, event | category | flops | bytes accessed | tf_op | source)
XLA Modules:
  0.0 557.3 jit_solution(13821541469656399827)
XLA Ops:
  0.6 7.2 %pair_tiles.3 = (bf16[2,12,128,128]{3,2,1,0:T(8,128)(2,1)}, bf16[2,12,128,128]{3,2,1,0:T(8,128)(2,1)}, bf16[2,16,128,128]{3,2,1,0:T(8,128)(2,1)}, bf16[2,16,128,128]{3,2,1,0:T(8,128)(2,1)}) custom-call(s32[104]{0:T(128)} %index_ref.15, s32[4]{0:T(128)} %pert_ref.5, s32[1]{0:T(128)} %bitcast.1.lane_ref, bf16[104,256,256]{2,1,0:T(8,128)(2,1)} %tiles.5, ...), custom_call_target="tpu_custom_call" | custom-call | tf_op jit(solution)/shard_map/pair_tiles/pallas_call | solution.py:179
  7.9 10.4 %pair_tiles.4 = (bf16[2,24,128,128]{3,2,1,0:T(8,128)(2,1)}, bf16[2,24,128,128]{3,2,1,0:T(8,128)(2,1)}, bf16[2,24,128,128]{3,2,1,0:T(8,128)(2,1)}, bf16[2,24,128,128]{3,2,1,0:T(8,128)(2,1)}) custom-call(s32[104]{0:T(128)} %index_ref.15, s32[4]{0:T(128)} %pert_ref.5, s32[1]{0:T(128)} %bitcast.1.lane_ref, bf16[104,256,256]{2,1,0:T(8,128)(2,1)} %tiles.5, ...), custom_call_target="tpu_custom_call" | custom-call | tf_op jit(solution)/shard_map/pair_tiles/pallas_call | solution.py:179
  18.3 3.0 collective-permute-start.2
  21.3 3.0 collective-permute-start.3
  24.3 0.5 collective-permute-start.4
  24.8 0.5 collective-permute-start.5
  25.3 7.7 %pair_tiles.5 = (bf16[2,16,128,128]{3,2,1,0:T(8,128)(2,1)}, bf16[2,16,128,128]{3,2,1,0:T(8,128)(2,1)}, bf16[2,16,128,128]{3,2,1,0:T(8,128)(2,1)}, bf16[2,16,128,128]{3,2,1,0:T(8,128)(2,1)}) custom-call(s32[104]{0:T(128)} %index_ref.15, s32[4]{0:T(128)} %pert_ref.5, s32[1]{0:T(128)} %bitcast.1.lane_ref, bf16[104,256,256]{2,1,0:T(8,128)(2,1)} %tiles.5, ...), custom_call_target="tpu_custom_call" | custom-call | tf_op jit(solution)/shard_map/pair_tiles/pallas_call | solution.py:179
  33.0 3.0 collective-permute-start
  36.0 38.2 %collective-permute-done.4.refs_1_.came = bf16[2,12,128,128]{3,2,1,0:T(8,128)(2,1)} collective-permute-done((bf16[2,12,128,128]{3,2,1,0:T(8,128)(2,1)}, bf16[2,12,128,128]{3,2,1,0:T(8,128)(2,1)}, u32[]{:S(2)}, u32[]{:S(2)}) %collective-permute-start.4) | collective-permute-done | bytes 786464 | tf_op jit(solution)/shard_map/ppermute | solution.py:26
  74.2 3.0 collective-permute-start.1
  77.2 13.3 %sum_rows.1._ = f32[16,256]{1,0:T(8,128)} custom-call(s32[104]{0:T(128)} %index_ref.15, bf16[2,12,128,128]{3,2,1,0:T(8,128)(2,1)} %get-tuple-element.33.rest_0_, bf16[2,12,128,128]{3,2,1,0:T(8,128)(2,1)} %get-tuple-element.34.rest_1_.refs_0_.kept, bf16[2,16,128,128]{3,2,1,0:T(8,128)(2,1)} %get-tuple-element.35.rest_2_, ...), custom_call_target="tpu_custom_call" | custom-call | tf_op jit(solution)/shard_map/sum_rows/pallas_call | solution.py:242
  90.5 1.3 copy.16
  91.8 6.0 %all-to-all-start = ((f32[16,1,256]{2,1,0:T(1,128)}), f32[16,1,256]{2,1,0:T(1,128)S(1)}, u32[]{:S(2)}, u32[]{:S(2)}) async-start(f32[16,1,256]{2,1,0:T(1,128)} %copy.16), calls=%async_computation | async-start | bytes 32768 | tf_op jit(solution)/shard_map/all_to_all | solution.py:547
  97.8 3.9 zero_buffer.1.refs_4_.refs_7_
  101.7 2.7 all-to-all-done
  104.4 0.6 copy.23
  105.0 0.0 collective-permute-done.5.refs_3_.refs_4_
  105.0 2.2 forward.3
  107.2 1.4 line_copies.1.refs_4_
  108.6 0.0 collective-permute-done.2.refs_1_
  108.6 0.0 collective-permute-done.3.refs_3_.refs_4_
  108.6 3.9 forward.4
  112.5 2.8 collective-permute-start.11
  115.4 0.7 collective-permute-start.13
  116.1 2.5 collective-permute-start.10
  118.6 0.0 collective-permute-done.refs_1_
  118.6 1.0 collective-permute-start.12
  119.6 0.0 collective-permute-done.1.refs_3_.refs_4_
  119.6 2.5 forward.5
  122.1 2.5 collective-permute-start.6
  124.6 19.3 %collective-permute-done.12.refs_2_ = bf16[8,128,128]{2,1,0:T(8,128)(2,1)} collective-permute-done((bf16[8,128,128]{2,1,0:T(8,128)(2,1)}, bf16[8,128,128]{2,1,0:T(8,128)(2,1)}, u32[]{:S(2)}, u32[]{:S(2)}) %collective-permute-start.12) | collective-permute-done | bytes 262176 | tf_op jit(solution)/shard_map/ppermute | solution.py:26
  143.9 0.8 collective-permute-start.7
  144.7 0.0 collective-permute-done.13.refs_5_
  144.7 2.7 collective-permute-start.9
  147.4 0.0 collective-permute-done.11.refs_5_
  147.4 2.2 collective-permute-start.8
  149.7 0.2 convert_reduce_fusion
  149.9 0.0 copy-done.1
  149.9 0.8 copy.17
  150.7 7.1 %all-to-all-start.1 = ((f32[128,1,256]{2,1,0:T(1,128)}), f32[128,1,256]{2,1,0:T(1,128)S(1)}, u32[]{:S(2)}, u32[]{:S(2)}) async-start(f32[128,1,256]{2,1,0:T(1,128)} %copy.17), calls=%async_computation.1 | async-start | bytes 262144 | tf_op jit(solution)/shard_map/all_to_all | solution.py:567
  157.8 0.5 multiply_add_fusion.place_ref
  158.3 8.8 %all-to-all-done.1 = f32[128,1,256]{2,1,0:T(1,128)S(1)} async-done(((f32[128,1,256]{2,1,0:T(1,128)}), f32[128,1,256]{2,1,0:T(1,128)S(1)}, u32[]{:S(2)}, u32[]{:S(2)}) %all-to-all-start.1) | async-done | bytes 131104 | tf_op jit(solution)/shard_map/all_to_all | solution.py:567
  167.1 0.7 copy.22
  167.8 2.1 join_features.1.refs_8_.refs_1_
  169.8 3.5 finish.4.refs_7_
  173.4 0.0 collective-permute-done.10.refs_2_
  173.4 5.3 finish.5.refs_7_
  178.7 0.0 collective-permute-done.9.refs_5_
  178.7 0.0 collective-permute-done.8.refs_2_
  178.7 3.2 finish.6.refs_7_
  181.9 0.0 collective-permute-done.6.refs_2_
  182.0 0.0 copy-start.2
  182.0 0.0 collective-permute-done.7.refs_5_
  182.0 0.7 copy-done.2
  182.7 3.2 finish.7
  185.9 6.2 %all-to-all-start.2 = ((bf16[256,128,128]{2,1,0:T(8,128)(2,1)}), bf16[256,128,128]{2,1,0:T(8,128)(2,1)}, u32[]{:S(2)}, u32[]{:S(2)}) async-start(bf16[256,128,128]{2,1,0:T(8,128)(2,1)} %finish.7), calls=%async_computation.2 | async-start | bytes 16777216 | tf_op jit(solution)/shard_map/all_to_all | solution.py:580
  192.2 2.9 collective-permute-start.16
  195.1 0.7 collective-permute-start.15
  195.8 0.9 collective-permute-start.14
  196.7 95.8 %collective-permute-done.16.refs_4_ = bf16[4,128,256]{2,1,0:T(8,128)(2,1)S(1)} collective-permute-done((bf16[4,128,256]{2,1,0:T(8,128)(2,1)S(1)}, bf16[4,128,256]{2,1,0:T(8,128)(2,1)S(1)}, u32[]{:S(2)}, u32[]{:S(2)}) %collective-permute-start.16) | collective-permute-done | bytes 262176 | tf_op jit(solution)/shard_map/ppermute | solution.py:576
  292.5 9.1 %collective-permute-done.15.refs_3_ = bf16[4,128,256]{2,1,0:T(8,128)(2,1)S(1)} collective-permute-done((bf16[4,128,256]{2,1,0:T(8,128)(2,1)S(1)}, bf16[4,128,256]{2,1,0:T(8,128)(2,1)S(1)}, u32[]{:S(2)}, u32[]{:S(2)}) %collective-permute-start.15) | collective-permute-done | bytes 262176 | tf_op jit(solution)/shard_map/ppermute | solution.py:576
  301.6 0.0 collective-permute-done.14.refs_2_
  301.6 0.0 all-to-all-done.2.refs_0_
  301.7 255.5 %copied.1 = (bf16[256,128,128]{2,1,0:T(8,128)(2,1)}, bf16[16,128,256]{2,1,0:T(8,128)(2,1)}) custom-call(bf16[256,128,128]{2,1,0:T(8,128)(2,1)} %all-to-all-done.2.refs_0_, bf16[4,128,256]{2,1,0:T(8,128)(2,1)S(1)} %copy-done, bf16[4,128,256]{2,1,0:T(8,128)(2,1)S(1)} %collective-permute-done.14.refs_2_, ...), custom_call_target="tpu_custom_call" | custom-call | tf_op jit(solution)/shard_map/copied/pallas_call | solution.py:489
  (6 shorter events, 0.0 us)
Async XLA Ops:
  18.3 90.4 %collective-permute-start.2 = (bf16[2,24,128,128]{3,2,1,0:T(8,128)(2,1)}, bf16[2,24,128,128]{3,2,1,0:T(8,128)(2,1)}, u32[]{:S(2)}, u32[]{:S(2)}) collective-permute-start(bf16[2,24,128,128]{3,2,1,0:T(8,128)(2,1)} %get-tuple-element.31.rest_4_), channel_id=1, source_target_pairs={{0,64},{16,80},{32,96},{48,112},{64,0},{80,16},{96,32},{112,48},{1... | collective-permute-start | bytes 4718600 | tf_op jit(solution)/shard_map/ppermute | solution.py:26
  21.3 87.3 %collective-permute-start.3 = (bf16[2,24,128,128]{3,2,1,0:T(8,128)(2,1)}, bf16[2,24,128,128]{3,2,1,0:T(8,128)(2,1)}, u32[]{:S(2)}, u32[]{:S(2)}) collective-permute-start(bf16[2,24,128,128]{3,2,1,0:T(8,128)(2,1)} %get-tuple-element.32.rest_6_), channel_id=1, source_target_pairs={{0,8},{1,9},{2,10},{3,11},{4,12},{5,13},{6,14},{7,15},{8,0},{9,1},... | collective-permute-start | bytes 4718600 | tf_op jit(solution)/shard_map/ppermute | solution.py:26
  24.3 49.9 %collective-permute-start.4 = (bf16[2,12,128,128]{3,2,1,0:T(8,128)(2,1)}, bf16[2,12,128,128]{3,2,1,0:T(8,128)(2,1)}, u32[]{:S(2)}, u32[]{:S(2)}) collective-permute-start(bf16[2,12,128,128]{3,2,1,0:T(8,128)(2,1)} %get-tuple-element.33.rest_0_), channel_id=1, source_target_pairs={{0,64},{16,80},{32,96},{48,112},{64,0},{80,16},{96,32},{112,48},{1... | collective-permute-start | bytes 2359304 | tf_op jit(solution)/shard_map/ppermute | solution.py:26
  24.8 80.2 %collective-permute-start.5 = (bf16[2,16,128,128]{3,2,1,0:T(8,128)(2,1)}, bf16[2,16,128,128]{3,2,1,0:T(8,128)(2,1)}, u32[]{:S(2)}, u32[]{:S(2)}) collective-permute-start(bf16[2,16,128,128]{3,2,1,0:T(8,128)(2,1)} %get-tuple-element.35.rest_2_), channel_id=1, source_target_pairs={{0,8},{1,9},{2,10},{3,11},{4,12},{5,13},{6,14},{7,15},{8,0},{9,1},... | collective-permute-start | bytes 3145736 | tf_op jit(solution)/shard_map/ppermute | solution.py:26
  33.0 85.6 %collective-permute-start = (bf16[2,16,128,128]{3,2,1,0:T(8,128)(2,1)}, bf16[2,16,128,128]{3,2,1,0:T(8,128)(2,1)}, u32[]{:S(2)}, u32[]{:S(2)}) collective-permute-start(bf16[2,16,128,128]{3,2,1,0:T(8,128)(2,1)} %get-tuple-element.27.rest_8_), channel_id=1, source_target_pairs={{0,64},{16,80},{32,96},{48,112},{64,0},{80,16},{96,32},{112,48},{1... | collective-permute-start | bytes 3145736 | tf_op jit(solution)/shard_map/ppermute | solution.py:26
  74.2 45.4 %collective-permute-start.1 = (bf16[2,16,128,128]{3,2,1,0:T(8,128)(2,1)}, bf16[2,16,128,128]{3,2,1,0:T(8,128)(2,1)}, u32[]{:S(2)}, u32[]{:S(2)}) collective-permute-start(bf16[2,16,128,128]{3,2,1,0:T(8,128)(2,1)} %get-tuple-element.29.rest_10_), channel_id=1, source_target_pairs={{0,8},{1,9},{2,10},{3,11},{4,12},{5,13},{6,14},{7,15},{8,0},{9,1},... | collective-permute-start | bytes 3145736 | tf_op jit(solution)/shard_map/ppermute | solution.py:26
  91.8 12.5 %all-to-all-start = ((f32[16,1,256]{2,1,0:T(1,128)}), f32[16,1,256]{2,1,0:T(1,128)S(1)}, u32[]{:S(2)}, u32[]{:S(2)}) async-start(f32[16,1,256]{2,1,0:T(1,128)} %copy.16), calls=%async_computation | async-start | bytes 32768 | tf_op jit(solution)/shard_map/all_to_all | solution.py:547
  105.0 14.6 %copy-start.3 = (s32[104,2]{0,1:T(2,128)S(1)}, s32[104,2]{0,1:T(2,128)}, u32[]{:S(2)}) copy-start(s32[104,2]{0,1:T(2,128)} %param.15) | copy-start | bytes 2500
  108.6 41.3 %copy-start.1 = (f32[128,256]{1,0:T(8,128)S(1)}, f32[128,256]{1,0:T(8,128)}, u32[]{:S(2)}) copy-start(f32[128,256]{1,0:T(8,128)} %line_copies.1.refs_4_) | copy-start | bytes 393220
  112.5 34.9 %collective-permute-start.11 = (bf16[24,128,128]{2,1,0:T(8,128)(2,1)}, bf16[24,128,128]{2,1,0:T(8,128)(2,1)}, u32[]{:S(2)}, u32[]{:S(2)}) collective-permute-start(bf16[24,128,128]{2,1,0:T(8,128)(2,1)} %get-tuple-element.42), channel_id=1, source_target_pairs={{0,64},{16,80},{32,96},{48,112},{64,0},{80,16},{96,32},{112,48},{1... | collective-permute-start | bytes 2359304 | tf_op jit(solution)/shard_map/ppermute | solution.py:26
  115.4 29.3 %collective-permute-start.13 = (bf16[16,128,128]{2,1,0:T(8,128)(2,1)}, bf16[16,128,128]{2,1,0:T(8,128)(2,1)}, u32[]{:S(2)}, u32[]{:S(2)}) collective-permute-start(bf16[16,128,128]{2,1,0:T(8,128)(2,1)} %get-tuple-element.43), channel_id=1, source_target_pairs={{0,64},{16,80},{32,96},{48,112},{64,0},{80,16},{96,32},{112,48},{1... | collective-permute-start | bytes 1572872 | tf_op jit(solution)/shard_map/ppermute | solution.py:26
  116.1 57.3 %collective-permute-start.10 = (bf16[24,128,128]{2,1,0:T(8,128)(2,1)}, bf16[24,128,128]{2,1,0:T(8,128)(2,1)}, u32[]{:S(2)}, u32[]{:S(2)}) collective-permute-start(bf16[24,128,128]{2,1,0:T(8,128)(2,1)} %get-tuple-element.37.refs_4_), channel_id=1, source_target_pairs={{0,8},{1,9},{2,10},{3,11},{4,12},{5,13},{6,14},{7,15},{8,0},{9,1},... | collective-permute-start | bytes 2359304 | tf_op jit(solution)/shard_map/ppermute | solution.py:26
  118.6 25.4 %collective-permute-start.12 = (bf16[8,128,128]{2,1,0:T(8,128)(2,1)}, bf16[8,128,128]{2,1,0:T(8,128)(2,1)}, u32[]{:S(2)}, u32[]{:S(2)}) collective-permute-start(bf16[8,128,128]{2,1,0:T(8,128)(2,1)} %get-tuple-element.36._), channel_id=1, source_target_pairs={{0,8},{1,9},{2,10},{3,11},{4,12},{5,13},{6,14},{7,15},{8,0},{9,1},... | collective-permute-start | bytes 786440 | tf_op jit(solution)/shard_map/ppermute | solution.py:26
  122.1 59.9 %collective-permute-start.6 = (bf16[16,64,128]{2,1,0:T(8,128)(2,1)}, bf16[16,64,128]{2,1,0:T(8,128)(2,1)S(1)}, u32[]{:S(2)}, u32[]{:S(2)}) collective-permute-start(bf16[16,64,128]{2,1,0:T(8,128)(2,1)} %get-tuple-element.38), channel_id=1, source_target_pairs={{0,8},{1,9},{2,10},{3,11},{4,12},{5,13},{6,14},{7,15},{8,0},{9,1},... | collective-permute-start | bytes 786440 | tf_op jit(solution)/shard_map/ppermute | solution.py:26
  143.9 38.1 %collective-permute-start.7 = (bf16[16,64,128]{2,1,0:T(8,128)(2,1)}, bf16[16,64,128]{2,1,0:T(8,128)(2,1)}, u32[]{:S(2)}, u32[]{:S(2)}) collective-permute-start(bf16[16,64,128]{2,1,0:T(8,128)(2,1)} %get-tuple-element.39), channel_id=1, source_target_pairs={{0,64},{16,80},{32,96},{48,112},{64,0},{80,16},{96,32},{112,48},{1... | collective-permute-start | bytes 786440 | tf_op jit(solution)/shard_map/ppermute | solution.py:26
  144.7 34.0 %collective-permute-start.9 = (bf16[16,64,128]{2,1,0:T(8,128)(2,1)}, bf16[16,64,128]{2,1,0:T(8,128)(2,1)}, u32[]{:S(2)}, u32[]{:S(2)}) collective-permute-start(bf16[16,64,128]{2,1,0:T(8,128)(2,1)} %get-tuple-element.41), channel_id=1, source_target_pairs={{0,64},{16,80},{32,96},{48,112},{64,0},{80,16},{96,32},{112,48},{1... | collective-permute-start | bytes 786440 | tf_op jit(solution)/shard_map/ppermute | solution.py:26
  147.4 31.3 %collective-permute-start.8 = (bf16[16,64,128]{2,1,0:T(8,128)(2,1)}, bf16[16,64,128]{2,1,0:T(8,128)(2,1)}, u32[]{:S(2)}, u32[]{:S(2)}) collective-permute-start(bf16[16,64,128]{2,1,0:T(8,128)(2,1)} %get-tuple-element.40._), channel_id=1, source_target_pairs={{0,8},{1,9},{2,10},{3,11},{4,12},{5,13},{6,14},{7,15},{8,0},{9,1},... | collective-permute-start | bytes 786440 | tf_op jit(solution)/shard_map/ppermute | solution.py:26
  150.7 16.4 %all-to-all-start.1 = ((f32[128,1,256]{2,1,0:T(1,128)}), f32[128,1,256]{2,1,0:T(1,128)S(1)}, u32[]{:S(2)}, u32[]{:S(2)}) async-start(f32[128,1,256]{2,1,0:T(1,128)} %copy.17), calls=%async_computation.1 | async-start | bytes 262144 | tf_op jit(solution)/shard_map/all_to_all | solution.py:567
  182.0 0.7 copy-start.2
  185.9 6.3 %copy-start = (bf16[4,128,256]{2,1,0:T(8,128)(2,1)S(1)}, bf16[4,128,256]{2,1,0:T(8,128)(2,1)}, u32[]{:S(2)}) copy-start(bf16[4,128,256]{2,1,0:T(8,128)(2,1)} %join_features.1.refs_8_.refs_1_) | copy-start | bytes 786436
  185.9 115.8 %all-to-all-start.2 = ((bf16[256,128,128]{2,1,0:T(8,128)(2,1)}), bf16[256,128,128]{2,1,0:T(8,128)(2,1)}, u32[]{:S(2)}, u32[]{:S(2)}) async-start(bf16[256,128,128]{2,1,0:T(8,128)(2,1)} %finish.7), calls=%async_computation.2 | async-start | bytes 16777216 | tf_op jit(solution)/shard_map/all_to_all | solution.py:580
  192.2 100.3 %collective-permute-start.16 = (bf16[4,128,256]{2,1,0:T(8,128)(2,1)S(1)}, bf16[4,128,256]{2,1,0:T(8,128)(2,1)S(1)}, u32[]{:S(2)}, u32[]{:S(2)}) collective-permute-start(bf16[4,128,256]{2,1,0:T(8,128)(2,1)S(1)} %copy-done), channel_id=1, source_target_pairs={{0,3},{1,0},{2,1},{3,2},{4,7},{5,4},{6,5},{7,6},{8,11},{9,8},{10,9... | collective-permute-start | bytes 786440 | tf_op jit(solution)/shard_map/ppermute | solution.py:576
  195.1 106.5 %collective-permute-start.15 = (bf16[4,128,256]{2,1,0:T(8,128)(2,1)S(1)}, bf16[4,128,256]{2,1,0:T(8,128)(2,1)S(1)}, u32[]{:S(2)}, u32[]{:S(2)}) collective-permute-start(bf16[4,128,256]{2,1,0:T(8,128)(2,1)S(1)} %copy-done), channel_id=1, source_target_pairs={{0,2},{1,3},{2,0},{3,1},{4,6},{5,7},{6,4},{7,5},{8,10},{9,11},{10,... | collective-permute-start | bytes 786440 | tf_op jit(solution)/shard_map/ppermute | solution.py:576
  195.8 105.8 %collective-permute-start.14 = (bf16[4,128,256]{2,1,0:T(8,128)(2,1)S(1)}, bf16[4,128,256]{2,1,0:T(8,128)(2,1)S(1)}, u32[]{:S(2)}, u32[]{:S(2)}) collective-permute-start(bf16[4,128,256]{2,1,0:T(8,128)(2,1)S(1)} %copy-done), channel_id=1, source_target_pairs={{0,1},{1,2},{2,3},{3,0},{4,5},{5,6},{6,7},{7,4},{8,9},{9,10},{10,1... | collective-permute-start | bytes 786440 | tf_op jit(solution)/shard_map/ppermute | solution.py:576

commit v7 on v6

--- a/solution.py
+++ b/solution.py
@@ -13,8 +13,8 @@
 STEP = 8
 LANES = 4
 ROW_FIRST = 48
-CHUNKS = (8, 16), (24, 24), (16, 16)
-SPLITS = 1, 1, 2
+CHUNKS = (8, 8), (8, 16), (16, 16), (16, 16)
+SPLITS = 1, 1, 1, 1
 BF16 = jnp.bfloat16
 F32 = jnp.float32
 PARAMS = pltpu.CompilerParams(vmem_limit_bytes=66_500_000)
@@ -555,14 +555,14 @@
     token = buffer
     for chunk, pair in enumerate(pairs):
         splits = SPLITS[chunk]
-        given = forward(pair, splits, [token])
+        given = forward(pair, splits, [token, place] if chunk == 0 else [token])
         token = given[0]
         for kind in range(2):
             pair[kind]["last"] = []
             for h in range(splits):
                 last = flipped(given[kind * splits + h], *masks[1 - kind])
                 pair[kind]["last"].append(last)
-        if chunk == 0:
+        if chunk == 1:
             token = line_copies(spread, devices, token)
             raw = lax.all_to_all(token, ("row", "col"), split_axis=0, concat_axis=0, tiled=True)
 

time: 562 us -> 544 us (0.968)
  waiting for transfers between devices: 174 us -> 105 us
  blocking collectives: 0 us -> 61.9 us
  starting transfers between devices: 52.3 us -> 40.8 us
    all_to_all x0 -> x2, blocking collectives: none -> 61.9 us  [the longest x1 31.8 us: level(): lax.all_to_all(token, ('row', 'col'), split_axis=0, concat_axis=0, tiled=...]
    ppermute x14 -> x16, waiting for transfers between devices: 57.5 us -> 0.04 us  [flipped(): return lax.ppermute(value, axis, pairs)]
    all_to_all x2 -> x0, starting transfers between devices: 13.1 us -> none  [the longest x1 7.08 us: level(): lax.all_to_all(token, ('row', 'col'), split_axis=0, concat_axis=0, tiled=...]
    all_to_all x2 -> x0, waiting for transfers between devices: 11.5 us -> none  [the longest x1 8.81 us: level(): lax.all_to_all(token, ('row', 'col'), split_axis=0, concat_axis=0, tiled=...]
    pallas_call x3 -> x4, Pallas kernels: 25.3 us -> 28.5 us  [pair_tiles(): pl.pallas_call(functools.partial(pair_kernel, starts, counts, with_featur...]
    ppermute x14 -> x16, starting transfers between devices: 28.4 us -> 29.9 us  [flipped(): return lax.ppermute(value, axis, pairs)]
  transfers between devices with their start and end apart: 20 -> 20, of which waited for: 6 -> 2; matrix products, arithmetic and copies ran while one was open for 1% -> 0% of each run, Pallas kernels for 9% -> 12%
where the time goes in v7:
time: 544 us; the launch traced here: 540 us
  Pallas kernels  329 us (60%)
  waiting for transfers between devices  105 us (19%)
  blocking collectives  61.9 us (11%)
  starting transfers between devices  40.8 us (7%)
    pallas_call x1, Pallas kernels, copied(): pl.pallas_call(functools.partial(copy_kernel, pieces), out_shape=[jax.Sha...  256 us
    ppermute x3, waiting for transfers between devices, level(): shared.append(lax.ppermute(joined, 'col', ring))  105 us
    all_to_all x1, blocking collectives, level(): lax.all_to_all(token, ('row', 'col'), split_axis=0, concat_axis=0, tiled=...  31.8 us
    all_to_all x1, blocking collectives, level(): spread = lax.all_to_all(own, 'col', split_axis=0, concat_axis=0, tiled=True)  30 us
    ppermute x16, starting transfers between devices, flipped(): return lax.ppermute(value, axis, pairs)  29.9 us
    pallas_call x4, Pallas kernels, pair_tiles(): pl.pallas_call(functools.partial(pair_kernel, starts, counts, with_featur...  28.5 us
    pallas_call x4, Pallas kernels, finish(): pl.pallas_call(functools.partial(finish_kernel, starts, counts, h), out_s...  14.5 us
    pallas_call x1, Pallas kernels, sum_rows(): pl.pallas_call(functools.partial(sum_kernel, bounds, tiles_col), out_shap...  14 us
  transfers between devices with their start and end apart: 20, of which 2 were waited for; matrix products, arithmetic and copies ran while one was open for 0% of the time, Pallas kernels for 12%

profile of v7, /device:TPU:32, one launch (start us, length us, event | category | flops | bytes accessed | tf_op | source)
XLA Modules:
  0.0 539.8 jit_solution(174720719053725137)
XLA Ops:
  0.6 6.2 %pair_tiles.4 = (bf16[2,12,128,128]{3,2,1,0:T(8,128)(2,1)}, bf16[2,12,128,128]{3,2,1,0:T(8,128)(2,1)}, bf16[2,8,128,128]{3,2,1,0:T(8,128)(2,1)}, bf16[2,8,128,128]{3,2,1,0:T(8,128)(2,1)}) custom-call(s32[104]{0:T(128)} %index_ref.17, s32[4]{0:T(128)} %pert_ref.7, s32[1]{0:T(128)} %bitcast.1.lane_ref, bf16[104,256,256]{2,1,0:T(8,128)(2,1)} %tiles.7, ...), custom_call_target="tpu_custom_call" | custom-call | tf_op jit(solution)/shard_map/pair_tiles/pallas_call | solution.py:179
  6.9 2.8 collective-permute-start.6
  9.7 2.8 collective-permute-start.7
  12.4 6.5 %pair_tiles.5 = (bf16[2,8,128,128]{3,2,1,0:T(8,128)(2,1)}, bf16[2,8,128,128]{3,2,1,0:T(8,128)(2,1)}, bf16[2,16,128,128]{3,2,1,0:T(8,128)(2,1)}, bf16[2,16,128,128]{3,2,1,0:T(8,128)(2,1)}) custom-call(s32[104]{0:T(128)} %index_ref.17, s32[4]{0:T(128)} %pert_ref.7, s32[1]{0:T(128)} %bitcast.1.lane_ref, bf16[104,256,256]{2,1,0:T(8,128)(2,1)} %tiles.7, ...), custom_call_target="tpu_custom_call" | custom-call | tf_op jit(solution)/shard_map/pair_tiles/pallas_call | solution.py:179
  19.0 0.7 collective-permute-start.4
  19.7 1.1 collective-permute-start.5
  20.8 8.0 %pair_tiles.6 = (bf16[2,16,128,128]{3,2,1,0:T(8,128)(2,1)}, bf16[2,16,128,128]{3,2,1,0:T(8,128)(2,1)}, bf16[2,16,128,128]{3,2,1,0:T(8,128)(2,1)}, bf16[2,16,128,128]{3,2,1,0:T(8,128)(2,1)}) custom-call(s32[104]{0:T(128)} %index_ref.17, s32[4]{0:T(128)} %pert_ref.7, s32[1]{0:T(128)} %bitcast.1.lane_ref, bf16[104,256,256]{2,1,0:T(8,128)(2,1)} %tiles.7, ...), custom_call_target="tpu_custom_call" | custom-call | tf_op jit(solution)/shard_map/pair_tiles/pallas_call | solution.py:179
  28.8 2.3 collective-permute-start.2
  31.2 0.0 collective-permute-done.7.refs_3_.refs_4_
  31.2 2.6 collective-permute-start.3
  33.7 7.7 %pair_tiles.7 = (bf16[2,16,128,128]{3,2,1,0:T(8,128)(2,1)}, bf16[2,16,128,128]{3,2,1,0:T(8,128)(2,1)}, bf16[2,16,128,128]{3,2,1,0:T(8,128)(2,1)}, bf16[2,16,128,128]{3,2,1,0:T(8,128)(2,1)}) custom-call(s32[104]{0:T(128)} %index_ref.17, s32[4]{0:T(128)} %pert_ref.7, s32[1]{0:T(128)} %bitcast.1.lane_ref, bf16[104,256,256]{2,1,0:T(8,128)(2,1)} %tiles.7, ...), custom_call_target="tpu_custom_call" | custom-call | tf_op jit(solution)/shard_map/pair_tiles/pallas_call | solution.py:179
  41.4 0.0 collective-permute-done.4.refs_1_
  41.4 1.7 collective-permute-start
  43.1 0.0 collective-permute-done.6.refs_1_.came
  43.1 2.8 collective-permute-start.1
  45.9 14.0 %sum_rows.1._ = f32[16,256]{1,0:T(8,128)} custom-call(s32[104]{0:T(128)} %index_ref.17, bf16[2,12,128,128]{3,2,1,0:T(8,128)(2,1)} %get-tuple-element.38.rest_0_, bf16[2,12,128,128]{3,2,1,0:T(8,128)(2,1)} %get-tuple-element.39.rest_1_.refs_0_.kept, bf16[2,8,128,128]{3,2,1,0:T(8,128)(2,1)} %get-tuple-element.40.rest_2_, ...), custom_call_target="tpu_custom_call" | custom-call | tf_op jit(solution)/shard_map/sum_rows/pallas_call | solution.py:242
  59.9 3.9 zero_buffer.1.refs_4_.refs_7_
  63.8 0.2 convert_reduce_fusion
  64.0 0.6 multiply_add_fusion.refs_5_.place_ref
  64.5 2.0 forward.4
  66.6 0.0 collective-permute-done.5.refs_3_.refs_4_
  66.6 0.5 collective-permute-start.15
  67.1 2.2 forward.5
  69.3 0.0 collective-permute-done.2.refs_1_
  69.3 2.2 collective-permute-start.14
  71.6 0.0 collective-permute-done.3.refs_3_.refs_4_
  71.6 2.4 collective-permute-start.12
  74.0 30.0 %all_to_all.27 = f32[16,1,256]{2,1,0:T(1,128)S(1)} all-to-all(f32[16,1,256]{2,1,0:T(1,128)S(1)} %copy.16), channel_id=1, replica_groups=mesh['row'=8,'col'=16] {'col'}, dimensions={0} | all-to-all | bytes 32768 | tf_op jit(solution)/shard_map/all_to_all | solution.py:547
  104.0 0.6 copy.23
  104.6 1.4 line_copies.1.refs_4_
  106.0 2.5 forward.6
  108.5 0.0 collective-permute-done.refs_1_
  108.5 0.9 collective-permute-start.13
  109.3 0.0 collective-permute-done.1.refs_3_.refs_4_
  109.3 2.3 collective-permute-start.10
  111.7 2.4 forward.7
  114.1 0.0 collective-permute-done.15.refs_5_
  114.1 2.9 collective-permute-start.11
  117.0 0.0 collective-permute-done.14.refs_2_
  117.0 0.7 collective-permute-start.9
  117.7 0.0 collective-permute-done.12.refs_2_
  117.7 1.2 collective-permute-start.8
  118.9 0.1 copy.17
  119.1 31.8 %all_to_all.28 = f32[128,1,256]{2,1,0:T(1,128)S(1)} all-to-all(f32[128,1,256]{2,1,0:T(1,128)S(1)} %copy.17), channel_id=1, replica_groups=mesh['row'=8,'col'=16] {'row','col'}, dimensions={0} | all-to-all | bytes 262144 | tf_op jit(solution)/shard_map/all_to_all | solution.py:567
  150.9 0.7 copy.22
  151.6 2.1 join_features.1.refs_8_.refs_1_
  153.6 3.3 finish.4.refs_7_
  157.0 0.0 collective-permute-done.13.refs_5_
  157.0 3.6 finish.5.refs_7_
  160.6 0.0 collective-permute-done.11.refs_5_
  160.6 0.0 collective-permute-done.10.refs_2_
  160.6 3.8 finish.6.refs_7_
  164.4 0.0 collective-permute-done.9.refs_5_
  164.4 0.0 collective-permute-done.8.refs_2_
  164.4 3.8 finish.7
  168.2 6.3 %all-to-all-start.2 = ((bf16[256,128,128]{2,1,0:T(8,128)(2,1)}), bf16[256,128,128]{2,1,0:T(8,128)(2,1)}, u32[]{:S(2)}, u32[]{:S(2)}) async-start(bf16[256,128,128]{2,1,0:T(8,128)(2,1)} %finish.7), calls=%async_computation.2 | async-start | bytes 16777216 | tf_op jit(solution)/shard_map/all_to_all | solution.py:580
  174.6 2.9 collective-permute-start.18
  177.5 0.7 collective-permute-start.17
  178.2 0.9 collective-permute-start.16
  179.2 95.8 %collective-permute-done.18.refs_4_ = bf16[4,128,256]{2,1,0:T(8,128)(2,1)S(1)} collective-permute-done((bf16[4,128,256]{2,1,0:T(8,128)(2,1)S(1)}, bf16[4,128,256]{2,1,0:T(8,128)(2,1)S(1)}, u32[]{:S(2)}, u32[]{:S(2)}) %collective-permute-start.18) | collective-permute-done | bytes 262176 | tf_op jit(solution)/shard_map/ppermute | solution.py:576
  274.9 9.1 %collective-permute-done.17.refs_3_ = bf16[4,128,256]{2,1,0:T(8,128)(2,1)S(1)} collective-permute-done((bf16[4,128,256]{2,1,0:T(8,128)(2,1)S(1)}, bf16[4,128,256]{2,1,0:T(8,128)(2,1)S(1)}, u32[]{:S(2)}, u32[]{:S(2)}) %collective-permute-start.17) | collective-permute-done | bytes 262176 | tf_op jit(solution)/shard_map/ppermute | solution.py:576
  284.1 0.0 collective-permute-done.16.refs_2_
  284.1 0.0 all-to-all-done.2.refs_0_
  284.1 255.5 %copied.1 = (bf16[256,128,128]{2,1,0:T(8,128)(2,1)}, bf16[16,128,256]{2,1,0:T(8,128)(2,1)}) custom-call(bf16[256,128,128]{2,1,0:T(8,128)(2,1)} %all-to-all-done.2.refs_0_, bf16[4,128,256]{2,1,0:T(8,128)(2,1)S(1)} %copy-done, bf16[4,128,256]{2,1,0:T(8,128)(2,1)S(1)} %collective-permute-done.16.refs_2_, ...), custom_call_target="tpu_custom_call" | custom-call | tf_op jit(solution)/shard_map/copied/pallas_call | solution.py:489
  (14 shorter events, 0.0 us)
Async XLA Ops:
  6.9 36.3 %collective-permute-start.6 = (bf16[2,12,128,128]{3,2,1,0:T(8,128)(2,1)}, bf16[2,12,128,128]{3,2,1,0:T(8,128)(2,1)}, u32[]{:S(2)}, u32[]{:S(2)}) collective-permute-start(bf16[2,12,128,128]{3,2,1,0:T(8,128)(2,1)} %get-tuple-element.38.rest_0_), channel_id=1, source_target_pairs={{0,64},{16,80},{32,96},{48,112},{64,0},{80,16},{96,32},{112,48},{1... | collective-permute-start | bytes 2359304 | tf_op jit(solution)/shard_map/ppermute | solution.py:26
  9.7 21.5 %collective-permute-start.7 = (bf16[2,8,128,128]{3,2,1,0:T(8,128)(2,1)}, bf16[2,8,128,128]{3,2,1,0:T(8,128)(2,1)S(1)}, u32[]{:S(2)}, u32[]{:S(2)}) collective-permute-start(bf16[2,8,128,128]{3,2,1,0:T(8,128)(2,1)} %get-tuple-element.40.rest_2_), channel_id=1, source_target_pairs={{0,8},{1,9},{2,10},{3,11},{4,12},{5,13},{6,14},{7,15},{8,0},{9,1},... | collective-permute-start | bytes 1572872 | tf_op jit(solution)/shard_map/ppermute | solution.py:26
  19.0 22.5 %collective-permute-start.4 = (bf16[2,8,128,128]{3,2,1,0:T(8,128)(2,1)}, bf16[2,8,128,128]{3,2,1,0:T(8,128)(2,1)}, u32[]{:S(2)}, u32[]{:S(2)}) collective-permute-start(bf16[2,8,128,128]{3,2,1,0:T(8,128)(2,1)} %get-tuple-element.41.rest_4_), channel_id=1, source_target_pairs={{0,64},{16,80},{32,96},{48,112},{64,0},{80,16},{96,32},{112,48},{1... | collective-permute-start | bytes 1572872 | tf_op jit(solution)/shard_map/ppermute | solution.py:26
  19.7 46.9 %collective-permute-start.5 = (bf16[2,16,128,128]{3,2,1,0:T(8,128)(2,1)}, bf16[2,16,128,128]{3,2,1,0:T(8,128)(2,1)}, u32[]{:S(2)}, u32[]{:S(2)}) collective-permute-start(bf16[2,16,128,128]{3,2,1,0:T(8,128)(2,1)} %get-tuple-element.43.rest_6_), channel_id=1, source_target_pairs={{0,8},{1,9},{2,10},{3,11},{4,12},{5,13},{6,14},{7,15},{8,0},{9,1},... | collective-permute-start | bytes 3145736 | tf_op jit(solution)/shard_map/ppermute | solution.py:26
  28.8 40.5 %collective-permute-start.2 = (bf16[2,16,128,128]{3,2,1,0:T(8,128)(2,1)}, bf16[2,16,128,128]{3,2,1,0:T(8,128)(2,1)}, u32[]{:S(2)}, u32[]{:S(2)}) collective-permute-start(bf16[2,16,128,128]{3,2,1,0:T(8,128)(2,1)} %get-tuple-element.36.rest_8_), channel_id=1, source_target_pairs={{0,64},{16,80},{32,96},{48,112},{64,0},{80,16},{96,32},{112,48},{1... | collective-permute-start | bytes 3145736 | tf_op jit(solution)/shard_map/ppermute | solution.py:26
  31.2 28.7 %copy-start.1 = (bf16[2,8,128,128]{3,2,1,0:T(8,128)(2,1)}, bf16[2,8,128,128]{3,2,1,0:T(8,128)(2,1)S(1)}, u32[]{:S(2)}) copy-start(bf16[2,8,128,128]{3,2,1,0:T(8,128)(2,1)S(1)} %collective-permute-done.7.refs_3_.refs_4_) | copy-start | bytes 1572868
  31.2 40.4 %collective-permute-start.3 = (bf16[2,16,128,128]{3,2,1,0:T(8,128)(2,1)}, bf16[2,16,128,128]{3,2,1,0:T(8,128)(2,1)}, u32[]{:S(2)}, u32[]{:S(2)}) collective-permute-start(bf16[2,16,128,128]{3,2,1,0:T(8,128)(2,1)} %get-tuple-element.37.rest_10_), channel_id=1, source_target_pairs={{0,8},{1,9},{2,10},{3,11},{4,12},{5,13},{6,14},{7,15},{8,0},{9,1},... | collective-permute-start | bytes 3145736 | tf_op jit(solution)/shard_map/ppermute | solution.py:26
  41.4 67.0 %collective-permute-start = (bf16[2,16,128,128]{3,2,1,0:T(8,128)(2,1)}, bf16[2,16,128,128]{3,2,1,0:T(8,128)(2,1)}, u32[]{:S(2)}, u32[]{:S(2)}) collective-permute-start(bf16[2,16,128,128]{3,2,1,0:T(8,128)(2,1)} %get-tuple-element.32.rest_12_), channel_id=1, source_target_pairs={{0,64},{16,80},{32,96},{48,112},{64,0},{80,16},{96,32},{112,48},{1... | collective-permute-start | bytes 3145736 | tf_op jit(solution)/shard_map/ppermute | solution.py:26
  43.1 66.2 %collective-permute-start.1 = (bf16[2,16,128,128]{3,2,1,0:T(8,128)(2,1)}, bf16[2,16,128,128]{3,2,1,0:T(8,128)(2,1)}, u32[]{:S(2)}, u32[]{:S(2)}) collective-permute-start(bf16[2,16,128,128]{3,2,1,0:T(8,128)(2,1)} %get-tuple-element.34.rest_14_), channel_id=1, source_target_pairs={{0,8},{1,9},{2,10},{3,11},{4,12},{5,13},{6,14},{7,15},{8,0},{9,1},... | collective-permute-start | bytes 3145736 | tf_op jit(solution)/shard_map/ppermute | solution.py:26
  45.9 17.9 %copy-start.5 = (s32[104,2]{0,1:T(2,128)S(1)}, s32[104,2]{0,1:T(2,128)}, u32[]{:S(2)}) copy-start(s32[104,2]{0,1:T(2,128)} %param.15) | copy-start | bytes 2500
  63.8 10.2 %copy-start.4 = (f32[16,256]{1,0:T(8,128)S(1)}, f32[16,256]{1,0:T(8,128)}, u32[]{:S(2)}) copy-start(f32[16,256]{1,0:T(8,128)} %sum_rows.1._) | copy-start | bytes 49156
  66.6 47.5 %collective-permute-start.15 = (bf16[8,128,128]{2,1,0:T(8,128)(2,1)}, bf16[8,128,128]{2,1,0:T(8,128)(2,1)S(1)}, u32[]{:S(2)}, u32[]{:S(2)}) collective-permute-start(bf16[8,128,128]{2,1,0:T(8,128)(2,1)} %get-tuple-element.51), channel_id=1, source_target_pairs={{0,64},{16,80},{32,96},{48,112},{64,0},{80,16},{96,32},{112,48},{1... | collective-permute-start | bytes 786440 | tf_op jit(solution)/shard_map/ppermute | solution.py:26
  69.3 47.7 %collective-permute-start.14 = (bf16[8,128,128]{2,1,0:T(8,128)(2,1)}, bf16[8,128,128]{2,1,0:T(8,128)(2,1)}, u32[]{:S(2)}, u32[]{:S(2)}) collective-permute-start(bf16[8,128,128]{2,1,0:T(8,128)(2,1)} %get-tuple-element.44.refs_4_), channel_id=1, source_target_pairs={{0,8},{1,9},{2,10},{3,11},{4,12},{5,13},{6,14},{7,15},{8,0},{9,1},... | collective-permute-start | bytes 786440 | tf_op jit(solution)/shard_map/ppermute | solution.py:26
  71.6 46.2 %collective-permute-start.12 = (bf16[8,128,128]{2,1,0:T(8,128)(2,1)}, bf16[8,128,128]{2,1,0:T(8,128)(2,1)}, u32[]{:S(2)}, u32[]{:S(2)}) collective-permute-start(bf16[8,128,128]{2,1,0:T(8,128)(2,1)} %get-tuple-element.45._), channel_id=1, source_target_pairs={{0,8},{1,9},{2,10},{3,11},{4,12},{5,13},{6,14},{7,15},{8,0},{9,1},... | collective-permute-start | bytes 786440 | tf_op jit(solution)/shard_map/ppermute | solution.py:26
  106.0 12.9 %copy-start.2 = (f32[128,256]{1,0:T(8,128)S(1)}, f32[128,256]{1,0:T(8,128)}, u32[]{:S(2)}) copy-start(f32[128,256]{1,0:T(8,128)} %line_copies.1.refs_4_) | copy-start | bytes 393220
  108.5 48.5 %collective-permute-start.13 = (bf16[16,128,128]{2,1,0:T(8,128)(2,1)}, bf16[16,128,128]{2,1,0:T(8,128)(2,1)}, u32[]{:S(2)}, u32[]{:S(2)}) collective-permute-start(bf16[16,128,128]{2,1,0:T(8,128)(2,1)} %get-tuple-element.50), channel_id=1, source_target_pairs={{0,64},{16,80},{32,96},{48,112},{64,0},{80,16},{96,32},{112,48},{1... | collective-permute-start | bytes 1572872 | tf_op jit(solution)/shard_map/ppermute | solution.py:26
  109.3 51.3 %collective-permute-start.10 = (bf16[16,128,128]{2,1,0:T(8,128)(2,1)}, bf16[16,128,128]{2,1,0:T(8,128)(2,1)}, u32[]{:S(2)}, u32[]{:S(2)}) collective-permute-start(bf16[16,128,128]{2,1,0:T(8,128)(2,1)} %get-tuple-element.46.refs_4_), channel_id=1, source_target_pairs={{0,8},{1,9},{2,10},{3,11},{4,12},{5,13},{6,14},{7,15},{8,0},{9,1},... | collective-permute-start | bytes 1572872 | tf_op jit(solution)/shard_map/ppermute | solution.py:26
  114.1 39.5 %copy-start.3 = (bf16[8,128,128]{2,1,0:T(8,128)(2,1)}, bf16[8,128,128]{2,1,0:T(8,128)(2,1)S(1)}, u32[]{:S(2)}) copy-start(bf16[8,128,128]{2,1,0:T(8,128)(2,1)S(1)} %collective-permute-done.15.refs_5_) | copy-start | bytes 786436
  114.1 46.5 %collective-permute-start.11 = (bf16[16,128,128]{2,1,0:T(8,128)(2,1)}, bf16[16,128,128]{2,1,0:T(8,128)(2,1)}, u32[]{:S(2)}, u32[]{:S(2)}) collective-permute-start(bf16[16,128,128]{2,1,0:T(8,128)(2,1)} %get-tuple-element.49), channel_id=1, source_target_pairs={{0,64},{16,80},{32,96},{48,112},{64,0},{80,16},{96,32},{112,48},{1... | collective-permute-start | bytes 1572872 | tf_op jit(solution)/shard_map/ppermute | solution.py:26
  117.0 47.4 %collective-permute-start.9 = (bf16[16,128,128]{2,1,0:T(8,128)(2,1)}, bf16[16,128,128]{2,1,0:T(8,128)(2,1)}, u32[]{:S(2)}, u32[]{:S(2)}) collective-permute-start(bf16[16,128,128]{2,1,0:T(8,128)(2,1)} %get-tuple-element.48), channel_id=1, source_target_pairs={{0,64},{16,80},{32,96},{48,112},{64,0},{80,16},{96,32},{112,48},{1... | collective-permute-start | bytes 1572872 | tf_op jit(solution)/shard_map/ppermute | solution.py:26
  117.7 46.7 %collective-permute-start.8 = (bf16[16,128,128]{2,1,0:T(8,128)(2,1)}, bf16[16,128,128]{2,1,0:T(8,128)(2,1)}, u32[]{:S(2)}, u32[]{:S(2)}) collective-permute-start(bf16[16,128,128]{2,1,0:T(8,128)(2,1)} %get-tuple-element.47._), channel_id=1, source_target_pairs={{0,8},{1,9},{2,10},{3,11},{4,12},{5,13},{6,14},{7,15},{8,0},{9,1},... | collective-permute-start | bytes 1572872 | tf_op jit(solution)/shard_map/ppermute | solution.py:26
  168.2 6.3 %copy-start = (bf16[4,128,256]{2,1,0:T(8,128)(2,1)S(1)}, bf16[4,128,256]{2,1,0:T(8,128)(2,1)}, u32[]{:S(2)}) copy-start(bf16[4,128,256]{2,1,0:T(8,128)(2,1)} %join_features.1.refs_8_.refs_1_) | copy-start | bytes 786436
  168.2 115.8 %all-to-all-start.2 = ((bf16[256,128,128]{2,1,0:T(8,128)(2,1)}), bf16[256,128,128]{2,1,0:T(8,128)(2,1)}, u32[]{:S(2)}, u32[]{:S(2)}) async-start(bf16[256,128,128]{2,1,0:T(8,128)(2,1)} %finish.7), calls=%async_computation.2 | async-start | bytes 16777216 | tf_op jit(solution)/shard_map/all_to_all | solution.py:580
  174.6 100.3 %collective-permute-start.18 = (bf16[4,128,256]{2,1,0:T(8,128)(2,1)S(1)}, bf16[4,128,256]{2,1,0:T(8,128)(2,1)S(1)}, u32[]{:S(2)}, u32[]{:S(2)}) collective-permute-start(bf16[4,128,256]{2,1,0:T(8,128)(2,1)S(1)} %copy-done), channel_id=1, source_target_pairs={{0,3},{1,0},{2,1},{3,2},{4,7},{5,4},{6,5},{7,6},{8,11},{9,8},{10,9... | collective-permute-start | bytes 786440 | tf_op jit(solution)/shard_map/ppermute | solution.py:576
  177.5 106.5 %collective-permute-start.17 = (bf16[4,128,256]{2,1,0:T(8,128)(2,1)S(1)}, bf16[4,128,256]{2,1,0:T(8,128)(2,1)S(1)}, u32[]{:S(2)}, u32[]{:S(2)}) collective-permute-start(bf16[4,128,256]{2,1,0:T(8,128)(2,1)S(1)} %copy-done), channel_id=1, source_target_pairs={{0,2},{1,3},{2,0},{3,1},{4,6},{5,7},{6,4},{7,5},{8,10},{9,11},{10,... | collective-permute-start | bytes 786440 | tf_op jit(solution)/shard_map/ppermute | solution.py:576
  178.2 105.8 %collective-permute-start.16 = (bf16[4,128,256]{2,1,0:T(8,128)(2,1)S(1)}, bf16[4,128,256]{2,1,0:T(8,128)(2,1)S(1)}, u32[]{:S(2)}, u32[]{:S(2)}) collective-permute-start(bf16[4,128,256]{2,1,0:T(8,128)(2,1)S(1)} %copy-done), channel_id=1, source_target_pairs={{0,1},{1,2},{2,3},{3,0},{4,5},{5,6},{6,7},{7,4},{8,9},{9,10},{10,1... | collective-permute-start | bytes 786440 | tf_op jit(solution)/shard_map/ppermute | solution.py:576

commit v8 on v7

--- a/solution.py
+++ b/solution.py
@@ -574,9 +574,9 @@
             for source in range(col_count)
         ]
         shared.append(lax.ppermute(joined, "col", ring))
-    for chunk, pair in enumerate(pairs):
-        for h in range(SPLITS[chunk]):
-            buffer = finish(pair, h, tile_index, place, raw, buffer, sizes, joined)
+    groups = [pairs[0] + pairs[1]] + pairs[2:]
+    for group in groups:
+        buffer = finish(group, 0, tile_index, place, raw, buffer, sizes, joined)
     arrived = lax.all_to_all(buffer, ("row", "col"), split_axis=0, concat_axis=0, tiled=True)
     result, coarse_features = copied(arrived, shared)
     return (coarse_features.reshape(tiles_row * HALF, width), result)

time: 544 us -> 541 us (level)
    pallas_call x4 -> x3, Pallas kernels: 14.5 us -> 11.9 us  [finish(): pl.pallas_call(functools.partial(finish_kernel, starts, counts, h), out_s...]
  transfers between devices with their start and end apart: 20 -> 20, of which waited for: 2 -> 2; matrix products, arithmetic and copies ran while one was open for 0% -> 0% of each run, Pallas kernels for 12% -> 11%
where the time goes in v8:
time: 541 us; the launch traced here: 537 us
  Pallas kernels  326 us (60%)
  waiting for transfers between devices  105 us (19%)
  blocking collectives  61.9 us (11%)
  starting transfers between devices  40.8 us (8%)
    pallas_call x1, Pallas kernels, copied(): pl.pallas_call(functools.partial(copy_kernel, pieces), out_shape=[jax.Sha...  256 us
    ppermute x3, waiting for transfers between devices, level(): shared.append(lax.ppermute(joined, 'col', ring))  105 us
    all_to_all x1, blocking collectives, level(): lax.all_to_all(token, ('row', 'col'), split_axis=0, concat_axis=0, tiled=...  31.8 us
    all_to_all x1, blocking collectives, level(): spread = lax.all_to_all(own, 'col', split_axis=0, concat_axis=0, tiled=True)  30 us
    ppermute x16, starting transfers between devices, flipped(): return lax.ppermute(value, axis, pairs)  29.9 us
    pallas_call x4, Pallas kernels, pair_tiles(): pl.pallas_call(functools.partial(pair_kernel, starts, counts, with_featur...  28.5 us
    pallas_call x1, Pallas kernels, sum_rows(): pl.pallas_call(functools.partial(sum_kernel, bounds, tiles_col), out_shap...  14 us
    pallas_call x3, Pallas kernels, finish(): pl.pallas_call(functools.partial(finish_kernel, starts, counts, h), out_s...  11.9 us
  transfers between devices with their start and end apart: 20, of which 2 were waited for; matrix products, arithmetic and copies ran while one was open for 0% of the time, Pallas kernels for 11%

profile of v8, /device:TPU:32, one launch (start us, length us, event | category | flops | bytes accessed | tf_op | source)
XLA Modules:
  0.0 537.1 jit_solution(18159662649660875291)
XLA Ops:
  0.6 6.2 %pair_tiles.4 = (bf16[2,12,128,128]{3,2,1,0:T(8,128)(2,1)}, bf16[2,12,128,128]{3,2,1,0:T(8,128)(2,1)}, bf16[2,8,128,128]{3,2,1,0:T(8,128)(2,1)}, bf16[2,8,128,128]{3,2,1,0:T(8,128)(2,1)}) custom-call(s32[104]{0:T(128)} %index_ref.15, s32[4]{0:T(128)} %pert_ref.7, s32[1]{0:T(128)} %bitcast.1.lane_ref, bf16[104,256,256]{2,1,0:T(8,128)(2,1)} %tiles.7, ...), custom_call_target="tpu_custom_call" | custom-call | tf_op jit(solution)/shard_map/pair_tiles/pallas_call | solution.py:179
  6.8 2.8 collective-permute-start.6
  9.6 2.8 collective-permute-start.7
  12.4 6.5 %pair_tiles.5 = (bf16[2,8,128,128]{3,2,1,0:T(8,128)(2,1)}, bf16[2,8,128,128]{3,2,1,0:T(8,128)(2,1)}, bf16[2,16,128,128]{3,2,1,0:T(8,128)(2,1)}, bf16[2,16,128,128]{3,2,1,0:T(8,128)(2,1)}) custom-call(s32[104]{0:T(128)} %index_ref.15, s32[4]{0:T(128)} %pert_ref.7, s32[1]{0:T(128)} %bitcast.1.lane_ref, bf16[104,256,256]{2,1,0:T(8,128)(2,1)} %tiles.7, ...), custom_call_target="tpu_custom_call" | custom-call | tf_op jit(solution)/shard_map/pair_tiles/pallas_call | solution.py:179
  18.9 0.7 collective-permute-start.4
  19.6 1.1 collective-permute-start.5
  20.8 8.0 %pair_tiles.6 = (bf16[2,16,128,128]{3,2,1,0:T(8,128)(2,1)}, bf16[2,16,128,128]{3,2,1,0:T(8,128)(2,1)}, bf16[2,16,128,128]{3,2,1,0:T(8,128)(2,1)}, bf16[2,16,128,128]{3,2,1,0:T(8,128)(2,1)}) custom-call(s32[104]{0:T(128)} %index_ref.15, s32[4]{0:T(128)} %pert_ref.7, s32[1]{0:T(128)} %bitcast.1.lane_ref, bf16[104,256,256]{2,1,0:T(8,128)(2,1)} %tiles.7, ...), custom_call_target="tpu_custom_call" | custom-call | tf_op jit(solution)/shard_map/pair_tiles/pallas_call | solution.py:179
  28.8 2.3 collective-permute-start.2
  31.1 0.0 collective-permute-done.7.refs_3_.refs_4_
  31.1 2.6 collective-permute-start.3
  33.7 7.7 %pair_tiles.7 = (bf16[2,16,128,128]{3,2,1,0:T(8,128)(2,1)}, bf16[2,16,128,128]{3,2,1,0:T(8,128)(2,1)}, bf16[2,16,128,128]{3,2,1,0:T(8,128)(2,1)}, bf16[2,16,128,128]{3,2,1,0:T(8,128)(2,1)}) custom-call(s32[104]{0:T(128)} %index_ref.15, s32[4]{0:T(128)} %pert_ref.7, s32[1]{0:T(128)} %bitcast.1.lane_ref, bf16[104,256,256]{2,1,0:T(8,128)(2,1)} %tiles.7, ...), custom_call_target="tpu_custom_call" | custom-call | tf_op jit(solution)/shard_map/pair_tiles/pallas_call | solution.py:179
  41.4 0.0 collective-permute-done.4.refs_1_.refs_7_
  41.4 1.7 collective-permute-start
  43.1 0.0 collective-permute-done.6.refs_1_.came
  43.1 2.8 collective-permute-start.1
  45.9 14.0 %sum_rows.1._ = f32[16,256]{1,0:T(8,128)} custom-call(s32[104]{0:T(128)} %index_ref.15, bf16[2,12,128,128]{3,2,1,0:T(8,128)(2,1)} %get-tuple-element.38.rest_0_, bf16[2,12,128,128]{3,2,1,0:T(8,128)(2,1)} %get-tuple-element.39.rest_1_.refs_0_.kept, bf16[2,8,128,128]{3,2,1,0:T(8,128)(2,1)} %get-tuple-element.40.rest_2_, ...), custom_call_target="tpu_custom_call" | custom-call | tf_op jit(solution)/shard_map/sum_rows/pallas_call | solution.py:242
  59.9 3.9 zero_buffer.1.refs_4_.refs_13_
  63.8 0.2 convert_reduce_fusion
  63.9 0.6 multiply_add_fusion.refs_5_.place_ref
  64.5 2.0 forward.4
  66.6 0.0 collective-permute-done.5.refs_3_.refs_10_
  66.6 0.5 collective-permute-start.13
  67.1 2.2 forward.5
  69.3 0.0 collective-permute-done.2.refs_1_
  69.3 2.2 collective-permute-start.12
  71.5 0.0 collective-permute-done.3.refs_3_.refs_4_
  71.5 2.4 collective-permute-start.14
  74.0 30.0 %all_to_all.27 = f32[16,1,256]{2,1,0:T(1,128)S(1)} all-to-all(f32[16,1,256]{2,1,0:T(1,128)S(1)} %copy.15), channel_id=1, replica_groups=mesh['row'=8,'col'=16] {'col'}, dimensions={0} | all-to-all | bytes 32768 | tf_op jit(solution)/shard_map/all_to_all | solution.py:547
  104.0 0.6 copy.22
  104.6 1.4 line_copies.1.refs_4_
  106.0 2.5 forward.6
  108.5 0.0 collective-permute-done.refs_1_
  108.5 0.9 collective-permute-start.15
  109.3 0.0 collective-permute-done.1.refs_3_.refs_4_
  109.3 2.3 collective-permute-start.10
  111.7 2.4 forward.7
  114.1 0.0 collective-permute-done.13.refs_5_
  114.1 2.9 collective-permute-start.11
  117.0 0.0 collective-permute-done.12.refs_2_
  117.0 0.7 collective-permute-start.9
  117.7 0.0 collective-permute-done.14.refs_8_
  117.7 1.2 collective-permute-start.8
  118.9 0.0 copy-done.2
  118.9 0.1 copy.16
  119.0 31.8 %all_to_all.28 = f32[128,1,256]{2,1,0:T(1,128)S(1)} all-to-all(f32[128,1,256]{2,1,0:T(1,128)S(1)} %copy.16), channel_id=1, replica_groups=mesh['row'=8,'col'=16] {'row','col'}, dimensions={0} | all-to-all | bytes 262144 | tf_op jit(solution)/shard_map/all_to_all | solution.py:567
  150.9 0.7 copy.21
  151.5 2.1 join_features.1.refs_14_.refs_8_.refs_1_
  153.6 0.0 collective-permute-done.15.refs_11_
  153.6 4.3 finish.3.refs_7_
  157.9 0.0 collective-permute-done.11.refs_5_
  157.9 0.0 collective-permute-done.10.refs_2_
  157.9 3.8 finish.4.refs_7_
  161.7 0.0 collective-permute-done.9.refs_5_
  161.7 0.0 collective-permute-done.8.refs_2_
  161.7 3.8 finish.5
  165.5 6.3 %all-to-all-start.2 = ((bf16[256,128,128]{2,1,0:T(8,128)(2,1)}), bf16[256,128,128]{2,1,0:T(8,128)(2,1)}, u32[]{:S(2)}, u32[]{:S(2)}) async-start(bf16[256,128,128]{2,1,0:T(8,128)(2,1)} %finish.5), calls=%async_computation.2 | async-start | bytes 16777216 | tf_op jit(solution)/shard_map/all_to_all | solution.py:580
  171.9 2.9 collective-permute-start.18
  174.8 0.7 collective-permute-start.17
  175.5 0.9 collective-permute-start.16
  176.5 95.8 %collective-permute-done.18.refs_4_ = bf16[4,128,256]{2,1,0:T(8,128)(2,1)S(1)} collective-permute-done((bf16[4,128,256]{2,1,0:T(8,128)(2,1)S(1)}, bf16[4,128,256]{2,1,0:T(8,128)(2,1)S(1)}, u32[]{:S(2)}, u32[]{:S(2)}) %collective-permute-start.18) | collective-permute-done | bytes 262176 | tf_op jit(solution)/shard_map/ppermute | solution.py:576
  272.2 9.1 %collective-permute-done.17.refs_3_ = bf16[4,128,256]{2,1,0:T(8,128)(2,1)S(1)} collective-permute-done((bf16[4,128,256]{2,1,0:T(8,128)(2,1)S(1)}, bf16[4,128,256]{2,1,0:T(8,128)(2,1)S(1)}, u32[]{:S(2)}, u32[]{:S(2)}) %collective-permute-start.17) | collective-permute-done | bytes 262176 | tf_op jit(solution)/shard_map/ppermute | solution.py:576
  281.4 0.0 collective-permute-done.16.refs_2_
  281.4 0.0 all-to-all-done.2.refs_0_
  281.4 255.5 %copied.1 = (bf16[256,128,128]{2,1,0:T(8,128)(2,1)}, bf16[16,128,256]{2,1,0:T(8,128)(2,1)}) custom-call(bf16[256,128,128]{2,1,0:T(8,128)(2,1)} %all-to-all-done.2.refs_0_, bf16[4,128,256]{2,1,0:T(8,128)(2,1)S(1)} %copy-done, bf16[4,128,256]{2,1,0:T(8,128)(2,1)S(1)} %collective-permute-done.16.refs_2_, ...), custom_call_target="tpu_custom_call" | custom-call | tf_op jit(solution)/shard_map/copied/pallas_call | solution.py:489
  (13 shorter events, 0.0 us)
Async XLA Ops:
  6.8 36.3 %collective-permute-start.6 = (bf16[2,12,128,128]{3,2,1,0:T(8,128)(2,1)}, bf16[2,12,128,128]{3,2,1,0:T(8,128)(2,1)}, u32[]{:S(2)}, u32[]{:S(2)}) collective-permute-start(bf16[2,12,128,128]{3,2,1,0:T(8,128)(2,1)} %get-tuple-element.38.rest_0_), channel_id=1, source_target_pairs={{0,64},{16,80},{32,96},{48,112},{64,0},{80,16},{96,32},{112,48},{1... | collective-permute-start | bytes 2359304 | tf_op jit(solution)/shard_map/ppermute | solution.py:26
  9.6 21.5 %collective-permute-start.7 = (bf16[2,8,128,128]{3,2,1,0:T(8,128)(2,1)}, bf16[2,8,128,128]{3,2,1,0:T(8,128)(2,1)S(1)}, u32[]{:S(2)}, u32[]{:S(2)}) collective-permute-start(bf16[2,8,128,128]{3,2,1,0:T(8,128)(2,1)} %get-tuple-element.40.rest_2_), channel_id=1, source_target_pairs={{0,8},{1,9},{2,10},{3,11},{4,12},{5,13},{6,14},{7,15},{8,0},{9,1},... | collective-permute-start | bytes 1572872 | tf_op jit(solution)/shard_map/ppermute | solution.py:26
  18.9 22.5 %collective-permute-start.4 = (bf16[2,8,128,128]{3,2,1,0:T(8,128)(2,1)}, bf16[2,8,128,128]{3,2,1,0:T(8,128)(2,1)}, u32[]{:S(2)}, u32[]{:S(2)}) collective-permute-start(bf16[2,8,128,128]{3,2,1,0:T(8,128)(2,1)} %get-tuple-element.41.rest_4_), channel_id=1, source_target_pairs={{0,64},{16,80},{32,96},{48,112},{64,0},{80,16},{96,32},{112,48},{1... | collective-permute-start | bytes 1572872 | tf_op jit(solution)/shard_map/ppermute | solution.py:26
  19.6 46.9 %collective-permute-start.5 = (bf16[2,16,128,128]{3,2,1,0:T(8,128)(2,1)}, bf16[2,16,128,128]{3,2,1,0:T(8,128)(2,1)}, u32[]{:S(2)}, u32[]{:S(2)}) collective-permute-start(bf16[2,16,128,128]{3,2,1,0:T(8,128)(2,1)} %get-tuple-element.43.rest_6_), channel_id=1, source_target_pairs={{0,8},{1,9},{2,10},{3,11},{4,12},{5,13},{6,14},{7,15},{8,0},{9,1},... | collective-permute-start | bytes 3145736 | tf_op jit(solution)/shard_map/ppermute | solution.py:26
  28.8 40.5 %collective-permute-start.2 = (bf16[2,16,128,128]{3,2,1,0:T(8,128)(2,1)}, bf16[2,16,128,128]{3,2,1,0:T(8,128)(2,1)}, u32[]{:S(2)}, u32[]{:S(2)}) collective-permute-start(bf16[2,16,128,128]{3,2,1,0:T(8,128)(2,1)} %get-tuple-element.36.rest_8_), channel_id=1, source_target_pairs={{0,64},{16,80},{32,96},{48,112},{64,0},{80,16},{96,32},{112,48},{1... | collective-permute-start | bytes 3145736 | tf_op jit(solution)/shard_map/ppermute | solution.py:26
  31.1 28.7 %copy-start.1 = (bf16[2,8,128,128]{3,2,1,0:T(8,128)(2,1)}, bf16[2,8,128,128]{3,2,1,0:T(8,128)(2,1)S(1)}, u32[]{:S(2)}) copy-start(bf16[2,8,128,128]{3,2,1,0:T(8,128)(2,1)S(1)} %collective-permute-done.7.refs_3_.refs_4_) | copy-start | bytes 1572868
  31.1 40.4 %collective-permute-start.3 = (bf16[2,16,128,128]{3,2,1,0:T(8,128)(2,1)}, bf16[2,16,128,128]{3,2,1,0:T(8,128)(2,1)}, u32[]{:S(2)}, u32[]{:S(2)}) collective-permute-start(bf16[2,16,128,128]{3,2,1,0:T(8,128)(2,1)} %get-tuple-element.37.rest_10_), channel_id=1, source_target_pairs={{0,8},{1,9},{2,10},{3,11},{4,12},{5,13},{6,14},{7,15},{8,0},{9,1},... | collective-permute-start | bytes 3145736 | tf_op jit(solution)/shard_map/ppermute | solution.py:26
  41.4 67.0 %collective-permute-start = (bf16[2,16,128,128]{3,2,1,0:T(8,128)(2,1)}, bf16[2,16,128,128]{3,2,1,0:T(8,128)(2,1)}, u32[]{:S(2)}, u32[]{:S(2)}) collective-permute-start(bf16[2,16,128,128]{3,2,1,0:T(8,128)(2,1)} %get-tuple-element.32.rest_12_), channel_id=1, source_target_pairs={{0,64},{16,80},{32,96},{48,112},{64,0},{80,16},{96,32},{112,48},{1... | collective-permute-start | bytes 3145736 | tf_op jit(solution)/shard_map/ppermute | solution.py:26
  43.1 66.2 %collective-permute-start.1 = (bf16[2,16,128,128]{3,2,1,0:T(8,128)(2,1)}, bf16[2,16,128,128]{3,2,1,0:T(8,128)(2,1)}, u32[]{:S(2)}, u32[]{:S(2)}) collective-permute-start(bf16[2,16,128,128]{3,2,1,0:T(8,128)(2,1)} %get-tuple-element.34.rest_14_), channel_id=1, source_target_pairs={{0,8},{1,9},{2,10},{3,11},{4,12},{5,13},{6,14},{7,15},{8,0},{9,1},... | collective-permute-start | bytes 3145736 | tf_op jit(solution)/shard_map/ppermute | solution.py:26
  45.9 17.9 %copy-start.5 = (s32[104,2]{0,1:T(2,128)S(1)}, s32[104,2]{0,1:T(2,128)}, u32[]{:S(2)}) copy-start(s32[104,2]{0,1:T(2,128)} %param.15) | copy-start | bytes 2500
  63.8 10.2 %copy-start.4 = (f32[16,256]{1,0:T(8,128)S(1)}, f32[16,256]{1,0:T(8,128)}, u32[]{:S(2)}) copy-start(f32[16,256]{1,0:T(8,128)} %sum_rows.1._) | copy-start | bytes 49156
  66.6 47.5 %collective-permute-start.13 = (bf16[8,128,128]{2,1,0:T(8,128)(2,1)}, bf16[8,128,128]{2,1,0:T(8,128)(2,1)S(1)}, u32[]{:S(2)}, u32[]{:S(2)}) collective-permute-start(bf16[8,128,128]{2,1,0:T(8,128)(2,1)} %get-tuple-element.50), channel_id=1, source_target_pairs={{0,64},{16,80},{32,96},{48,112},{64,0},{80,16},{96,32},{112,48},{1... | collective-permute-start | bytes 786440 | tf_op jit(solution)/shard_map/ppermute | solution.py:26
  69.3 47.7 %collective-permute-start.12 = (bf16[8,128,128]{2,1,0:T(8,128)(2,1)}, bf16[8,128,128]{2,1,0:T(8,128)(2,1)}, u32[]{:S(2)}, u32[]{:S(2)}) collective-permute-start(bf16[8,128,128]{2,1,0:T(8,128)(2,1)} %get-tuple-element.44.refs_4_), channel_id=1, source_target_pairs={{0,8},{1,9},{2,10},{3,11},{4,12},{5,13},{6,14},{7,15},{8,0},{9,1},... | collective-permute-start | bytes 786440 | tf_op jit(solution)/shard_map/ppermute | solution.py:26
  71.5 46.2 %collective-permute-start.14 = (bf16[8,128,128]{2,1,0:T(8,128)(2,1)}, bf16[8,128,128]{2,1,0:T(8,128)(2,1)}, u32[]{:S(2)}, u32[]{:S(2)}) collective-permute-start(bf16[8,128,128]{2,1,0:T(8,128)(2,1)} %get-tuple-element.45._), channel_id=1, source_target_pairs={{0,8},{1,9},{2,10},{3,11},{4,12},{5,13},{6,14},{7,15},{8,0},{9,1},... | collective-permute-start | bytes 786440 | tf_op jit(solution)/shard_map/ppermute | solution.py:26
  106.0 12.9 %copy-start.2 = (f32[128,256]{1,0:T(8,128)S(1)}, f32[128,256]{1,0:T(8,128)}, u32[]{:S(2)}) copy-start(f32[128,256]{1,0:T(8,128)} %line_copies.1.refs_4_) | copy-start | bytes 393220
  108.5 45.1 %collective-permute-start.15 = (bf16[16,128,128]{2,1,0:T(8,128)(2,1)}, bf16[16,128,128]{2,1,0:T(8,128)(2,1)}, u32[]{:S(2)}, u32[]{:S(2)}) collective-permute-start(bf16[16,128,128]{2,1,0:T(8,128)(2,1)} %get-tuple-element.51), channel_id=1, source_target_pairs={{0,64},{16,80},{32,96},{48,112},{64,0},{80,16},{96,32},{112,48},{1... | collective-permute-start | bytes 1572872 | tf_op jit(solution)/shard_map/ppermute | solution.py:26
  109.3 48.6 %collective-permute-start.10 = (bf16[16,128,128]{2,1,0:T(8,128)(2,1)}, bf16[16,128,128]{2,1,0:T(8,128)(2,1)}, u32[]{:S(2)}, u32[]{:S(2)}) collective-permute-start(bf16[16,128,128]{2,1,0:T(8,128)(2,1)} %get-tuple-element.46.refs_4_), channel_id=1, source_target_pairs={{0,8},{1,9},{2,10},{3,11},{4,12},{5,13},{6,14},{7,15},{8,0},{9,1},... | collective-permute-start | bytes 1572872 | tf_op jit(solution)/shard_map/ppermute | solution.py:26
  114.1 39.5 %copy-start.3 = (bf16[8,128,128]{2,1,0:T(8,128)(2,1)}, bf16[8,128,128]{2,1,0:T(8,128)(2,1)S(1)}, u32[]{:S(2)}) copy-start(bf16[8,128,128]{2,1,0:T(8,128)(2,1)S(1)} %collective-permute-done.13.refs_5_) | copy-start | bytes 786436
  114.1 43.8 %collective-permute-start.11 = (bf16[16,128,128]{2,1,0:T(8,128)(2,1)}, bf16[16,128,128]{2,1,0:T(8,128)(2,1)}, u32[]{:S(2)}, u32[]{:S(2)}) collective-permute-start(bf16[16,128,128]{2,1,0:T(8,128)(2,1)} %get-tuple-element.49), channel_id=1, source_target_pairs={{0,64},{16,80},{32,96},{48,112},{64,0},{80,16},{96,32},{112,48},{1... | collective-permute-start | bytes 1572872 | tf_op jit(solution)/shard_map/ppermute | solution.py:26
  117.0 44.7 %collective-permute-start.9 = (bf16[16,128,128]{2,1,0:T(8,128)(2,1)}, bf16[16,128,128]{2,1,0:T(8,128)(2,1)}, u32[]{:S(2)}, u32[]{:S(2)}) collective-permute-start(bf16[16,128,128]{2,1,0:T(8,128)(2,1)} %get-tuple-element.48), channel_id=1, source_target_pairs={{0,64},{16,80},{32,96},{48,112},{64,0},{80,16},{96,32},{112,48},{1... | collective-permute-start | bytes 1572872 | tf_op jit(solution)/shard_map/ppermute | solution.py:26
  117.7 44.0 %collective-permute-start.8 = (bf16[16,128,128]{2,1,0:T(8,128)(2,1)}, bf16[16,128,128]{2,1,0:T(8,128)(2,1)}, u32[]{:S(2)}, u32[]{:S(2)}) collective-permute-start(bf16[16,128,128]{2,1,0:T(8,128)(2,1)} %get-tuple-element.47._), channel_id=1, source_target_pairs={{0,8},{1,9},{2,10},{3,11},{4,12},{5,13},{6,14},{7,15},{8,0},{9,1},... | collective-permute-start | bytes 1572872 | tf_op jit(solution)/shard_map/ppermute | solution.py:26
  165.5 6.3 %copy-start = (bf16[4,128,256]{2,1,0:T(8,128)(2,1)S(1)}, bf16[4,128,256]{2,1,0:T(8,128)(2,1)}, u32[]{:S(2)}) copy-start(bf16[4,128,256]{2,1,0:T(8,128)(2,1)} %join_features.1.refs_14_.refs_8_.refs_1_) | copy-start | bytes 786436
  165.5 115.8 %all-to-all-start.2 = ((bf16[256,128,128]{2,1,0:T(8,128)(2,1)}), bf16[256,128,128]{2,1,0:T(8,128)(2,1)}, u32[]{:S(2)}, u32[]{:S(2)}) async-start(bf16[256,128,128]{2,1,0:T(8,128)(2,1)} %finish.5), calls=%async_computation.2 | async-start | bytes 16777216 | tf_op jit(solution)/shard_map/all_to_all | solution.py:580
  171.9 100.3 %collective-permute-start.18 = (bf16[4,128,256]{2,1,0:T(8,128)(2,1)S(1)}, bf16[4,128,256]{2,1,0:T(8,128)(2,1)S(1)}, u32[]{:S(2)}, u32[]{:S(2)}) collective-permute-start(bf16[4,128,256]{2,1,0:T(8,128)(2,1)S(1)} %copy-done), channel_id=1, source_target_pairs={{0,3},{1,0},{2,1},{3,2},{4,7},{5,4},{6,5},{7,6},{8,11},{9,8},{10,9... | collective-permute-start | bytes 786440 | tf_op jit(solution)/shard_map/ppermute | solution.py:576
  174.8 106.5 %collective-permute-start.17 = (bf16[4,128,256]{2,1,0:T(8,128)(2,1)S(1)}, bf16[4,128,256]{2,1,0:T(8,128)(2,1)S(1)}, u32[]{:S(2)}, u32[]{:S(2)}) collective-permute-start(bf16[4,128,256]{2,1,0:T(8,128)(2,1)S(1)} %copy-done), channel_id=1, source_target_pairs={{0,2},{1,3},{2,0},{3,1},{4,6},{5,7},{6,4},{7,5},{8,10},{9,11},{10,... | collective-permute-start | bytes 786440 | tf_op jit(solution)/shard_map/ppermute | solution.py:576
  175.5 105.8 %collective-permute-start.16 = (bf16[4,128,256]{2,1,0:T(8,128)(2,1)S(1)}, bf16[4,128,256]{2,1,0:T(8,128)(2,1)S(1)}, u32[]{:S(2)}, u32[]{:S(2)}) collective-permute-start(bf16[4,128,256]{2,1,0:T(8,128)(2,1)S(1)} %copy-done), channel_id=1, source_target_pairs={{0,1},{1,2},{2,3},{3,0},{4,5},{5,6},{6,7},{7,4},{8,9},{9,10},{10,1... | collective-permute-start | bytes 786440 | tf_op jit(solution)/shard_map/ppermute | solution.py:576
